TPU v7x, 512 devices: a whole 4x4x16 slice. The times are simulated.
512 devices in a mesh: seq: 64 (over z, y), head: 8 (over x, core).
Axes of the slice: x: 4, y: 4, z: 16, core: 2. Of those that a mesh axis runs over, the one named last changes fastest.
Arguments:
- queries: bfloat16 [65536, 2048], P('seq', 'head'), may hold values from -6 to 6
- keys: bfloat16 [65536, 2048], P('seq', 'head'), may hold values from -6 to 6
- values: bfloat16 [65536, 2048], P('seq', 'head'), may hold values from -6 to 6
- offsets: int32 [16, 3], P('head'), may hold values from 0 to 63, as said below
- w_out: bfloat16 [2048, 2048], P('head'), may hold values from -0.1875 to 0.1875
Outputs:
- projected: bfloat16 [65536, 2048], P('seq', 'head')
Inputs may be any that keep to these rules, and one draw needn't show every extreme that they name: offsets[h, 0] is below 4, offsets[h, 1] below 16, offsets[h, 2] below 64.
All inputs are finite; a program needn't handle non-finite values.
Results may differ from a plain program's by a relative error of at most 0.017.
Values may be sent and summed in bfloat16 or wider, within the bound.
No kernel may reach another device: no remote copies, remote signals or barrier semaphores. Data moves between devices by JAX's collectives and lax.ppermute only.
A program may use at most 64 MiB of HBM per device.

v0:
```python
import jax
import jax.numpy as jnp
from jax import lax
from jax.sharding import PartitionSpec as P

HEAD_DIM = 128


def from_partner(value, axis, bit):
    mask = 2**bit
    pairs = [(source, source ^ mask) for source in range(lax.axis_size(axis))]
    return lax.ppermute(value, axis, pairs)


def choose_rows(source, dilation_step, level_offsets):
    count = source.shape[0] // dilation_step
    grid = source.reshape(count, dilation_step, source.shape[1], source.shape[2])
    picked = (
        lax.broadcasted_iota(jnp.int32, (1, dilation_step, source.shape[1], 1), 1)
        == level_offsets[None, None, :, None]
    )
    masked = jnp.where(picked, grid, jnp.zeros((), source.dtype))
    return jnp.sum(masked, axis=1, dtype=source.dtype)


def attend(chosen_q, key_grid, value_grid, first_index):
    query_count = chosen_q.shape[0]
    key_count = key_grid.shape[0]
    scores = jnp.einsum(
        "qhd,khd->hqk", chosen_q, key_grid, preferred_element_type=jnp.float32
    ) * HEAD_DIM ** (-0.5)
    query_index = first_index + lax.broadcasted_iota(jnp.int32, (query_count, key_count), 0)
    key_index = lax.broadcasted_iota(jnp.int32, (query_count, key_count), 1)
    scores = jnp.where((key_index <= query_index)[None], scores, jnp.float32(-1e30))
    maxima = jnp.max(scores, axis=-1)
    weights = jnp.exp(scores - maxima[..., None])
    totals = jnp.sum(weights, axis=-1)
    summed = jnp.einsum(
        "hqk,khd->qhd", weights.astype(jnp.bfloat16), value_grid, preferred_element_type=jnp.float32
    )
    return (maxima.T, summed, totals.T)


def spread_back(terms, dilation_step, level_offsets):
    level_max, level_sum, level_total = terms
    count, heads_here, head_width = level_sum.shape
    picked = (
        lax.broadcasted_iota(jnp.int32, (1, dilation_step, heads_here), 1)
        == level_offsets[None, None, :]
    )
    level_sum = jnp.where(picked[..., None], level_sum[:, None], jnp.float32(0.0)).reshape(
        count * dilation_step, heads_here, head_width
    )
    level_max = jnp.where(picked, level_max[:, None], jnp.float32(-1e30)).reshape(
        count * dilation_step, heads_here
    )
    level_total = jnp.where(picked, level_total[:, None], jnp.float32(0.0)).reshape(
        count * dilation_step, heads_here
    )
    return (level_max, level_sum, level_total)


def combine(run_state, terms):
    old_top, old_sum, old_total = run_state
    level_max, level_sum, level_total = terms
    new_top = jnp.maximum(old_top, level_max)
    keep_old = jnp.exp(old_top - new_top)
    keep_new = jnp.exp(level_max - new_top)
    return (
        new_top,
        old_sum * keep_old[..., None] + level_sum * keep_new[..., None],
        old_total * keep_old + level_total * keep_new,
    )


def pair_gather(block, bit_total, seq_index):
    for bit_number in range(bit_total):
        theirs = from_partner(block, "seq", bit_number)
        upper_half = seq_index // 2**bit_number % 2
        block = jnp.where(
            upper_half == 1,
            jnp.concatenate([theirs, block], axis=1),
            jnp.concatenate([block, theirs], axis=1),
        )
    return block


def shards(queries, keys, values, offsets, w_out):
    row_count = queries.shape[0]
    feature_width = queries.shape[1]
    heads_here = feature_width // HEAD_DIM
    spread = lax.axis_size("seq")
    seq_index = lax.axis_index("seq")
    query_grid = queries.reshape(row_count, heads_here, HEAD_DIM)
    key_grid = keys.reshape(row_count, heads_here, HEAD_DIM)
    value_grid = values.reshape(row_count, heads_here, HEAD_DIM)
    run_state = attend(query_grid, key_grid, value_grid, 0)

    def level_pairs(dilation_step, column_slot):
        level_offsets = offsets[:, column_slot]
        paired = jnp.stack(
            [
                choose_rows(key_grid, dilation_step, level_offsets),
                choose_rows(value_grid, dilation_step, level_offsets),
            ]
        )
        return (level_offsets, paired.reshape(2, row_count // dilation_step, feature_width))

    near_offsets, near_pairs = level_pairs(4, 0)
    middle_offsets, middle_pairs = level_pairs(16, 1)
    whole_offsets, whole_pairs = level_pairs(spread, 2)
    near_pairs = pair_gather(near_pairs, 2, seq_index)
    middle_pairs = pair_gather(middle_pairs, 4, seq_index)
    whole_pairs = lax.all_gather(whole_pairs, "seq", axis=1, tiled=True)
    for dilation_step, level_offsets, paired, group_size in (
        (4, near_offsets, near_pairs, 4),
        (16, middle_offsets, middle_pairs, 16),
        (spread, whole_offsets, whole_pairs, spread),
    ):
        chosen_q = choose_rows(query_grid, dilation_step, level_offsets)
        first_index = seq_index % group_size * (row_count // dilation_step)
        key_count = paired.shape[1]
        terms = attend(
            chosen_q,
            paired[0].reshape(key_count, heads_here, HEAD_DIM),
            paired[1].reshape(key_count, heads_here, HEAD_DIM),
            first_index,
        )
        run_state = combine(run_state, spread_back(terms, dilation_step, level_offsets))
    attention = (
        (run_state[1] / run_state[2][..., None])
        .astype(jnp.bfloat16)
        .reshape(row_count, feature_width)
    )
    partial_term = jnp.dot(attention, w_out, preferred_element_type=jnp.float32)
    return lax.psum_scatter(
        partial_term.astype(jnp.bfloat16), "head", scatter_dimension=1, tiled=True
    )


def solution(mesh):
    in_specs = (
        P("seq", "head"),
        P("seq", "head"),
        P("seq", "head"),
        P("head", None),
        P("head", None),
    )
    out_specs = P("seq", "head")
    return jax.shard_map(shards, mesh=mesh, in_specs=in_specs, out_specs=out_specs, check_vma=False)
```

profile of v0, /device:TPU:1, one launch (start us, length us, event | category | flops | bytes accessed | tf_op | source)
XLA Modules:
  0.0 249.8 jit_solution(9959556793777187245)
XLA Ops:
  6.5 1.6 slice_reduce_fusion.2
  8.3 1.2 reshape_reshape.27
  9.5 2.0 reshape_reshape.28
  11.4 0.9 reshape_reshape.29
  12.4 4.9 %fusion.39 = (bf16[256,2,128]{2,1,0:T(2,128)(2,1)S(1)}, bf16[256,2,128]{2,1,0:T(2,128)(2,1)S(1)}, bf16[256,2,128]{2,1,0:T(2,128)(2,1)}) fusion(bf16[256,4,2,128]{3,2,1,0:T(2,128)(2,1)S(1)} %reshape_reshape.27, pred[4,2]{1,0:T(4,128)(4,1)S(1)} %copy.35, bf16[256,4,2,128]{3,2,1,0:T(2,128)(2,1)} %reshape_reshape.28, bf16[256,4,2,128]{3,2,1,0:T(2,128)(2,1)} %reshape_reshape.29), kind=kLoop, calls=%fused_computation.45 | loop fusion | flops 1376256 | bytes 1966088 | tf_op jit(solution)/shard_map/reduce_sum | solution.py:23
  17.4 1.0 copy.65
  18.4 0.7 pad_maximum_fusion
  19.2 4.0 %collective-permute-start = (bf16[2,256,256]{1,2,0:T(8,128)(2,1)}, bf16[2,256,256]{1,2,0:T(8,128)(2,1)}, u32[]{:S(2)}, u32[]{:S(2)}) collective-permute-start(bf16[2,256,256]{1,2,0:T(8,128)(2,1)} %pad_maximum_fusion), channel_id=1, source_target_pairs={{0,8},{8,0},{16,24},{24,16},{32,40},{40,32},{48,56},{56,48},{64,72... | collective-permute-start | bytes 786440 | tf_op jit(solution)/shard_map/ppermute | solution.py:12
  23.4 0.9 reshape_reshape.34
  24.3 0.9 reshape_reshape.35
  25.2 3.6 %fusion.45 = (bf16[16,2,128]{2,1,0:T(2,128)(2,1)S(1)}, bf16[16,2,128]{2,1,0:T(2,128)(2,1)}, bf16[16,2,128]{2,1,0:T(2,128)(2,1)}) fusion(bf16[16,64,2,128]{3,2,1,0:T(2,128)(2,1)S(1)} %reshape_reshape.33, pred[64,2]{1,0:T(8,128)(4,1)S(1)} %iota_compare_fusion.4, bf16[16,64,2,128]{3,2,1,0:T(2,128)(2,1)} %reshape_reshape.34, ...), kind=kLoop, calls=%fused_computation.51 | loop fusion | flops 1560576 | bytes 1597568 | tf_op jit(solution)/shard_map/reduce_sum | solution.py:23
  28.8 0.7 stack.33
  29.5 0.7 stack.34
  30.2 0.6 copy.50
  31.1 0.9 reshape_reshape.31
  32.0 0.9 reshape_reshape.32
  32.9 1.2 iota_compare_fusion.5
  34.1 1.3 copy.42
  35.4 4.2 %fusion.42 = (bf16[64,2,128]{2,1,0:T(2,128)(2,1)}, bf16[64,2,128]{2,1,0:T(2,128)(2,1)}, bf16[64,2,128]{2,1,0:T(2,128)(2,1)}) fusion(bf16[64,16,2,128]{3,2,1,0:T(2,128)(2,1)S(1)} %reshape_reshape.30, pred[16,2]{1,0:T(8,128)(4,1)} %copy.42, bf16[64,16,2,128]{3,2,1,0:T(2,128)(2,1)} %reshape_reshape.31, bf16[64,16,2,128]{3,2,1,0:T(2,128)(2,1)} %reshape_reshape.32), kind=kLoop, calls=%fused_computation.48 | loop fusion | flops 1523712 | bytes 1671200 | tf_op jit(solution)/shard_map/reduce_sum | solution.py:23
  39.6 0.9 copy.66
  40.5 0.9 copy.67
  41.4 2.1 collective-permute-start.2
  43.5 1.3 iota_compare_fusion
  44.8 0.7 iota_compare_fusion.2
  45.5 3.1 %fusion = (f32[2,1024]{1,0:T(2,128)S(1)}, f32[2,1024,1024]{1,2,0:T(8,128)S(1)}) fusion(pred[1024,1024]{0,1:T(8,128)(4,1)} %iota_compare_fusion, bf16[1024,256]{1,0:T(8,128)(2,1)S(1)} %copy-done.4, bf16[1024,256]{1,0:T(8,128)(2,1)S(1)} %copy-done.3), kind=kOutput, calls=%fused_computation.2 | convolution fusion | flops 543160320 | bytes 10493952 | tf_op jit(solution)/shard_map/qhd,khd->hqk/dot_general | solution.py:29
  48.7 3.1 %fusion.1 = f32[2,1024]{1,0:T(2,128)} fusion(f32[2,1024,1024]{1,2,0:T(8,128)S(1)} %get-tuple-element.37, f32[2,1024]{1,0:T(2,128)S(1)} %get-tuple-element.36, pred[1024,1024]{0,1:T(8,128)(4,1)S(1)} %copy-done.5), kind=kLoop, calls=%fused_computation.3 | loop fusion | flops 8386560 | bytes 9453568 | tf_op jit(solution)/shard_map/reduce_sum | solution.py:37
  52.1 5.0 %collective-permute-start.3 = (bf16[2,128,256]{1,2,0:T(8,128)(2,1)S(1)}, bf16[2,128,256]{1,2,0:T(8,128)(2,1)S(1)}, u32[]{:S(2)}, u32[]{:S(2)}) collective-permute-start(bf16[2,128,256]{1,2,0:T(8,128)(2,1)S(1)} %maximum_select_fusion.5), channel_id=1, source_target_pairs={{0,16},{8,24},{16,0},{24,8},{32,48},{40,56},{48,32},{56,40},{64,80... | collective-permute-start | bytes 393224 | tf_op jit(solution)/shard_map/ppermute | solution.py:12
  57.0 0.7 iota_compare_fusion.3
  57.7 1.2 maximum_select_fusion.2
  58.9 1.9 collective-permute-start.1
  61.0 3.6 %collective-permute-start.4 = (bf16[2,256,256]{1,2,0:T(8,128)(2,1)S(1)}, bf16[2,256,256]{1,2,0:T(8,128)(2,1)S(1)}, u32[]{:S(2)}, u32[]{:S(2)}) collective-permute-start(bf16[2,256,256]{1,2,0:T(8,128)(2,1)S(1)} %maximum_select_fusion.4), channel_id=1, source_target_pairs={{0,32},{8,40},{16,48},{24,56},{32,0},{40,8},{48,16},{56,24},{64,96... | collective-permute-start | bytes 786440 | tf_op jit(solution)/shard_map/ppermute | solution.py:12
  64.6 0.6 iota_add_fusion
  65.2 1.0 copy.63
  66.3 0.7 broadcast_in_dim.327
  66.9 0.6 broadcast_in_dim.315
  67.7 0.6 broadcast_in_dim.302
  68.3 0.8 broadcast_in_dim.303
  69.1 0.9 iota_compare_fusion.1
  70.0 0.9 maximum_select_fusion.3
  70.9 4.9 %collective-permute-start.5 = (bf16[2,512,256]{1,2,0:T(8,128)(2,1)}, bf16[2,512,256]{1,2,0:T(8,128)(2,1)}, u32[]{:S(2)}, u32[]{:S(2)}) collective-permute-start(bf16[2,512,256]{1,2,0:T(8,128)(2,1)} %maximum_select_fusion.3), channel_id=1, source_target_pairs={{0,64},{8,72},{16,80},{24,88},{32,96},{40,104},{48,112},{56,120},{... | collective-permute-start | bytes 1572872 | tf_op jit(solution)/shard_map/ppermute | solution.py:12
  75.8 0.3 maximum_select_fusion
  76.2 0.7 fusion.6
  76.9 1.4 convolution_bitcast_fusion
  78.3 1.8 copy.40
  80.1 0.8 broadcast_in_dim.308
  80.9 1.1 broadcast_in_dim.309
  82.0 0.6 fusion.7
  83.0 1.1 broadcast_in_dim.312
  84.1 1.3 copy.41
  85.4 13.8 %collective-permute-done.5 = bf16[2,512,256]{1,2,0:T(8,128)(2,1)} collective-permute-done((bf16[2,512,256]{1,2,0:T(8,128)(2,1)}, bf16[2,512,256]{1,2,0:T(8,128)(2,1)}, u32[]{:S(2)}, u32[]{:S(2)}) %collective-permute-start.5) | collective-permute-done | bytes 524320 | tf_op jit(solution)/shard_map/ppermute | solution.py:12
  99.3 1.9 maximum_select_fusion.1
  101.3 0.3 fusion.84
  102.2 0.3 convolution_bitcast_fusion.1
  102.6 1.3 copy.48
  104.0 68.7 %all-gather.2.cloned.1.call-done = bf16[2,1024,256]{2,0,1:T(2,128)(2,1)} async-done(((bf16[2,16,256]{2,0,1:T(2,128)(2,1)}), bf16[2,1024,256]{2,0,1:T(2,128)(2,1)}) %all-gather.2.cloned.1.call-update) | async-done | bytes 1048592 | tf_op jit(solution)/shard_map/all_gather | solution.py:114
  172.7 3.4 %fusion.82 = (bf16[1,1024,256]{2,0,1:T(2,128)(2,1)S(1)}, bf16[1,1024,256]{2,0,1:T(2,128)(2,1)S(1)}) fusion(bf16[2,1024,256]{2,0,1:T(2,128)(2,1)} %all-gather.2.cloned.1.call-done), kind=kLoop, calls=%fused_computation.112 | loop fusion | bytes 2097152 | tf_op jit(solution)/shard_map/slice | solution.py:125
  176.0 2.3 copy.68
  178.3 1.3 fusion.83
  180.1 1.3 copy.69
  181.5 0.3 convolution_bitcast_fusion.2
  181.9 1.4 copy.56
  183.4 7.3 %divide_convert_fusion = bf16[1024,2,128]{0,2,1:T(8,128)(2,1)S(1)} fusion(f32[1024,2,128]{0,2,1:T(8,128)} %copy.56, f32[1024,2,128]{0,2,1:T(8,128)} %copy.48, f32[1024,2,128]{0,2,1:T(8,128)} %copy.41, bf16[1024,2,128]{0,2,1:T(8,128)(2,1)} %bitcast.123, f32[2,1024,1024]{1,2,0:T(8,128)} %copy-done.1, f32[2,1024]{1,0:T(2,128)S(1)} %copy-done.11, ...), kind=kOutput, calls=%fused_computation.30 | convolution fusion | flops 548929536 | bytes 13703168 | tf_op jit(solution)/shard_map/hqk,khd->qhd/dot_general | solution.py:38
  190.7 3.2 %convolution_convert_fusion = bf16[1024,2048]{1,0:T(8,128)(2,1)} fusion(bf16[1024,256]{0,1:T(8,128)(2,1)S(1)} %bitcast.118, bf16[256,2048]{1,0:T(8,128)(2,1)S(1)} %copy-done), kind=kOutput, calls=%fused_computation.8 | convolution fusion | flops 1075838976 | bytes 5767168 | tf_op jit(solution)/shard_map/dot_general | solution.py:135
  194.0 49.0 %reduce-scatter.2.cloned.1.call-done = bf16[1024,256]{1,0:T(8,128)(2,1)} async-done(((bf16[1024,2048]{1,0:T(8,128)(2,1)}), bf16[1024,256]{1,0:T(8,128)(2,1)}) %reduce-scatter.2.cloned.1.call-update) | async-done | bytes 524304 | tf_op jit(solution)/shard_map/reduce_scatter | solution.py:136
  (73 shorter events, 3.0 us)
Async XLA Ops:
  6.5 184.2 %copy-start = (bf16[256,2048]{1,0:T(8,128)(2,1)S(1)}, bf16[256,2048]{1,0:T(8,128)(2,1)}, u32[]{:S(2)}) copy-start(bf16[256,2048]{1,0:T(8,128)(2,1)} %param.9) | copy-start | bytes 3145732
  6.5 4.9 %copy-start.2 = (bf16[1024,256]{1,0:T(8,128)(2,1)S(1)}, bf16[1024,256]{1,0:T(8,128)(2,1)}, u32[]{:S(2)}) copy-start(bf16[1024,256]{1,0:T(8,128)(2,1)} %param.7) | copy-start | bytes 1572868
  6.5 166.1 %all-gather.2.cloned.1.call-start = ((), (), s32[]{:S(2)}) async-start(), calls=%async_computation.1 | async-start | bytes 1064960 | tf_op jit(solution)/shard_map/all_gather | solution.py:114
  8.2 1.3 copy-start.15
  11.4 11.8 %copy-start.3 = (bf16[1024,256]{1,0:T(8,128)(2,1)S(1)}, bf16[1024,256]{1,0:T(8,128)(2,1)}, u32[]{:S(2)}) copy-start(bf16[1024,256]{1,0:T(8,128)(2,1)} %param.5) | copy-start | bytes 1572868
  12.4 11.0 %copy-start.4 = (bf16[1024,256]{1,0:T(8,128)(2,1)S(1)}, bf16[1024,256]{1,0:T(8,128)(2,1)}, u32[]{:S(2)}) copy-start(bf16[1024,256]{1,0:T(8,128)(2,1)} %param.6) | copy-start | bytes 1572868
  19.2 38.5 %collective-permute-start = (bf16[2,256,256]{1,2,0:T(8,128)(2,1)}, bf16[2,256,256]{1,2,0:T(8,128)(2,1)}, u32[]{:S(2)}, u32[]{:S(2)}) collective-permute-start(bf16[2,256,256]{1,2,0:T(8,128)(2,1)} %pad_maximum_fusion), channel_id=1, source_target_pairs={{0,8},{8,0},{16,24},{24,16},{32,40},{40,32},{48,56},{56,48},{64,72... | collective-permute-start | bytes 786440 | tf_op jit(solution)/shard_map/ppermute | solution.py:12
  30.9 212.1 %reduce-scatter.2.cloned.1.call-start = ((), (), s32[]{:S(2)}) async-start(), calls=%async_computation.2 | async-start | bytes 4718592 | tf_op jit(solution)/shard_map/reduce_scatter | solution.py:136
  41.4 10.5 %collective-permute-start.2 = (bf16[2,64,256]{1,2,0:T(8,128)(2,1)S(1)}, bf16[2,64,256]{1,2,0:T(8,128)(2,1)S(1)}, u32[]{:S(2)}, u32[]{:S(2)}) collective-permute-start(bf16[2,64,256]{1,2,0:T(8,128)(2,1)S(1)} %pad_maximum_fusion.1), channel_id=1, source_target_pairs={{0,8},{8,0},{16,24},{24,16},{32,40},{40,32},{48,56},{56,48},{64,72... | collective-permute-start | bytes 196616 | tf_op jit(solution)/shard_map/ppermute | solution.py:12
  45.5 3.2 %copy-start.5 = (pred[1024,1024]{0,1:T(8,128)(4,1)S(1)}, pred[1024,1024]{0,1:T(8,128)(4,1)}, u32[]{:S(2)}) copy-start(pred[1024,1024]{0,1:T(8,128)(4,1)} %iota_compare_fusion) | copy-start | bytes 3145732
  48.7 3.2 %copy-start.1 = (f32[2,1024,1024]{1,2,0:T(8,128)}, f32[2,1024,1024]{1,2,0:T(8,128)S(1)}, u32[]{:S(2)}) copy-start(f32[2,1024,1024]{1,2,0:T(8,128)S(1)} %get-tuple-element.37) | copy-start | bytes 25165828
  48.7 3.2 %copy-start.10 = (f32[2,1024]{1,0:T(2,128)}, f32[2,1024]{1,0:T(2,128)S(1)}, u32[]{:S(2)}) copy-start(f32[2,1024]{1,0:T(2,128)S(1)} %get-tuple-element.36) | copy-start | bytes 24580
  52.1 8.8 %collective-permute-start.3 = (bf16[2,128,256]{1,2,0:T(8,128)(2,1)S(1)}, bf16[2,128,256]{1,2,0:T(8,128)(2,1)S(1)}, u32[]{:S(2)}, u32[]{:S(2)}) collective-permute-start(bf16[2,128,256]{1,2,0:T(8,128)(2,1)S(1)} %maximum_select_fusion.5), channel_id=1, source_target_pairs={{0,16},{8,24},{16,0},{24,8},{32,48},{40,56},{48,32},{56,40},{64,80... | collective-permute-start | bytes 393224 | tf_op jit(solution)/shard_map/ppermute | solution.py:12
  58.9 16.9 %collective-permute-start.1 = (bf16[2,512,256]{1,2,0:T(8,128)(2,1)S(1)}, bf16[2,512,256]{1,2,0:T(8,128)(2,1)S(1)}, u32[]{:S(2)}, u32[]{:S(2)}) collective-permute-start(bf16[2,512,256]{1,2,0:T(8,128)(2,1)S(1)} %maximum_select_fusion.2), channel_id=1, source_target_pairs={{0,16},{8,24},{16,0},{24,8},{32,48},{40,56},{48,32},{56,40},{64,80... | collective-permute-start | bytes 1572872 | tf_op jit(solution)/shard_map/ppermute | solution.py:12
  61.0 9.0 %collective-permute-start.4 = (bf16[2,256,256]{1,2,0:T(8,128)(2,1)S(1)}, bf16[2,256,256]{1,2,0:T(8,128)(2,1)S(1)}, u32[]{:S(2)}, u32[]{:S(2)}) collective-permute-start(bf16[2,256,256]{1,2,0:T(8,128)(2,1)S(1)} %maximum_select_fusion.4), channel_id=1, source_target_pairs={{0,32},{8,40},{16,48},{24,56},{32,0},{40,8},{48,16},{56,24},{64,96... | collective-permute-start | bytes 786440 | tf_op jit(solution)/shard_map/ppermute | solution.py:12
  70.9 28.4 %collective-permute-start.5 = (bf16[2,512,256]{1,2,0:T(8,128)(2,1)}, bf16[2,512,256]{1,2,0:T(8,128)(2,1)}, u32[]{:S(2)}, u32[]{:S(2)}) collective-permute-start(bf16[2,512,256]{1,2,0:T(8,128)(2,1)} %maximum_select_fusion.3), channel_id=1, source_target_pairs={{0,64},{8,72},{16,80},{24,88},{32,96},{40,104},{48,112},{56,120},{... | collective-permute-start | bytes 1572872 | tf_op jit(solution)/shard_map/ppermute | solution.py:12
  85.4 15.8 %copy-start.7 = (pred[64,1024]{1,0:T(8,128)(4,1)S(1)}, pred[64,1024]{1,0:T(8,128)(4,1)}, u32[]{:S(2)}) copy-start(pred[64,1024]{1,0:T(8,128)(4,1)} %iota_compare_fusion.2) | copy-start | bytes 196612
  85.4 15.9 %copy-start.8 = (bf16[64,2,128]{2,1,0:T(2,128)(2,1)S(1)}, bf16[64,2,128]{2,1,0:T(2,128)(2,1)}, u32[]{:S(2)}) copy-start(bf16[64,2,128]{2,1,0:T(2,128)(2,1)} %get-tuple-element.8) | copy-start | bytes 98308
  103.9 74.4 %copy-start.9 = (pred[16,1024]{1,0:T(8,128)(4,1)S(1)}, pred[16,1024]{1,0:T(8,128)(4,1)}, u32[]{:S(2)}) copy-start(pred[16,1024]{1,0:T(8,128)(4,1)} %iota_compare_fusion.3) | copy-start | bytes 49156
  181.5 1.8 copy-start.11
  181.5 1.8 copy-start.12
  181.5 1.8 copy-start.13
  181.5 1.8 copy-start.14
  181.5 1.9 copy-start.6
Sparse Core Ops, SparseCore 0:
  31.0 141.6 all-gather.1
  194.1 48.8 reduce-scatter.1
where the time goes:
time: 252 us; the launch traced here: 250 us
  waiting for transfers between devices  132 us (52%)
  local copies, waits for them, and re-layouts  37 us (15%)
  other arithmetic  27.8 us (11%)
  starting transfers between devices  21.5 us (9%)
  matrix products  18 us (7%)
  between operations  13.8 us (5%)
    all_gather x1, waiting for transfers between devices, shards(): whole_pairs = lax.all_gather(whole_pairs, 'seq', axis=1, tiled=True)  68.7 us
    reduce_scatter x1, waiting for transfers between devices, shards(): lax.psum_scatter(partial_term.astype(jnp.bfloat16), 'head', scatter_dimen...  49 us
    ppermute x6, starting transfers between devices, from_partner(): return lax.ppermute(value, axis, pairs)  21.5 us
    ppermute x6, waiting for transfers between devices, from_partner(): return lax.ppermute(value, axis, pairs)  13.9 us
    reduce_sum x3, other arithmetic, choose_rows(): return jnp.sum(masked, axis=1, dtype=source.dtype)  12.7 us
    dot_general x4, matrix products, attend(): jnp.einsum('hqk,khd->qhd', weights.astype(jnp.bfloat16), value_grid, pref...  9.33 us
    another operation x9, local copies, waits for them, and re-layouts, choose_rows(): source.reshape(count, dilation_step, source.shape[1], source.shape[2])  7.94 us
    dot_general x4, matrix products, attend(): jnp.einsum('qhd,khd->hqk', chosen_q, key_grid, preferred_element_type=jnp...  5.42 us
  transfers between devices with their start and end apart: 8, of which 3 were waited for; matrix products, arithmetic and copies ran while one was open for 20% of the time, Pallas kernels for 0%

commit v1 on v0

v1 whole, which is shorter than its diff:
```python
import math

import jax
import jax.numpy as jnp
from jax import lax
from jax.experimental import pallas as pl
from jax.experimental.pallas import tpu as pltpu
from jax.sharding import PartitionSpec as P

HEAD_DIM = 128
SCALE = HEAD_DIM ** (-0.5)
SCALE2 = SCALE * math.log2(math.e)
NEG = -1e30
F32 = jnp.float32
BF16 = jnp.bfloat16
STEPS = (4, 16, 64)
VMEM = pl.BlockSpec(memory_space=pltpu.VMEM)
SMEM = pl.BlockSpec(memory_space=pltpu.SMEM)
PARAMS = pltpu.CompilerParams(vmem_limit_bytes=48 << 20)


def half(head):
    return slice(head * HEAD_DIM, (head + 1) * HEAD_DIM)


def rows_of(offset, total, step):
    return pl.ds(offset, total // step, stride=step)


def call(kernel, out, specs, scratch=()):
    return pl.pallas_call(
        kernel,
        out_shape=out,
        in_specs=specs,
        out_specs=jax.tree.map(lambda _: VMEM, out),
        scratch_shapes=scratch,
        compiler_params=PARAMS,
    )


def shape(dims, dtype):
    return jax.ShapeDtypeStruct(dims, dtype)


def pick_kernel(off, q, k, v, near, middle, whole, own_q, wide):
    rows = q.shape[0]
    for head in range(2):
        for slot, source in enumerate((q, k, v)):
            wide[slot] = source[:, half(head)].astype(F32)

        def pick(slot, level):
            return wide[slot, rows_of(off[head, level], rows, STEPS[level]), :].astype(BF16)

        count = [rows // step for step in STEPS]
        own_q[:, half(head)] = pick(0, 0)
        parts = (pick(1, 0), pick(2, 0), pick(0, 1), pick(0, 2))
        for target in range(near.shape[0]):
            at = 0
            for part in parts:
                near[target, at : at + part.shape[0], half(head)] = part
                at += part.shape[0]
        for level, out in ((1, middle), (2, whole)):
            keys, values = pick(1, level), pick(2, level)
            for target in range(out.shape[0]):
                out[target, : count[level], half(head)] = keys
                out[target, count[level] :, half(head)] = values


def local_kernel(off, q, k, v, early, mixed, logs):
    rows = q.shape[0]
    block = 256
    for head in range(2):
        for first in range(0, rows, block):
            last = first + block
            scores = lax.dot_general(
                q[first:last, half(head)], k[:last, half(head)], (((1,), (1,)), ((), ())), preferred_element_type=F32
            )
            query = first + lax.broadcasted_iota(jnp.int32, scores.shape, 0)
            key = lax.broadcasted_iota(jnp.int32, scores.shape, 1)
            scores = jnp.where(key <= query, scores, NEG)
            top = jnp.max(scores, axis=-1, keepdims=True)
            weights = jnp.exp2((scores - top) * SCALE2)
            total = jnp.sum(weights, axis=-1, keepdims=True)
            out = jnp.dot(weights.astype(BF16), v[:last, half(head)], preferred_element_type=F32) / total
            mixed[head, first:last, :] = out
            logs[head, first:last, :] = jnp.broadcast_to(top * SCALE + jnp.log(total), out.shape)
            for target in range(early.shape[0]):
                early[target, first:last, half(head)] = out.astype(BF16)
        line = lax.broadcasted_iota(jnp.int32, (16, HEAD_DIM), 0)
        marks = jnp.where(line == 0, off[head, 0], jnp.where(line == 1, off[head, 1], off[head, 2]))
        for target in range(early.shape[0]):
            early[target, rows:, half(head)] = marks.astype(F32).astype(BF16)


def near_kernel(own_q, near, mixed, logs):
    count = own_q.shape[0]
    place = lax.rem(lax.axis_index("seq"), near.shape[0]) * count
    for head in range(2):
        keys = near[:, :count, half(head)].reshape(-1, HEAD_DIM)
        values = near[:, count : 2 * count, half(head)].reshape(-1, HEAD_DIM)
        scores = lax.dot_general(own_q[:, half(head)], keys, (((1,), (1,)), ((), ())), preferred_element_type=F32)
        query = place + lax.broadcasted_iota(jnp.int32, scores.shape, 0)
        key = lax.broadcasted_iota(jnp.int32, scores.shape, 1)
        scores = jnp.where(key <= query, scores, NEG)
        top = jnp.max(scores, axis=-1, keepdims=True)
        weights = jnp.exp2((scores - top) * SCALE2)
        total = jnp.sum(weights, axis=-1, keepdims=True)
        out = jnp.dot(weights.astype(BF16), values, preferred_element_type=F32) / total
        mixed[head] = out
        logs[head] = jnp.broadcast_to(top * SCALE + jnp.log(total), out.shape)


def far_kernel(near, middle, whole, back):
    across = near.shape[0]
    seq = lax.axis_index("seq")
    column, line = lax.rem(seq, across), lax.div(seq, across)
    skip = 512
    at = 0
    for level, source in ((1, middle), (2, whole)):
        blocks = source.shape[0]
        count = source.shape[1] // 2
        place = lax.rem(line, blocks) if level == 1 else line
        logs = []
        for head in range(2):
            queries = near[:, skip + at : skip + at + count, half(head)].reshape(-1, HEAD_DIM)
            keys = source[:, :count, half(head)].reshape(-1, HEAD_DIM)
            values = source[:, count:, half(head)].reshape(-1, HEAD_DIM)
            scores = lax.dot_general(queries, keys, (((1,), (1,)), ((), ())), preferred_element_type=F32)
            query = place * (across * count) + lax.broadcasted_iota(jnp.int32, scores.shape, 0)
            key = lax.broadcasted_iota(jnp.int32, scores.shape, 1)
            key = (lax.div(key, count) * across + column) * count + lax.rem(key, count)
            kept = key <= query
            scores = jnp.where(kept, scores, NEG)
            top = jnp.max(scores, axis=-1, keepdims=True)
            weights = jnp.where(kept, jnp.exp2((scores - top) * SCALE2), 0.0)
            total = jnp.sum(weights, axis=-1, keepdims=True)
            some = total > 0.0
            safe = jnp.where(some, total, 1.0)
            out = jnp.dot(weights.astype(BF16), values, preferred_element_type=F32) / safe
            logs.append(jnp.where(some, top * SCALE + jnp.log(safe), NEG))
            back[:, at : at + count, half(head)] = out.reshape(across, count, HEAD_DIM)
        lane = lax.broadcasted_iota(jnp.int32, (across * count, HEAD_DIM), 1)
        both = jnp.where(lane < HEAD_DIM // 2, logs[0], logs[1])
        back[:, at : at + count, 2 * HEAD_DIM :] = both.reshape(across, count, HEAD_DIM)
        at += count


def merge(parts):
    top = parts[0][1]
    for _, log in parts[1:]:
        top = jnp.maximum(top, log)
    total, out = 0.0, 0.0
    for value, log in parts:
        share = jnp.exp(log - top)
        total = total + share
        out = out + share * value
    return out / total, top + jnp.log(total)


def merge_kernel(off, mixed, logs, near_mixed, near_logs, back, late, run, run_logs):
    rows = mixed.shape[1]
    for head in range(2):
        run[head] = mixed[head]
        run_logs[head] = logs[head]
        at = 0
        for level, step in enumerate(STEPS):
            count = rows // step
            where = rows_of(off[head, level], rows, step)
            if level == 0:
                new = (near_mixed[head], near_logs[head])
            else:
                parts = []
                for source in range(back.shape[0]):
                    lane = 2 * HEAD_DIM + head * (HEAD_DIM // 2)
                    log = back[source, at : at + count, lane : lane + 1]
                    parts.append(
                        (back[source, at : at + count, half(head)], jnp.broadcast_to(log, (count, HEAD_DIM)))
                    )
                new = merge(parts)
                at += count
            out, log = merge([(run[head, where, :], run_logs[head, where, :]), new])
            run[head, where, :] = out
            run_logs[head, where, :] = log
        at = 0
        for level, step in enumerate(STEPS):
            count = rows // step
            final = run[head, rows_of(off[head, level], rows, step), :].astype(BF16)
            for target in range(late.shape[0]):
                late[target, at : at + count, half(head)] = final
            at += count


def project_kernel(marks, early, late, weight, send, keep, wide, whole):
    rows = send.shape[0]
    for group in range(early.shape[0]):
        for head in range(2):
            slot = 2 * group + head
            wide[slot] = early[group, :rows, half(head)].astype(F32)
            at = 0
            for level, step in enumerate(STEPS):
                count = rows // step
                wide[slot, rows_of(marks[group, level, head], rows, step), :] = late[
                    group, at : at + count, half(head)
                ].astype(F32)
                at += count
            whole[:, half(slot)] = wide[slot].astype(BF16)
    core = lax.rem(lax.axis_index("head"), 2)
    width = keep.shape[1]

    def product(which):
        columns = pl.ds(pl.multiple_of(which * width, width), width)
        return jnp.dot(whole[...], weight[:, columns], preferred_element_type=F32)

    send[...] = product(1 - core).astype(BF16)
    keep[...] = product(core)


def shards(queries, keys, values, offsets, w_out):
    rows, width = queries.shape
    spread, heads = lax.axis_size("seq"), lax.axis_size("head")
    across, cores = 4, 2
    lines, chips = spread // across, heads // cores
    along_y = [[line * across + y for y in range(across)] for line in range(lines)]
    along_z = [[line * across + y for line in range(lines)] for y in range(across)]
    blocks_z = [[(4 * b + line) * across + y for line in range(4)] for b in range(lines // 4) for y in range(across)]
    along_x = [[chip * cores + core for chip in range(chips)] for core in range(cores)]

    def swap(value, axis, groups):
        return lax.all_to_all(value, axis, 0, 0, axis_index_groups=groups)

    count = [rows // step for step in STEPS]
    near_rows = 2 * count[0] + count[1] + count[2]
    near, middle, whole, own_q = call(
        pick_kernel,
        (
            shape((across, near_rows, width), BF16),
            shape((4, 2 * count[1], width), BF16),
            shape((lines, 2 * count[2], width), BF16),
            shape((count[0], width), BF16),
        ),
        [SMEM, VMEM, VMEM, VMEM],
        [pltpu.VMEM((3, rows, HEAD_DIM), F32)],
    )(offsets, queries, keys, values)
    whole = swap(whole, "seq", along_z)
    near = swap(near, "seq", along_y)
    middle = swap(middle, "seq", blocks_z)
    weight = w_out.reshape(width, chips, cores * width).transpose(1, 0, 2)
    weight = swap(weight, "head", along_x).reshape(chips * width, cores * width)
    early, mixed, logs = call(
        local_kernel,
        (
            shape((chips, rows + 16, width), BF16),
            shape((2, rows, HEAD_DIM), F32),
            shape((2, rows, HEAD_DIM), F32),
        ),
        [SMEM, VMEM, VMEM, VMEM],
    )(offsets, queries, keys, values)
    early = swap(early, "head", along_x)
    marks = early[:, rows : rows + 3, ::HEAD_DIM].astype(jnp.int32)
    near_mixed, near_logs = call(
        near_kernel,
        (shape((2, count[0], HEAD_DIM), F32), shape((2, count[0], HEAD_DIM), F32)),
        [VMEM, VMEM],
    )(own_q, near)
    back = call(
        far_kernel,
        shape((across, count[1] + count[2], 3 * HEAD_DIM), F32),
        [VMEM, VMEM, VMEM],
    )(near, middle, whole)
    back = swap(back, "seq", along_y)
    late = call(
        merge_kernel,
        shape((chips, sum(count), width), BF16),
        [SMEM] + [VMEM] * 5,
        [pltpu.VMEM((2, rows, HEAD_DIM), F32), pltpu.VMEM((2, rows, HEAD_DIM), F32)],
    )(offsets, mixed, logs, near_mixed, near_logs, back)
    late = swap(late, "head", along_x)
    send, keep = call(
        project_kernel,
        (shape((rows, width), BF16), shape((rows, width), F32)),
        [SMEM, VMEM, VMEM, VMEM],
        [pltpu.VMEM((2 * chips, rows, HEAD_DIM), F32), pltpu.VMEM((rows, chips * width), BF16)],
    )(marks, early, late, weight)
    other = lax.ppermute(send, "head", [(device, device ^ 1) for device in range(heads)])
    return (keep + other.astype(F32)).astype(BF16)


def solution(mesh):
    in_specs = (
        P("seq", "head"),
        P("seq", "head"),
        P("seq", "head"),
        P("head", None),
        P("head", None),
    )
    out_specs = P("seq", "head")
    return jax.shard_map(shards, mesh=mesh, in_specs=in_specs, out_specs=out_specs, check_vma=False)
```

time: 252 us -> 144 us (0.57)
  waiting for transfers between devices: 132 us -> 39.5 us
  blocking collectives: 0 us -> 31 us
  other arithmetic: 27.8 us -> 0.92 us
  local copies, waits for them, and re-layouts: 37 us -> 16.1 us
  starting transfers between devices: 21.5 us -> 42.2 us
  matrix products: 18 us -> 0 us
  between operations: 13.8 us -> 0.17 us
  Pallas kernels: 0 us -> 12.8 us
    all_gather x1 -> x0, waiting for transfers between devices: 68.7 us -> none  [shards(): whole_pairs = lax.all_gather(whole_pairs, 'seq', axis=1, tiled=True)]
    reduce_scatter x1 -> x0, waiting for transfers between devices: 49 us -> none  [shards(): lax.psum_scatter(partial_term.astype(jnp.bfloat16), 'head', scatter_dimen...]
    all_to_all x0 -> x5, waiting for transfers between devices: none -> 37.9 us  [swap(): return lax.all_to_all(value, axis, 0, 0, axis_index_groups=groups)]
    all_to_all x0 -> x2, blocking collectives: none -> 31 us  [swap(): return lax.all_to_all(value, axis, 0, 0, axis_index_groups=groups)]
    all_to_all x0 -> x5, starting transfers between devices: none -> 29.9 us  [swap(): return lax.all_to_all(value, axis, 0, 0, axis_index_groups=groups)]
    dot_general x9 -> x0, matrix products: 18 us -> none  [the longest x4 9.33 us: attend(): jnp.einsum('hqk,khd->qhd', weights.astype(jnp.bfloat16), value_grid, pref...]
    reduce_sum x7 -> x0, other arithmetic: 16.9 us -> none  [the longest x3 12.7 us: choose_rows(): return jnp.sum(masked, axis=1, dtype=source.dtype)]
    another operation x16 -> x0, local copies, waits for them, and re-layouts: 12.9 us -> none  [the longest x9 7.94 us: choose_rows(): source.reshape(count, dilation_step, source.shape[1], source.shape[2])]
  transfers between devices with their start and end apart: 8 -> 6, of which waited for: 3 -> 5; matrix products, arithmetic and copies ran while one was open for 20% -> 1% of each run, Pallas kernels for 0% -> 6%
where the time goes in v1:
time: 144 us; the launch traced here: 143 us
  starting transfers between devices  42.2 us (29%)
  waiting for transfers between devices  39.5 us (27%)
  blocking collectives  31 us (22%)
  local copies, waits for them, and re-layouts  16.1 us (11%)
  Pallas kernels  12.8 us (9%)
    all_to_all x5, waiting for transfers between devices, swap(): return lax.all_to_all(value, axis, 0, 0, axis_index_groups=groups)  37.9 us
    all_to_all x2, blocking collectives, swap(): return lax.all_to_all(value, axis, 0, 0, axis_index_groups=groups)  31 us
    all_to_all x5, starting transfers between devices, swap(): return lax.all_to_all(value, axis, 0, 0, axis_index_groups=groups)  29.9 us
    unnamed x42, local copies, waits for them, and re-layouts  14.9 us
    ppermute x1, starting transfers between devices, shards(): lax.ppermute(send, 'head', [(device, device ^ 1) for device in range(head...  12.3 us
    pallas_call x1, Pallas kernels, shards(): call(local_kernel, (shape((chips, rows + 16, width), BF16), shape((2, row...  4.02 us
    pallas_call x1, Pallas kernels, shards(): call(project_kernel, (shape((rows, width), BF16), shape((rows, width), F3...  2.98 us
  transfers between devices with their start and end apart: 6, of which 5 were waited for; matrix products, arithmetic and copies ran while one was open for 1% of the time, Pallas kernels for 6%

profile of v1, /device:TPU:1, one launch (start us, length us, event | category | flops | bytes accessed | tf_op | source)
XLA Modules:
  0.0 142.6 jit_solution(13638782438690812254)
XLA Ops:
  0.0 0.0 copy-start.4
  0.0 1.0 copy-done.4
  1.0 0.0 copy-start.6
  1.0 1.0 copy-done.6
  2.1 0.0 copy-start.8
  2.1 1.0 copy-done.8
  3.1 0.0 copy-start.18
  3.1 0.7 copy-done.18
  3.8 1.8 %shard_map.56 = (bf16[4,592,256]{2,1,0:T(8,128)(2,1)S(1)}, bf16[4,128,256]{2,1,0:T(8,128)(2,1)S(1)}, bf16[16,32,256]{2,1,0:T(8,128)(2,1)}, bf16[256,256]{1,0:T(8,128)(2,1)S(1)}) custom-call(s32[2,3]{1,0:T(2,128)S(1)} %copy-done.18, bf16[1024,256]{1,0:T(8,128)(2,1)S(1)} %copy-done.4, bf16[1024,256]{1,0:T(8,128)(2,1)S(1)} %copy-done.6, ...), custom_call_target="tpu_custom_call" | custom-call | tf_op jit(solution)/shard_map/pallas_call | solution.py:233
  5.6 0.0 copy-start.20
  5.7 12.4 %all_to_all.35.middle = bf16[4,128,256]{2,1,0:T(8,128)(2,1)} all-to-all(bf16[4,128,256]{2,1,0:T(8,128)(2,1)S(1)} %get-tuple-element.23), channel_id=1, replica_groups={{0,32,64,96},{8,40,72,104},{16,48,80,112},{24,56,88,120},{128,160,192,2..., dimensions={0} | all-to-all | bytes 524288 | tf_op jit(solution)/shard_map/all_to_all | solution.py:229
  18.1 18.5 %all_to_all.36.near = bf16[4,592,256]{2,1,0:T(8,128)(2,1)S(1)} all-to-all(bf16[4,592,256]{2,1,0:T(8,128)(2,1)S(1)} %get-tuple-element.20), channel_id=1, replica_groups={{0,8,16,24},{32,40,48,56},{64,72,80,88},{96,104,112,120},{128,136,144,1..., dimensions={0} | all-to-all | bytes 2424832 | tf_op jit(solution)/shard_map/all_to_all | solution.py:229
  36.6 13.9 %all-to-all-start.3 = ((bf16[16,32,256]{2,1,0:T(8,128)(2,1)}), bf16[16,32,256]{2,1,0:T(8,128)(2,1)S(1)}, u32[]{:S(2)}, u32[]{:S(2)}) async-start(bf16[16,32,256]{2,1,0:T(8,128)(2,1)} %get-tuple-element.24), calls=%async_computation.3 | async-start | bytes 524288 | tf_op jit(solution)/shard_map/all_to_all | solution.py:229
  50.5 0.0 copy-done.20
  50.5 1.1 copy.9
  51.6 11.7 %all-to-all-done.3.whole = bf16[16,32,256]{2,1,0:T(8,128)(2,1)S(1)} async-done(((bf16[16,32,256]{2,1,0:T(8,128)(2,1)}), bf16[16,32,256]{2,1,0:T(8,128)(2,1)S(1)}, u32[]{:S(2)}, u32[]{:S(2)}) %all-to-all-start.3) | async-done | bytes 262176 | tf_op jit(solution)/shard_map/all_to_all | solution.py:229
  63.3 0.0 copy-start.12
  63.3 0.7 copy-done.12
  64.0 0.0 copy-start.5
  64.0 0.0 copy-start.7
  64.0 4.1 %all-to-all-start.6 = ((bf16[4,256,512]{2,1,0:T(8,128)(2,1)}), bf16[4,256,512]{2,1,0:T(8,128)(2,1)S(1)}, u32[]{:S(2)}, u32[]{:S(2)}) async-start(bf16[4,256,512]{2,1,0:T(8,128)(2,1)} %bitcast.9), calls=%async_computation.6 | async-start | bytes 2097152 | tf_op jit(solution)/shard_map/all_to_all | solution.py:229
  68.1 0.0 copy-start.11
  68.1 0.9 copy-done.11
  69.1 0.0 copy-start.13
  69.1 0.9 copy-done.13
  70.0 0.7 shard_map.58
  70.8 0.0 copy-start.10
  70.8 0.8 copy-done.10
  71.6 6.3 %all-to-all-done.6 = bf16[4,256,512]{2,1,0:T(8,128)(2,1)S(1)} async-done(((bf16[4,256,512]{2,1,0:T(8,128)(2,1)}), bf16[4,256,512]{2,1,0:T(8,128)(2,1)S(1)}, u32[]{:S(2)}, u32[]{:S(2)}) %all-to-all-start.6) | async-done | bytes 1048608 | tf_op jit(solution)/shard_map/all_to_all | solution.py:229
  77.9 0.0 copy-start
  77.9 4.1 %all-to-all-start.4 = ((f32[4,80,384]{2,1,0:T(8,128)}), f32[4,80,384]{2,1,0:T(8,128)}, u32[]{:S(2)}, u32[]{:S(2)}) async-start(f32[4,80,384]{2,1,0:T(8,128)} %copy-done.10), calls=%async_computation.4 | async-start | bytes 983040 | tf_op jit(solution)/shard_map/all_to_all | solution.py:229
  82.0 0.0 copy-done.5
  82.0 0.0 copy-done.7
  82.0 0.0 copy-done.19
  82.1 0.0 copy-start.9
  82.1 1.0 copy-done.9
  83.1 4.0 %shard_map.55 = (bf16[4,1040,256]{2,1,0:T(8,128)(2,1)S(1)}, f32[2,1024,128]{2,1,0:T(8,128)S(1)}, f32[2,1024,128]{2,1,0:T(8,128)S(1)}) custom-call(s32[2,3]{1,0:T(2,128)S(1)} %copy-done.19, bf16[1024,256]{1,0:T(8,128)(2,1)S(1)} %copy-done.5, bf16[1024,256]{1,0:T(8,128)(2,1)S(1)} %copy-done.7, bf16[1024,256]{1,0:T(8,128)(2,1)S(1)} %copy-done.9), custom_call_target="tpu_custom_call" | custom-call | tf_op jit(solution)/shard_map/pallas_call | solution.py:249
  87.1 0.0 copy-start.3
  87.1 1.4 copy-done.3
  88.5 0.0 copy-start.14
  88.5 1.0 copy-done.14
  89.5 0.0 copy-start.16
  89.5 1.0 copy-done.16
  90.5 0.0 all-to-all-done.4.back
  90.5 0.0 copy-done
  90.5 3.6 %all-to-all-start = ((bf16[4,1040,256]{2,1,0:T(8,128)(2,1)}), bf16[4,1040,256]{2,1,0:T(8,128)(2,1)S(1)}, u32[]{:S(2)}, u32[]{:S(2)}) async-start(bf16[4,1040,256]{2,1,0:T(8,128)(2,1)} %copy-done.3), calls=%async_computation | async-start | bytes 4259840 | tf_op jit(solution)/shard_map/all_to_all | solution.py:229
  94.1 1.3 shard_map.57
  95.4 0.0 copy-start.15
  95.4 1.2 copy-done.15
  96.6 0.0 copy-start.17
  96.6 1.2 copy-done.17
  97.9 0.0 copy-start.1
  97.9 1.9 %shard_map.59 = bf16[4,336,256]{2,1,0:T(8,128)(2,1)S(1)} custom-call(s32[2,3]{1,0:T(2,128)S(1)} %copy-done.19, f32[2,1024,128]{2,1,0:T(8,128)S(1)} %copy-done.15, f32[2,1024,128]{2,1,0:T(8,128)S(1)} %copy-done.17, f32[2,256,128]{2,1,0:T(8,128)S(1)} %get-tuple-element.21.near_mixed, f32[2,256,128]{2,1,0:T(8,128)S(1)} %get-tuple-element.22.near_logs, ...), custom_call_target="tpu_custom_call" | custom-call | tf_op jit(solution)/shard_map/pallas_call | solution.py:271
  99.8 0.0 copy-start.2
  99.8 0.8 copy-done.2
  100.6 11.8 %all-to-all-done.early = bf16[4,1040,256]{2,1,0:T(8,128)(2,1)S(1)} async-done(((bf16[4,1040,256]{2,1,0:T(8,128)(2,1)}), bf16[4,1040,256]{2,1,0:T(8,128)(2,1)S(1)}, u32[]{:S(2)}, u32[]{:S(2)}) %all-to-all-start) | async-done | bytes 2129952 | tf_op jit(solution)/shard_map/all_to_all | solution.py:229
  112.4 4.2 %all-to-all-start.5 = ((bf16[4,336,256]{2,1,0:T(8,128)(2,1)}), bf16[4,336,256]{2,1,0:T(8,128)(2,1)}, u32[]{:S(2)}, u32[]{:S(2)}) async-start(bf16[4,336,256]{2,1,0:T(8,128)(2,1)} %copy-done.2), calls=%async_computation.5 | async-start | bytes 1376256 | tf_op jit(solution)/shard_map/all_to_all | solution.py:229
  116.6 0.1 slice.3
  116.7 8.2 %all-to-all-done.5.late = bf16[4,336,256]{2,1,0:T(8,128)(2,1)} async-done(((bf16[4,336,256]{2,1,0:T(8,128)(2,1)}), bf16[4,336,256]{2,1,0:T(8,128)(2,1)}, u32[]{:S(2)}, u32[]{:S(2)}) %all-to-all-start.5) | async-done | bytes 688160 | tf_op jit(solution)/shard_map/all_to_all | solution.py:229
  124.8 0.0 copy-done.1
  124.8 3.0 %shard_map.60 = (bf16[1024,256]{1,0:T(8,128)(2,1)S(1)}, f32[1024,256]{1,0:T(8,128)S(1)}) custom-call(s32[4,3,2]{2,1,0:T(4,128)S(1)} %convert_element_type.9.marks, bf16[4,1040,256]{2,1,0:T(8,128)(2,1)S(1)} %all-to-all-done.early, bf16[4,336,256]{2,1,0:T(8,128)(2,1)} %all-to-all-done.5.late, bf16[1024,512]{1,0:T(8,128)(2,1)S(1)} %bitcast.8), custom_call_target="tpu_custom_call" | custom-call | tf_op jit(solution)/shard_map/pallas_call | solution.py:278
  127.8 12.3 %collective-permute-start = (bf16[1024,256]{1,0:T(8,128)(2,1)S(1)}, bf16[1024,256]{1,0:T(8,128)(2,1)S(1)}, u32[]{:S(2)}, u32[]{:S(2)}) collective-permute-start(bf16[1024,256]{1,0:T(8,128)(2,1)S(1)} %get-tuple-element.26), channel_id=1, source_target_pairs={{0,1},{1,0},{2,3},{3,2},{4,5},{5,4},{6,7},{7,6},{8,9},{9,8},{10,11... | collective-permute-start | bytes 1572872 | tf_op jit(solution)/shard_map/ppermute | solution.py:284
  140.2 1.5 %collective-permute-done = bf16[1024,256]{1,0:T(8,128)(2,1)S(1)} collective-permute-done((bf16[1024,256]{1,0:T(8,128)(2,1)S(1)}, bf16[1024,256]{1,0:T(8,128)(2,1)S(1)}, u32[]{:S(2)}, u32[]{:S(2)}) %collective-permute-start) | collective-permute-done | bytes 524320 | tf_op jit(solution)/shard_map/ppermute | solution.py:284
  141.7 0.9 add_convert_fusion
  (2 shorter events, 0.0 us)
Async XLA Ops:
  0.0 1.0 copy-start.4
  1.0 1.0 copy-start.6
  2.1 1.0 copy-start.8
  3.1 0.7 copy-start.18
  5.6 44.9 %copy-start.20 = (bf16[256,2048]{1,0:T(8,128)(2,1)S(1)}, bf16[256,2048]{1,0:T(8,128)(2,1)}, u32[]{:S(2)}) copy-start(bf16[256,2048]{1,0:T(8,128)(2,1)} %param.9) | copy-start | bytes 3145732
  36.6 26.6 %all-to-all-start.3 = ((bf16[16,32,256]{2,1,0:T(8,128)(2,1)}), bf16[16,32,256]{2,1,0:T(8,128)(2,1)S(1)}, u32[]{:S(2)}, u32[]{:S(2)}) async-start(bf16[16,32,256]{2,1,0:T(8,128)(2,1)} %get-tuple-element.24), calls=%async_computation.3 | async-start | bytes 524288 | tf_op jit(solution)/shard_map/all_to_all | solution.py:229
  63.3 0.7 copy-start.12
  64.0 18.0 %copy-start.5 = (bf16[1024,256]{1,0:T(8,128)(2,1)S(1)}, bf16[1024,256]{1,0:T(8,128)(2,1)}, u32[]{:S(2)}) copy-start(bf16[1024,256]{1,0:T(8,128)(2,1)} %q.3) | copy-start | bytes 1572868
  64.0 18.0 %copy-start.7 = (bf16[1024,256]{1,0:T(8,128)(2,1)S(1)}, bf16[1024,256]{1,0:T(8,128)(2,1)}, u32[]{:S(2)}) copy-start(bf16[1024,256]{1,0:T(8,128)(2,1)} %k.3) | copy-start | bytes 1572868
  64.0 18.1 %copy-start.19 = (s32[2,3]{1,0:T(2,128)S(1)}, s32[2,3]{1,0:T(2,128)}, u32[]{:S(2)}) copy-start(s32[2,3]{1,0:T(2,128)} %off.5) | copy-start | bytes 76
  64.0 13.9 %all-to-all-start.6 = ((bf16[4,256,512]{2,1,0:T(8,128)(2,1)}), bf16[4,256,512]{2,1,0:T(8,128)(2,1)S(1)}, u32[]{:S(2)}, u32[]{:S(2)}) async-start(bf16[4,256,512]{2,1,0:T(8,128)(2,1)} %bitcast.9), calls=%async_computation.6 | async-start | bytes 2097152 | tf_op jit(solution)/shard_map/all_to_all | solution.py:229
  68.1 0.9 copy-start.11
  69.1 0.9 copy-start.13
  70.8 0.8 copy-start.10
  77.9 12.6 %copy-start = (bf16[4,256,512]{2,1,0:T(8,128)(2,1)}, bf16[4,256,512]{2,1,0:T(8,128)(2,1)S(1)}, u32[]{:S(2)}) copy-start(bf16[4,256,512]{2,1,0:T(8,128)(2,1)S(1)} %all-to-all-done.6) | copy-start | bytes 3145732
  77.9 12.6 %all-to-all-start.4 = ((f32[4,80,384]{2,1,0:T(8,128)}), f32[4,80,384]{2,1,0:T(8,128)}, u32[]{:S(2)}, u32[]{:S(2)}) async-start(f32[4,80,384]{2,1,0:T(8,128)} %copy-done.10), calls=%async_computation.4 | async-start | bytes 983040 | tf_op jit(solution)/shard_map/all_to_all | solution.py:229
  82.1 1.0 copy-start.9
  87.1 1.4 copy-start.3
  88.5 1.0 copy-start.14
  89.5 1.0 copy-start.16
  90.5 21.9 %all-to-all-start = ((bf16[4,1040,256]{2,1,0:T(8,128)(2,1)}), bf16[4,1040,256]{2,1,0:T(8,128)(2,1)S(1)}, u32[]{:S(2)}, u32[]{:S(2)}) async-start(bf16[4,1040,256]{2,1,0:T(8,128)(2,1)} %copy-done.3), calls=%async_computation | async-start | bytes 4259840 | tf_op jit(solution)/shard_map/all_to_all | solution.py:229
  95.4 1.2 copy-start.15
  96.6 1.2 copy-start.17
  97.9 27.0 %copy-start.1 = (bf16[4,256,512]{2,1,0:T(8,128)(2,1)S(1)}, bf16[4,256,512]{2,1,0:T(8,128)(2,1)}, u32[]{:S(2)}) copy-start(bf16[4,256,512]{2,1,0:T(8,128)(2,1)} %copy-done) | copy-start | bytes 3145732
  99.8 0.9 copy-start.2
  112.4 12.4 %all-to-all-start.5 = ((bf16[4,336,256]{2,1,0:T(8,128)(2,1)}), bf16[4,336,256]{2,1,0:T(8,128)(2,1)}, u32[]{:S(2)}, u32[]{:S(2)}) async-start(bf16[4,336,256]{2,1,0:T(8,128)(2,1)} %copy-done.2), calls=%async_computation.5 | async-start | bytes 1376256 | tf_op jit(solution)/shard_map/all_to_all | solution.py:229
  127.8 13.8 %collective-permute-start = (bf16[1024,256]{1,0:T(8,128)(2,1)S(1)}, bf16[1024,256]{1,0:T(8,128)(2,1)S(1)}, u32[]{:S(2)}, u32[]{:S(2)}) collective-permute-start(bf16[1024,256]{1,0:T(8,128)(2,1)S(1)} %get-tuple-element.26), channel_id=1, source_target_pairs={{0,1},{1,0},{2,3},{3,2},{4,5},{5,4},{6,7},{7,6},{8,9},{9,8},{10,11... | collective-permute-start | bytes 1572872 | tf_op jit(solution)/shard_map/ppermute | solution.py:284

commit v2 on v1

v2 whole, which is shorter than its diff:
```python
import math

import jax
import jax.numpy as jnp
from jax import lax
from jax.experimental import pallas as pl
from jax.experimental.pallas import tpu as pltpu
from jax.sharding import PartitionSpec as P

HEAD_DIM = 128
SCALE = HEAD_DIM ** (-0.5)
SCALE2 = SCALE * math.log2(math.e)
NEG = -1e30
F32 = jnp.float32
BF16 = jnp.bfloat16
STEPS = (4, 16, 64)
VMEM = pl.BlockSpec(memory_space=pltpu.VMEM)
SMEM = pl.BlockSpec(memory_space=pltpu.SMEM)
HBM = pl.BlockSpec(memory_space=pltpu.HBM)
ANY = pl.BlockSpec(memory_space=pl.ANY)
PARAMS = pltpu.CompilerParams(vmem_limit_bytes=20 << 20)


def half(head):
    return slice(head * HEAD_DIM, (head + 1) * HEAD_DIM)


def rows_of(offset, total, step):
    return pl.ds(offset, total // step, stride=step)


def call(kernel, out, in_specs, out_specs, scratch=()):
    return pl.pallas_call(
        kernel,
        out_shape=out,
        in_specs=in_specs,
        out_specs=out_specs,
        scratch_shapes=scratch,
        compiler_params=PARAMS,
    )


def shape(dims, dtype):
    return jax.ShapeDtypeStruct(dims, dtype)


def stay(value):
    return pltpu.with_memory_space_constraint(value, pltpu.HBM)


def copy(source, target, sem):
    moved = pltpu.make_async_copy(source, target, sem)
    moved.start()
    return moved


def attend(queries, keys, values, kept):
    scores = lax.dot_general(queries, keys, (((1,), (1,)), ((), ())), preferred_element_type=F32)
    scores = jnp.where(kept, scores, NEG)
    top = jnp.max(scores, axis=-1, keepdims=True)
    weights = jnp.where(kept, jnp.exp2((scores - top) * SCALE2), 0.0)
    total = jnp.sum(weights, axis=-1, keepdims=True)
    some = total > 0.0
    safe = jnp.where(some, total, 1.0)
    out = jnp.dot(weights.astype(BF16), values, preferred_element_type=F32) / safe
    return out, jnp.where(some, top * SCALE + jnp.log(safe), NEG)


def pick_kernel(off_in, q, k, v, near_out, near_z, own_q, off, raw, wide, near, pack, query, sems):
    rows = q.shape[0]
    count = [rows // step for step in STEPS]
    first = copy(off_in, off, sems.at[0])
    loads = [copy(source, raw.at[slot], sems.at[1 + slot]) for slot, source in enumerate((k, v, q))]
    moves = []
    first.wait()
    for slot in range(3):
        loads[slot].wait()
        for head in range(2):
            wide[slot, head] = raw[slot, :, half(head)].astype(F32)
            picks = [
                wide[slot, head, rows_of(off[head, level], rows, step), :].astype(BF16)
                for level, step in enumerate(STEPS)
            ]
            if slot < 2:
                near[slot * count[0] : (slot + 1) * count[0], half(head)] = picks[0]
                pack[slot * count[1] : (slot + 1) * count[1], half(head)] = picks[1]
                at = 2 * count[1] + slot * count[2]
                pack[at : at + count[2], half(head)] = picks[2]
            else:
                query[:, half(head)] = picks[0]
                at = 2 * count[0]
                near[at : at + count[1], half(head)] = picks[1]
                near[at + count[1] : at + count[1] + count[2], half(head)] = picks[2]
        if slot == 1:
            moves = [copy(pack, near_z, sems.at[4])]
    moves.append(copy(query, own_q, sems.at[8]))
    moves += [copy(near, near_out.at[target], sems.at[9 + target]) for target in range(4)]
    for moved in moves:
        moved.wait()


def relay_kernel(z0, z1, z2, z3, _1, _2, far_z, part, sems):
    line = lax.rem(lax.div(lax.axis_index("seq"), 4), 4)
    loads = [
        copy(z.at[pl.ds(128, 32), :], part.at[lax.rem(line + 4 - shift, 4)], sems.at[shift])
        for shift, z in enumerate((z0, z1, z2, z3))
    ]
    for moved in loads:
        moved.wait()
    moves = [copy(part, far_z.at[target], sems.at[4 + target]) for target in range(far_z.shape[0])]
    for moved in moves:
        moved.wait()


def local_kernel(off_in, q, k, v, w, own, out1, out2, out3, mixed, logs, off, raw, wide, early, some, some_logs, held, sems):
    chip = lax.div(lax.axis_index("head"), 2)
    width = q.shape[1]
    moves = []
    column = copy(w, held, sems.at[16])
    rows = q.shape[0]
    block = 256
    first_copy = copy(off_in, off, sems.at[0])
    loads = [copy(source, raw.at[slot], sems.at[1 + slot]) for slot, source in enumerate((q, k, v))]
    for moved in loads:
        moved.wait()
    first_copy.wait()
    column.wait()
    for shift, out in enumerate((out1, out2, out3), 1):
        for part in range(2):
            place = pl.multiple_of((2 * lax.rem(chip + shift, 4) + part) * width, width)
            at = 3 * rows // 4 + 16 + part * width
            moves.append(copy(held.at[:, pl.ds(place, width)], out.at[pl.ds(at, width), :], sems.at[2 + 2 * shift + part]))
    row = lax.broadcasted_iota(jnp.int32, (block, block), 0)
    kept = lax.broadcasted_iota(jnp.int32, (block, block), 1) <= row
    for head in range(2):
        for first in range(0, rows, block):
            last = first + block
            query = raw[0, first:last, half(head)]
            pieces = [(first, last)] + ([(0, first)] if first else [])
            scores = [
                lax.dot_general(
                    query, raw[1, low:high, half(head)], (((1,), (1,)), ((), ())), preferred_element_type=F32
                )
                for low, high in pieces
            ]
            scores[0] = jnp.where(kept, scores[0], NEG)
            top = jnp.max(scores[0], axis=-1, keepdims=True)
            for piece in scores[1:]:
                top = jnp.maximum(top, jnp.max(piece, axis=-1, keepdims=True))
            total, out = 0.0, 0.0
            for piece, (low, high) in zip(scores, pieces):
                weights = jnp.exp2((piece - top) * SCALE2)
                total = total + jnp.sum(weights, axis=-1, keepdims=True)
                out = out + jnp.dot(weights.astype(BF16), raw[2, low:high, half(head)], preferred_element_type=F32)
            out = out / total
            wide[0, first:last, :] = out
            wide[1, first:last, :] = jnp.broadcast_to(top * SCALE + jnp.log(total), out.shape)
        part = rows // 4
        for turn in range(3):
            where = rows_of(lax.rem(off[head, 0] + turn + 1, 4), rows, 4)
            early[turn * part : (turn + 1) * part, half(head)] = wide[0, where, :].astype(BF16)
        line = lax.broadcasted_iota(jnp.int32, (16, HEAD_DIM), 0)
        marks = jnp.where(line == 0, off[head, 0], jnp.where(line == 1, off[head, 1], off[head, 2]))
        early[3 * part :, half(head)] = marks.astype(F32).astype(BF16)
        at = 0
        for level, step in enumerate(STEPS):
            count = rows // step
            where = rows_of(off[head, level], rows, step)
            some[head, at : at + count, :] = wide[0, where, :]
            some_logs[head, at : at + count, :] = wide[1, where, :]
            at += count
    for slot, out in enumerate((own, out1, out2, out3)):
        moves.append(copy(early, out.at[pl.ds(0, 3 * rows // 4 + 16), :], sems.at[10 + slot]))
    moves += [copy(some, mixed, sems.at[14]), copy(some_logs, logs, sems.at[15])]
    for moved in moves:
        moved.wait()


def near_kernel(own_q, near_in, mixed, logs, queries, near, some, some_logs, sems):
    count = own_q.shape[0]
    loads = [copy(own_q, queries, sems.at[0]), copy(near_in.at[:, pl.ds(0, 2 * count), :], near, sems.at[3])]
    for moved in loads:
        moved.wait()
    mine = lax.rem(lax.axis_index("seq"), 4)
    for head in range(2):
        keys = near[:, :count, half(head)].reshape(-1, HEAD_DIM)
        values = near[:, count:, half(head)].reshape(-1, HEAD_DIM)
        dims = (count, 4 * count)
        query = mine * count + lax.broadcasted_iota(jnp.int32, dims, 0)
        key = lax.broadcasted_iota(jnp.int32, dims, 1)
        out, log = attend(queries[:, half(head)], keys, values, key <= query)
        some[head] = out
        some_logs[head] = jnp.broadcast_to(log, out.shape)
    moves = [copy(some, mixed, sems.at[1]), copy(some_logs, logs, sems.at[2])]
    for moved in moves:
        moved.wait()


def far_kernel(near_in, z0, z1, z2, z3, far_z, back, near, zs, hi, part, sems):
    seq = lax.axis_index("seq")
    mine, line = lax.rem(seq, 4), lax.div(seq, 4)
    loads = [copy(z.at[pl.ds(0, 128), :], zs.at[shift], sems.at[2 + shift]) for shift, z in enumerate((z0, z1, z2, z3))]
    loads.append(copy(far_z, hi, sems.at[6]))
    loads.append(copy(near_in.at[:, pl.ds(512, 80), :], near, sems.at[0]))
    for moved in loads:
        moved.wait()
    at = 0
    for level, count in ((1, 64), (2, 16)):
        place = lax.rem(line, 4) if level == 1 else line
        logs = []
        for head in range(2):
            queries = near[:, at : at + count, half(head)].reshape(-1, HEAD_DIM)
            if level == 1:
                keys = zs[:, :count, half(head)].reshape(-1, HEAD_DIM)
                values = zs[:, count:, half(head)].reshape(-1, HEAD_DIM)
            else:
                keys = hi[:, :, :count, half(head)].reshape(-1, HEAD_DIM)
                values = hi[:, :, count:, half(head)].reshape(-1, HEAD_DIM)
            dims = (4 * count, keys.shape[0])
            row = lax.broadcasted_iota(jnp.int32, dims, 0)
            query = place * 4 * count + row
            key = lax.broadcasted_iota(jnp.int32, dims, 1)
            source = lax.rem(place + 4 - lax.div(key, count), 4) if level == 1 else lax.div(key, count)
            key = (source * 4 + mine) * count + lax.rem(key, count)
            out, log = attend(queries, keys, values, key <= query)
            logs.append(log)
            part[:, at : at + count, half(head)] = out.reshape(4, count, HEAD_DIM)
        lane = lax.broadcasted_iota(jnp.int32, (4 * count, HEAD_DIM), 1)
        both = jnp.where(lane < HEAD_DIM // 2, logs[0], logs[1])
        part[:, at : at + count, 2 * HEAD_DIM :] = both.reshape(4, count, HEAD_DIM)
        at += count
    moves = [copy(part, back, sems.at[1])]
    for moved in moves:
        moved.wait()


def merge(parts):
    top = parts[0][1]
    for _, log in parts[1:]:
        top = jnp.maximum(top, log)
    total, out = 0.0, 0.0
    for value, log in parts:
        share = jnp.exp(log - top)
        total = total + share
        out = out + share * value
    return out / total, top + jnp.log(total)


def merge_kernel(off_in, m_in, l_in, nm_in, nl_in, back_in, _1, _2, _3, late, off, mixed, logs, near_mixed, near_logs, back, run, run_logs, pack, sems):
    rows = run.shape[1]
    places = ((off_in, off), (m_in, mixed), (l_in, logs), (nm_in, near_mixed), (nl_in, near_logs), (back_in, back))
    loads = [copy(source, target, sems.at[slot]) for slot, (source, target) in enumerate(places)]
    for moved in loads:
        moved.wait()
    for head in range(2):
        at = 0
        for level, step in enumerate(STEPS):
            count = rows // step
            where = rows_of(off[head, level], rows, step)
            run[head, where, :] = mixed[head, at : at + count, :]
            run_logs[head, where, :] = logs[head, at : at + count, :]
            at += count
        at = 0
        for level, step in enumerate(STEPS):
            count = rows // step
            where = rows_of(off[head, level], rows, step)
            if level == 0:
                new = (near_mixed[head], near_logs[head])
            else:
                parts = []
                for source in range(4):
                    lane = 2 * HEAD_DIM + head * (HEAD_DIM // 2)
                    log = back[source, at : at + count, lane : lane + 1]
                    parts.append(
                        (back[source, at : at + count, half(head)], jnp.broadcast_to(log, (count, HEAD_DIM)))
                    )
                new = merge(parts)
                at += count
            out, log = merge([(run[head, where, :], run_logs[head, where, :]), new])
            run[head, where, :] = out
            run_logs[head, where, :] = log
        at = 0
        for level, step in enumerate(STEPS):
            count = rows // step
            pack[at : at + count, half(head)] = run[head, rows_of(off[head, level], rows, step), :].astype(BF16)
            at += count
    moves = [copy(pack, late.at[target], sems.at[6 + target]) for target in range(4)]
    for moved in moves:
        moved.wait()


def project_kernel(marks, own, e1, e2, e3, late, w, send, keep, e0, wide, whole, weight, sems):
    rows, width = keep.shape
    part = rows // 4
    most = 3 * part
    place = lax.axis_index("head")
    chip, core = lax.div(place, 2), lax.rem(place, 2)
    column = pl.multiple_of(2 * chip * width, width)
    loads = [
        copy(own.at[pl.ds(0, most), :], e0, sems.at[0]),
        copy(w.at[:, pl.ds(column, 2 * width)], weight, sems.at[1]),
    ]
    for shift, pack in ((1, e1), (2, e2), (3, e3), (0, e0)):
        group = lax.rem(chip + 4 - shift, 4)
        if shift == 0:
            for moved in loads:
                moved.wait()
        for head in range(2):
            slot = 2 * shift + head
            first = marks[shift, 0, head]
            for turn in range(3):
                block = pl.multiple_of(lax.rem(first + turn + 1, 4) * part, part)
                whole[pl.ds(block, part), half(slot)] = pack[turn * part : (turn + 1) * part, half(head)]
            whole[pl.ds(pl.multiple_of(first * part, part), part), half(slot)] = late[group, :part, half(head)]
            at = part
            for level in (1, 2):
                step = STEPS[level] // 4
                count = part // step
                mark = marks[shift, level, head]
                block = pl.multiple_of(lax.rem(mark, 4) * part, part)
                held = 2 * slot + level - 1
                wide[held] = whole[pl.ds(block, part), half(slot)].astype(F32)
                wide[held, pl.ds(lax.div(mark, 4), count, stride=step), :] = late[
                    group, at : at + count, half(head)
                ].astype(F32)
                whole[pl.ds(block, part), half(slot)] = wide[held].astype(BF16)
                at += count

    def product(which):
        total = 0.0
        for shift, pack in enumerate((None, e1, e2, e3)):
            if shift:
                chosen = pack[pl.ds(pl.multiple_of(most + 16 + which * width, 16), width), :]
            else:
                chosen = weight[:, pl.ds(pl.multiple_of(which * width, width), width)]
            total = total + jnp.dot(
                whole[:, shift * width : (shift + 1) * width], chosen, preferred_element_type=F32
            )
        return total

    send[...] = product(1 - core).astype(BF16)
    keep[...] = product(core)


def finish_kernel(keep, other, out, wide):
    part = keep.shape[0] // 4
    for head in range(2):
        for turn in range(4):
            block = slice(turn * part, (turn + 1) * part)
            wide[head, pl.ds(turn, part, stride=4), :] = keep[block, half(head)] + other[block, half(head)].astype(F32)
        out[:, half(head)] = wide[head].astype(BF16)


def shards(queries, keys, values, offsets, w_out):
    rows, width = queries.shape
    spread, heads = lax.axis_size("seq"), lax.axis_size("head")
    lines = spread // 4
    along_y = [[4 * line + y for y in range(4)] for line in range(lines)]
    far_lines = [[(4 * b + line) * 4 + y for b in range(4)] for line in range(4) for y in range(4)]
    along_x = [[2 * chip + core for chip in range(4)] for core in range(2)]
    dma = pltpu.SemaphoreType.DMA

    def swap(value, axis, groups):
        return lax.all_to_all(value, axis, 0, 0, axis_index_groups=groups)

    def shift_z(value, by):
        hops = [(4 * (4 * b + z) + y, 4 * (4 * b + (z + by) % 4) + y) for b in range(lines // 4) for z in range(4) for y in range(4)]
        return lax.ppermute(value, "seq", hops)

    def shift_x(value, by):
        return lax.ppermute(value, "head", [(place, (place + 2 * by) % heads) for place in range(heads)])

    count = [rows // step for step in STEPS]
    late_rows = sum(count)
    near_rows = 2 * count[0] + count[1] + count[2]
    z_rows = 2 * count[1] + 2 * count[2]
    queries, keys, values, offsets, w_out = map(stay, (queries, keys, values, offsets, w_out))
    near, near_z, own_q = call(
        pick_kernel,
        (pltpu.HBM((4, near_rows, width), BF16), pltpu.HBM((z_rows, width), BF16), pltpu.HBM((count[0], width), BF16)),
        [HBM] * 4,
        (HBM,) * 3,
        [
            pltpu.SMEM((2, 3), jnp.int32),
            pltpu.VMEM((3, rows, width), BF16),
            pltpu.VMEM((3, 2, rows, HEAD_DIM), F32),
            pltpu.VMEM((near_rows, width), BF16),
            pltpu.VMEM((z_rows, width), BF16),
            pltpu.VMEM((count[0], width), BF16),
            dma((13,)),
        ],
    )(offsets, queries, keys, values)
    zs = [stay(part) for part in [near_z] + [shift_z(near_z, by) for by in (1, 2, 3)]]
    near = swap(near, "seq", along_y)
    most = 3 * rows // 4
    packed = pltpu.HBM((most + 16 + 2 * width, width), BF16)
    kept = pltpu.HBM((2, late_rows, HEAD_DIM), F32)
    early, *packs, mixed, logs = call(
        local_kernel,
        (pltpu.HBM((most + 16, width), BF16), packed, packed, packed, kept, kept),
        [HBM] * 5,
        (HBM,) * 6,
        [
            pltpu.SMEM((2, 3), jnp.int32),
            pltpu.VMEM((3, rows, width), BF16),
            pltpu.VMEM((2, rows, HEAD_DIM), F32),
            pltpu.VMEM((most + 16, width), BF16),
            pltpu.VMEM((2, late_rows, HEAD_DIM), F32),
            pltpu.VMEM((2, late_rows, HEAD_DIM), F32),
            pltpu.VMEM(w_out.shape, BF16),
            dma((17,)),
        ],
    )(offsets, queries, keys, values, w_out)
    far_z = call(
        relay_kernel, pltpu.HBM((4, 4, 2 * count[2], width), BF16), [ANY] * 4 + [HBM, ANY], HBM, [pltpu.VMEM((4, 2 * count[2], width), BF16), dma((8,))]
    )(*zs, stay(early), near)
    far_z = swap(far_z, "seq", far_lines)
    packs = [shift_x(pack, by) for by, pack in enumerate(packs, 1)]
    marks = jnp.stack([part[most : most + 3, ::HEAD_DIM] for part in [early] + packs]).astype(jnp.int32)
    near_mixed, near_logs = call(
        near_kernel,
        (pltpu.HBM((2, count[0], HEAD_DIM), F32),) * 2,
        [HBM, ANY],
        (HBM,) * 2,
        [
            pltpu.VMEM((count[0], width), BF16),
            pltpu.VMEM((4, 2 * count[0], width), BF16),
            pltpu.VMEM((2, count[0], HEAD_DIM), F32),
            pltpu.VMEM((2, count[0], HEAD_DIM), F32),
            dma((4,)),
        ],
    )(stay(own_q), near)
    back = call(
        far_kernel,
        pltpu.HBM((4, count[1] + count[2], 3 * HEAD_DIM), F32),
        [ANY] * 6,
        HBM,
        [
            pltpu.VMEM((4, count[1] + count[2], width), BF16),
            pltpu.VMEM((4, 2 * count[1], width), BF16),
            pltpu.VMEM((4, 4, 2 * count[2], width), BF16),
            pltpu.VMEM((4, count[1] + count[2], 3 * HEAD_DIM), F32),
            dma((7,)),
        ],
    )(near, *zs, far_z)
    back = swap(back, "seq", along_y)
    late = call(
        merge_kernel,
        pltpu.HBM((4, late_rows, width), BF16),
        [HBM] * 5 + [ANY] * 4,
        HBM,
        [
            pltpu.SMEM((2, 3), jnp.int32),
            pltpu.VMEM(mixed.shape, F32),
            pltpu.VMEM(mixed.shape, F32),
            pltpu.VMEM(near_mixed.shape, F32),
            pltpu.VMEM(near_mixed.shape, F32),
            pltpu.VMEM(back.shape, F32),
            pltpu.VMEM((2, rows, HEAD_DIM), F32),
            pltpu.VMEM((2, rows, HEAD_DIM), F32),
            pltpu.VMEM((late_rows, width), BF16),
            dma((10,)),
        ],
    )(offsets, *map(stay, (mixed, logs, near_mixed, near_logs)), back, *packs)
    late = swap(late, "head", along_x)
    send, keep = call(
        project_kernel,
        (shape((rows, width), BF16), shape((rows, width), F32)),
        [SMEM, HBM] + [VMEM] * 4 + [HBM],
        (VMEM,) * 2,
        [
            pltpu.VMEM((most, width), BF16),
            pltpu.VMEM((16, count[0], HEAD_DIM), F32),
            pltpu.VMEM((rows, 4 * width), BF16),
            pltpu.VMEM((width, 2 * width), BF16),
            dma((2,)),
        ],
    )(marks, stay(early), *packs, late, w_out)
    other = lax.ppermute(send, "head", [(place, place ^ 1) for place in range(heads)])
    return call(
        finish_kernel,
        shape((rows, width), BF16),
        [VMEM] * 2,
        VMEM,
        [pltpu.VMEM((2, rows, HEAD_DIM), F32)],
    )(keep, other)


def solution(mesh):
    in_specs = (
        P("seq", "head"),
        P("seq", "head"),
        P("seq", "head"),
        P("head", None),
        P("head", None),
    )
    out_specs = P("seq", "head")
    return jax.shard_map(shards, mesh=mesh, in_specs=in_specs, out_specs=out_specs, check_vma=False)
```

time: 144 us -> 105 us (0.73)
  blocking collectives: 31 us -> 0 us
  local copies, waits for them, and re-layouts: 16.1 us -> 1.68 us
  waiting for transfers between devices: 39.5 us -> 25.3 us
  Pallas kernels: 12.8 us -> 24 us
  starting transfers between devices: 42.2 us -> 52.6 us
    all_to_all x2 -> x0, blocking collectives: 31 us -> none  [swap(): return lax.all_to_all(value, axis, 0, 0, axis_index_groups=groups)]
    all_to_all x5 -> x4, waiting for transfers between devices: 37.9 us -> 11.4 us  [swap(): return lax.all_to_all(value, axis, 0, 0, axis_index_groups=groups)]
    unnamed x42 -> x8, local copies, waits for them, and re-layouts: 14.9 us -> 0.65 us
    ppermute x1 -> x7, starting transfers between devices: 12.3 us -> 25 us  [the longest x3 10.6 us: shift_x(): lax.ppermute(value, 'head', [(place, (place + 2 * by) % heads) for place...]
    ppermute x1 -> x7, waiting for transfers between devices: 1.51 us -> 13.9 us  [the longest x3 12.4 us: shift_x(): lax.ppermute(value, 'head', [(place, (place + 2 * by) % heads) for place...]
    pallas_call x5 -> x7, Pallas kernels: 9.78 us -> 20.7 us  [the longest x1 6.66 us: shards(): call(local_kernel, (pltpu.HBM((most + 16, width), BF16), packed, packed,...]
    all_to_all x5 -> x4, starting transfers between devices: 29.9 us -> 27.6 us  [swap(): return lax.all_to_all(value, axis, 0, 0, axis_index_groups=groups)]
  transfers between devices with their start and end apart: 6 -> 11, of which waited for: 5 -> 5; matrix products, arithmetic and copies ran while one was open for 1% -> 1% of each run, Pallas kernels for 6% -> 12%
where the time goes in v2:
time: 105 us; the launch traced here: 104 us
  starting transfers between devices  52.6 us (50%)
  waiting for transfers between devices  25.3 us (24%)
  Pallas kernels  24 us (23%)
  local copies, waits for them, and re-layouts  1.68 us (2%)
    all_to_all x4, starting transfers between devices, swap(): return lax.all_to_all(value, axis, 0, 0, axis_index_groups=groups)  27.6 us
    ppermute x3, waiting for transfers between devices, shift_x(): lax.ppermute(value, 'head', [(place, (place + 2 * by) % heads) for place...  12.4 us
    all_to_all x4, waiting for transfers between devices, swap(): return lax.all_to_all(value, axis, 0, 0, axis_index_groups=groups)  11.4 us
    ppermute x3, starting transfers between devices, shift_x(): lax.ppermute(value, 'head', [(place, (place + 2 * by) % heads) for place...  10.6 us
    ppermute x3, starting transfers between devices, shift_z(): return lax.ppermute(value, 'seq', hops)  10.4 us
    pallas_call x1, Pallas kernels, shards(): call(local_kernel, (pltpu.HBM((most + 16, width), BF16), packed, packed,...  6.66 us
    ppermute x1, starting transfers between devices, shards(): lax.ppermute(send, 'head', [(place, place ^ 1) for place in range(heads)])  4.05 us
    pallas_call x1, Pallas kernels, shards(): call(project_kernel, (shape((rows, width), BF16), shape((rows, width), F3...  3.26 us
  transfers between devices with their start and end apart: 11, of which 5 were waited for; matrix products, arithmetic and copies ran while one was open for 1% of the time, Pallas kernels for 12%

profile of v2, /device:TPU:1, one launch (start us, length us, event | category | flops | bytes accessed | tf_op | source)
XLA Modules:
  0.0 103.8 jit_solution(5673371847870684806)
XLA Ops:
  0.0 2.7 %shard_map.56 = (bf16[4,592,256]{2,1,0:T(8,128)(2,1)}, bf16[160,256]{1,0:T(8,128)(2,1)}, bf16[256,256]{1,0:T(8,128)(2,1)}) custom-call(s32[2,3]{1,0:T(2,128)} %off_in.5, bf16[1024,256]{1,0:T(8,128)(2,1)} %q.3, bf16[1024,256]{1,0:T(8,128)(2,1)} %k.3, bf16[1024,256]{1,0:T(8,128)(2,1)} %v.3), custom_call_target="tpu_custom_call" | custom-call | tf_op jit(solution)/shard_map/pallas_call | solution.py:378
  2.7 0.0 copy-start
  2.7 5.2 %all-to-all-start = ((bf16[4,592,256]{2,1,0:T(8,128)(2,1)}), bf16[4,592,256]{2,1,0:T(8,128)(2,1)S(1)}, u32[]{:S(2)}, u32[]{:S(2)}) async-start(bf16[4,592,256]{2,1,0:T(8,128)(2,1)} %get-tuple-element.25), calls=%async_computation | async-start | bytes 2424832 | tf_op jit(solution)/shard_map/all_to_all | solution.py:364
  7.9 0.0 copy-done
  7.9 6.2 %collective-permute-start.5 = (bf16[160,256]{1,0:T(8,128)(2,1)S(1)}, bf16[160,256]{1,0:T(8,128)(2,1)S(1)}, u32[]{:S(2)}, u32[]{:S(2)}) collective-permute-start(bf16[160,256]{1,0:T(8,128)(2,1)S(1)} %copy-done), channel_id=1, source_target_pairs={{0,96},{8,104},{16,112},{24,120},{32,0},{40,8},{48,16},{56,24},{64... | collective-permute-start | bytes 245768 | tf_op jit(solution)/shard_map/ppermute | solution.py:368
  14.2 1.9 %collective-permute-start.4 = (bf16[160,256]{1,0:T(8,128)(2,1)S(1)}, bf16[160,256]{1,0:T(8,128)(2,1)S(1)}, u32[]{:S(2)}, u32[]{:S(2)}) collective-permute-start(bf16[160,256]{1,0:T(8,128)(2,1)S(1)} %copy-done), channel_id=1, source_target_pairs={{0,64},{8,72},{16,80},{24,88},{32,96},{40,104},{48,112},{56,120},{... | collective-permute-start | bytes 245768 | tf_op jit(solution)/shard_map/ppermute | solution.py:368
  16.1 2.2 %collective-permute-start.3 = (bf16[160,256]{1,0:T(8,128)(2,1)S(1)}, bf16[160,256]{1,0:T(8,128)(2,1)S(1)}, u32[]{:S(2)}, u32[]{:S(2)}) collective-permute-start(bf16[160,256]{1,0:T(8,128)(2,1)S(1)} %copy-done), channel_id=1, source_target_pairs={{0,32},{8,40},{16,48},{24,56},{32,64},{40,72},{48,80},{56,88},{64,... | collective-permute-start | bytes 245768 | tf_op jit(solution)/shard_map/ppermute | solution.py:368
  18.3 6.7 %shard_map.55 = (bf16[784,256]{1,0:T(8,128)(2,1)}, bf16[1296,256]{1,0:T(8,128)(2,1)}, bf16[1296,256]{1,0:T(8,128)(2,1)}, bf16[1296,256]{1,0:T(8,128)(2,1)}, f32[...) custom-call(s32[2,3]{1,0:T(2,128)} %off_in.5, bf16[1024,256]{1,0:T(8,128)(2,1)} %q.3, bf16[1024,256]{1,0:T(8,128)(2,1)} %k.3, ...), custom_call_target="tpu_custom_call" | custom-call | tf_op jit(solution)/shard_map/pallas_call | solution.py:398
  25.0 0.0 collective-permute-done.5.z3
  25.0 0.0 copy-start.1
  25.0 0.0 collective-permute-done.4.z2
  25.0 0.0 copy-start.2
  25.0 0.0 collective-permute-done.3.z1
  25.0 0.0 copy-start.3
  25.0 0.0 all-to-all-done.near_in._2
  25.0 0.6 copy-done.1
  25.6 0.0 copy-done.2
  25.6 0.0 copy-done.3
  25.7 1.5 %shard_map.58 = bf16[4,4,32,256]{3,2,1,0:T(8,128)(2,1)} custom-call(bf16[160,256]{1,0:T(8,128)(2,1)} %get-tuple-element.28.z0, bf16[160,256]{1,0:T(8,128)(2,1)} %copy-done.3, bf16[160,256]{1,0:T(8,128)(2,1)} %copy-done.2, bf16[160,256]{1,0:T(8,128)(2,1)} %copy-done.1, bf16[784,256]{1,0:T(8,128)(2,1)} %get-tuple-element.18._1.own, ...), custom_call_target="tpu_custom_call" | custom-call | tf_op jit(solution)/shard_map/pallas_call | solution.py:414
  27.2 13.0 %all-to-all-start.1 = ((bf16[4,4,32,256]{3,2,1,0:T(8,128)(2,1)}), bf16[4,4,32,256]{3,2,1,0:T(8,128)(2,1)S(1)}, u32[]{:S(2)}, u32[]{:S(2)}) async-start(bf16[4,4,32,256]{3,2,1,0:T(8,128)(2,1)} %shard_map.58), calls=%async_computation.1 | async-start | bytes 524288 | tf_op jit(solution)/shard_map/all_to_all | solution.py:364
  40.2 3.1 %collective-permute-start = (bf16[1296,256]{1,0:T(8,128)(2,1)}, bf16[1296,256]{1,0:T(8,128)(2,1)S(1)}, u32[]{:S(2)}, u32[]{:S(2)}) collective-permute-start(bf16[1296,256]{1,0:T(8,128)(2,1)} %get-tuple-element.19), channel_id=1, source_target_pairs={{0,2},{1,3},{2,4},{3,5},{4,6},{5,7},{6,0},{7,1},{8,10},{9,11},{10,... | collective-permute-start | bytes 1990664 | tf_op jit(solution)/shard_map/ppermute | solution.py:371
  43.3 4.4 %collective-permute-start.1 = (bf16[1296,256]{1,0:T(8,128)(2,1)}, bf16[1296,256]{1,0:T(8,128)(2,1)S(1)}, u32[]{:S(2)}, u32[]{:S(2)}) collective-permute-start(bf16[1296,256]{1,0:T(8,128)(2,1)} %get-tuple-element.20), channel_id=1, source_target_pairs={{0,4},{1,5},{2,6},{3,7},{4,0},{5,1},{6,2},{7,3},{8,12},{9,13},{10,... | collective-permute-start | bytes 1990664 | tf_op jit(solution)/shard_map/ppermute | solution.py:371
  47.7 3.1 %collective-permute-start.2 = (bf16[1296,256]{1,0:T(8,128)(2,1)}, bf16[1296,256]{1,0:T(8,128)(2,1)S(1)}, u32[]{:S(2)}, u32[]{:S(2)}) collective-permute-start(bf16[1296,256]{1,0:T(8,128)(2,1)} %get-tuple-element.21), channel_id=1, source_target_pairs={{0,6},{1,7},{2,0},{3,1},{4,2},{5,3},{6,4},{7,5},{8,14},{9,15},{10,... | collective-permute-start | bytes 1990664 | tf_op jit(solution)/shard_map/ppermute | solution.py:371
  50.8 2.4 %all-to-all-done.1.far_z = bf16[4,4,32,256]{3,2,1,0:T(8,128)(2,1)S(1)} async-done(((bf16[4,4,32,256]{3,2,1,0:T(8,128)(2,1)}), bf16[4,4,32,256]{3,2,1,0:T(8,128)(2,1)S(1)}, u32[]{:S(2)}, u32[]{:S(2)}) %all-to-all-start.1) | async-done | bytes 262176 | tf_op jit(solution)/shard_map/all_to_all | solution.py:364
  53.2 2.5 %shard_map.59 = f32[4,80,384]{2,1,0:T(8,128)} custom-call(bf16[4,592,256]{2,1,0:T(8,128)(2,1)S(1)} %all-to-all-done.near_in._2, bf16[160,256]{1,0:T(8,128)(2,1)} %get-tuple-element.28.z0, bf16[160,256]{1,0:T(8,128)(2,1)} %copy-done.3, bf16[160,256]{1,0:T(8,128)(2,1)} %copy-done.2, bf16[160,256]{1,0:T(8,128)(2,1)} %copy-done.1, ...), custom_call_target="tpu_custom_call" | custom-call | tf_op jit(solution)/shard_map/pallas_call | solution.py:433
  55.8 4.9 %all-to-all-start.2 = ((f32[4,80,384]{2,1,0:T(8,128)}), f32[4,80,384]{2,1,0:T(8,128)}, u32[]{:S(2)}, u32[]{:S(2)}) async-start(f32[4,80,384]{2,1,0:T(8,128)} %shard_map.59), calls=%async_computation.2 | async-start | bytes 983040 | tf_op jit(solution)/shard_map/all_to_all | solution.py:364
  60.6 3.1 %shard_map.57 = (f32[2,256,128]{2,1,0:T(8,128)}, f32[2,256,128]{2,1,0:T(8,128)}) custom-call(bf16[256,256]{1,0:T(8,128)(2,1)} %get-tuple-element.24.own_q, bf16[4,592,256]{2,1,0:T(8,128)(2,1)S(1)} %all-to-all-done.near_in._2), custom_call_target="tpu_custom_call" | custom-call | tf_op jit(solution)/shard_map/pallas_call | solution.py:420
  63.8 0.0 collective-permute-done._1.e1
  63.8 9.2 %collective-permute-done.1._2.e2 = bf16[1296,256]{1,0:T(8,128)(2,1)S(1)} collective-permute-done((bf16[1296,256]{1,0:T(8,128)(2,1)}, bf16[1296,256]{1,0:T(8,128)(2,1)S(1)}, u32[]{:S(2)}, u32[]{:S(2)}) %collective-permute-start.1) | collective-permute-done | bytes 663584 | tf_op jit(solution)/shard_map/ppermute | solution.py:371
  73.0 3.2 %collective-permute-done.2._3.e3 = bf16[1296,256]{1,0:T(8,128)(2,1)S(1)} collective-permute-done((bf16[1296,256]{1,0:T(8,128)(2,1)}, bf16[1296,256]{1,0:T(8,128)(2,1)S(1)}, u32[]{:S(2)}, u32[]{:S(2)}) %collective-permute-start.2) | collective-permute-done | bytes 663584 | tf_op jit(solution)/shard_map/ppermute | solution.py:371
  76.2 0.0 all-to-all-done.2.back_in
  76.2 3.1 %shard_map.60 = bf16[4,336,256]{2,1,0:T(8,128)(2,1)} custom-call(s32[2,3]{1,0:T(2,128)} %off_in.5, f32[2,336,128]{2,1,0:T(8,128)} %get-tuple-element.22.m_in, f32[2,336,128]{2,1,0:T(8,128)} %get-tuple-element.23.l_in, f32[2,256,128]{2,1,0:T(8,128)} %get-tuple-element.26.nm_in, f32[2,256,128]{2,1,0:T(8,128)} %get-tuple-element.27.nl_in, ...), custom_call_target="tpu_custom_call" | custom-call | tf_op jit(solution)/shard_map/pallas_call | solution.py:447
  79.3 4.6 %all-to-all-start.3 = ((bf16[4,336,256]{2,1,0:T(8,128)(2,1)}), bf16[4,336,256]{2,1,0:T(8,128)(2,1)S(1)}, u32[]{:S(2)}, u32[]{:S(2)}) async-start(bf16[4,336,256]{2,1,0:T(8,128)(2,1)} %shard_map.60), calls=%async_computation.3 | async-start | bytes 1376256 | tf_op jit(solution)/shard_map/all_to_all | solution.py:364
  83.8 0.8 slice.12
  84.6 0.1 slice.13
  84.7 0.1 slice.14
  84.8 0.1 slice.15
  84.9 9.0 %all-to-all-done.3.late = bf16[4,336,256]{2,1,0:T(8,128)(2,1)S(1)} async-done(((bf16[4,336,256]{2,1,0:T(8,128)(2,1)}), bf16[4,336,256]{2,1,0:T(8,128)(2,1)S(1)}, u32[]{:S(2)}, u32[]{:S(2)}) %all-to-all-start.3) | async-done | bytes 688160 | tf_op jit(solution)/shard_map/all_to_all | solution.py:364
  93.9 3.3 %shard_map.61 = (bf16[1024,256]{1,0:T(8,128)(2,1)S(1)}, f32[1024,256]{1,0:T(8,128)S(1)}) custom-call(s32[4,3,2]{2,1,0:T(4,128)S(1)} %maximum_convert_fusion.marks, bf16[784,256]{1,0:T(8,128)(2,1)} %get-tuple-element.18._1.own, bf16[1296,256]{1,0:T(8,128)(2,1)S(1)} %collective-permute-done._1.e1, bf16[1296,256]{1,0:T(8,128)(2,1)S(1)} %collective-permute-done.1._2.e2, ...), custom_call_target="tpu_custom_call" | custom-call | tf_op jit(solution)/shard_map/pallas_call | solution.py:466
  97.2 4.0 %collective-permute-start.6 = (bf16[1024,256]{1,0:T(8,128)(2,1)S(1)}, bf16[1024,256]{1,0:T(8,128)(2,1)S(1)}, u32[]{:S(2)}, u32[]{:S(2)}) collective-permute-start(bf16[1024,256]{1,0:T(8,128)(2,1)S(1)} %get-tuple-element.30), channel_id=1, source_target_pairs={{0,1},{1,0},{2,3},{3,2},{4,5},{5,4},{6,7},{7,6},{8,9},{9,8},{10,11... | collective-permute-start | bytes 1572872 | tf_op jit(solution)/shard_map/ppermute | solution.py:479
  101.2 1.5 %collective-permute-done.6.other = bf16[1024,256]{1,0:T(8,128)(2,1)S(1)} collective-permute-done((bf16[1024,256]{1,0:T(8,128)(2,1)S(1)}, bf16[1024,256]{1,0:T(8,128)(2,1)S(1)}, u32[]{:S(2)}, u32[]{:S(2)}) %collective-permute-start.6) | collective-permute-done | bytes 524320 | tf_op jit(solution)/shard_map/ppermute | solution.py:479
  102.7 1.0 %shard_map.62 = bf16[1024,256]{1,0:T(8,128)(2,1)} custom-call(f32[1024,256]{1,0:T(8,128)S(1)} %get-tuple-element.29.keep, bf16[1024,256]{1,0:T(8,128)(2,1)S(1)} %collective-permute-done.6.other), custom_call_target="tpu_custom_call" | custom-call | tf_op jit(solution)/shard_map/pallas_call | solution.py:480
  (1 shorter events, 0.0 us)
Async XLA Ops:
  2.7 5.2 %copy-start = (bf16[160,256]{1,0:T(8,128)(2,1)S(1)}, bf16[160,256]{1,0:T(8,128)(2,1)}, u32[]{:S(2)}) copy-start(bf16[160,256]{1,0:T(8,128)(2,1)} %get-tuple-element.28.z0) | copy-start | bytes 245764
  2.7 22.3 %all-to-all-start = ((bf16[4,592,256]{2,1,0:T(8,128)(2,1)}), bf16[4,592,256]{2,1,0:T(8,128)(2,1)S(1)}, u32[]{:S(2)}, u32[]{:S(2)}) async-start(bf16[4,592,256]{2,1,0:T(8,128)(2,1)} %get-tuple-element.25), calls=%async_computation | async-start | bytes 2424832 | tf_op jit(solution)/shard_map/all_to_all | solution.py:364
  7.9 17.1 %collective-permute-start.5 = (bf16[160,256]{1,0:T(8,128)(2,1)S(1)}, bf16[160,256]{1,0:T(8,128)(2,1)S(1)}, u32[]{:S(2)}, u32[]{:S(2)}) collective-permute-start(bf16[160,256]{1,0:T(8,128)(2,1)S(1)} %copy-done), channel_id=1, source_target_pairs={{0,96},{8,104},{16,112},{24,120},{32,0},{40,8},{48,16},{56,24},{64... | collective-permute-start | bytes 245768 | tf_op jit(solution)/shard_map/ppermute | solution.py:368
  14.2 10.8 %collective-permute-start.4 = (bf16[160,256]{1,0:T(8,128)(2,1)S(1)}, bf16[160,256]{1,0:T(8,128)(2,1)S(1)}, u32[]{:S(2)}, u32[]{:S(2)}) collective-permute-start(bf16[160,256]{1,0:T(8,128)(2,1)S(1)} %copy-done), channel_id=1, source_target_pairs={{0,64},{8,72},{16,80},{24,88},{32,96},{40,104},{48,112},{56,120},{... | collective-permute-start | bytes 245768 | tf_op jit(solution)/shard_map/ppermute | solution.py:368
  16.1 8.9 %collective-permute-start.3 = (bf16[160,256]{1,0:T(8,128)(2,1)S(1)}, bf16[160,256]{1,0:T(8,128)(2,1)S(1)}, u32[]{:S(2)}, u32[]{:S(2)}) collective-permute-start(bf16[160,256]{1,0:T(8,128)(2,1)S(1)} %copy-done), channel_id=1, source_target_pairs={{0,32},{8,40},{16,48},{24,56},{32,64},{40,72},{48,80},{56,88},{64,... | collective-permute-start | bytes 245768 | tf_op jit(solution)/shard_map/ppermute | solution.py:368
  25.0 0.6 copy-start.1
  25.0 0.6 copy-start.2
  25.0 0.7 copy-start.3
  27.2 26.0 %all-to-all-start.1 = ((bf16[4,4,32,256]{3,2,1,0:T(8,128)(2,1)}), bf16[4,4,32,256]{3,2,1,0:T(8,128)(2,1)S(1)}, u32[]{:S(2)}, u32[]{:S(2)}) async-start(bf16[4,4,32,256]{3,2,1,0:T(8,128)(2,1)} %shard_map.58), calls=%async_computation.1 | async-start | bytes 524288 | tf_op jit(solution)/shard_map/all_to_all | solution.py:364
  40.2 23.5 %collective-permute-start = (bf16[1296,256]{1,0:T(8,128)(2,1)}, bf16[1296,256]{1,0:T(8,128)(2,1)S(1)}, u32[]{:S(2)}, u32[]{:S(2)}) collective-permute-start(bf16[1296,256]{1,0:T(8,128)(2,1)} %get-tuple-element.19), channel_id=1, source_target_pairs={{0,2},{1,3},{2,4},{3,5},{4,6},{5,7},{6,0},{7,1},{8,10},{9,11},{10,... | collective-permute-start | bytes 1990664 | tf_op jit(solution)/shard_map/ppermute | solution.py:371
  43.3 29.7 %collective-permute-start.1 = (bf16[1296,256]{1,0:T(8,128)(2,1)}, bf16[1296,256]{1,0:T(8,128)(2,1)S(1)}, u32[]{:S(2)}, u32[]{:S(2)}) collective-permute-start(bf16[1296,256]{1,0:T(8,128)(2,1)} %get-tuple-element.20), channel_id=1, source_target_pairs={{0,4},{1,5},{2,6},{3,7},{4,0},{5,1},{6,2},{7,3},{8,12},{9,13},{10,... | collective-permute-start | bytes 1990664 | tf_op jit(solution)/shard_map/ppermute | solution.py:371
  47.7 28.4 %collective-permute-start.2 = (bf16[1296,256]{1,0:T(8,128)(2,1)}, bf16[1296,256]{1,0:T(8,128)(2,1)S(1)}, u32[]{:S(2)}, u32[]{:S(2)}) collective-permute-start(bf16[1296,256]{1,0:T(8,128)(2,1)} %get-tuple-element.21), channel_id=1, source_target_pairs={{0,6},{1,7},{2,0},{3,1},{4,2},{5,3},{6,4},{7,5},{8,14},{9,15},{10,... | collective-permute-start | bytes 1990664 | tf_op jit(solution)/shard_map/ppermute | solution.py:371
  55.8 20.4 %all-to-all-start.2 = ((f32[4,80,384]{2,1,0:T(8,128)}), f32[4,80,384]{2,1,0:T(8,128)}, u32[]{:S(2)}, u32[]{:S(2)}) async-start(f32[4,80,384]{2,1,0:T(8,128)} %shard_map.59), calls=%async_computation.2 | async-start | bytes 983040 | tf_op jit(solution)/shard_map/all_to_all | solution.py:364
  79.3 14.6 %all-to-all-start.3 = ((bf16[4,336,256]{2,1,0:T(8,128)(2,1)}), bf16[4,336,256]{2,1,0:T(8,128)(2,1)S(1)}, u32[]{:S(2)}, u32[]{:S(2)}) async-start(bf16[4,336,256]{2,1,0:T(8,128)(2,1)} %shard_map.60), calls=%async_computation.3 | async-start | bytes 1376256 | tf_op jit(solution)/shard_map/all_to_all | solution.py:364
  97.2 5.6 %collective-permute-start.6 = (bf16[1024,256]{1,0:T(8,128)(2,1)S(1)}, bf16[1024,256]{1,0:T(8,128)(2,1)S(1)}, u32[]{:S(2)}, u32[]{:S(2)}) collective-permute-start(bf16[1024,256]{1,0:T(8,128)(2,1)S(1)} %get-tuple-element.30), channel_id=1, source_target_pairs={{0,1},{1,0},{2,3},{3,2},{4,5},{5,4},{6,7},{7,6},{8,9},{9,8},{10,11... | collective-permute-start | bytes 1572872 | tf_op jit(solution)/shard_map/ppermute | solution.py:479

commit v3 on v2

--- a/solution.py
+++ b/solution.py
@@ -114,33 +114,29 @@
 
 def local_kernel(off_in, q, k, v, w, own, out1, out2, out3, mixed, logs, off, raw, wide, early, some, some_logs, held, sems):
     chip = lax.div(lax.axis_index("head"), 2)
-    width = q.shape[1]
-    moves = []
-    column = copy(w, held, sems.at[16])
-    rows = q.shape[0]
-    block = 256
+    rows, width = q.shape
+    block = 512
+    part = rows // 4
     first_copy = copy(off_in, off, sems.at[0])
-    loads = [copy(source, raw.at[slot], sems.at[1 + slot]) for slot, source in enumerate((q, k, v))]
-    for moved in loads:
-        moved.wait()
-    first_copy.wait()
-    column.wait()
-    for shift, out in enumerate((out1, out2, out3), 1):
-        for part in range(2):
-            place = pl.multiple_of((2 * lax.rem(chip + shift, 4) + part) * width, width)
-            at = 3 * rows // 4 + 16 + part * width
-            moves.append(copy(held.at[:, pl.ds(place, width)], out.at[pl.ds(at, width), :], sems.at[2 + 2 * shift + part]))
+    loads = []
+    for head in range(2):
+        for slot, source in enumerate((q, k, v)):
+            loads.append(copy(source.at[:, pl.ds(head * HEAD_DIM, HEAD_DIM)], raw.at[head, slot], sems.at[1 + 3 * head + slot]))
+    column = copy(w, held, sems.at[7])
     row = lax.broadcasted_iota(jnp.int32, (block, block), 0)
     kept = lax.broadcasted_iota(jnp.int32, (block, block), 1) <= row
+    line = lax.broadcasted_iota(jnp.int32, (16, HEAD_DIM), 0)
+    moves = []
+    first_copy.wait()
     for head in range(2):
+        for moved in loads[3 * head : 3 * head + 3]:
+            moved.wait()
         for first in range(0, rows, block):
             last = first + block
-            query = raw[0, first:last, half(head)]
+            query = raw[head, 0, first:last, :]
             pieces = [(first, last)] + ([(0, first)] if first else [])
             scores = [
-                lax.dot_general(
-                    query, raw[1, low:high, half(head)], (((1,), (1,)), ((), ())), preferred_element_type=F32
-                )
+                lax.dot_general(query, raw[head, 1, low:high, :], (((1,), (1,)), ((), ())), preferred_element_type=F32)
                 for low, high in pieces
             ]
             scores[0] = jnp.where(kept, scores[0], NEG)
@@ -151,34 +147,74 @@
             for piece, (low, high) in zip(scores, pieces):
                 weights = jnp.exp2((piece - top) * SCALE2)
                 total = total + jnp.sum(weights, axis=-1, keepdims=True)
-                out = out + jnp.dot(weights.astype(BF16), raw[2, low:high, half(head)], preferred_element_type=F32)
-            out = out / total
-            wide[0, first:last, :] = out
-            wide[1, first:last, :] = jnp.broadcast_to(top * SCALE + jnp.log(total), out.shape)
-        part = rows // 4
+                out = out + jnp.dot(weights.astype(BF16), raw[head, 2, low:high, :], preferred_element_type=F32)
+            wide[head, 0, first:last, :] = out / total
+            wide[head, 1, first:last, :] = jnp.broadcast_to(top * SCALE + jnp.log(total), out.shape)
         for turn in range(3):
             where = rows_of(lax.rem(off[head, 0] + turn + 1, 4), rows, 4)
-            early[turn * part : (turn + 1) * part, half(head)] = wide[0, where, :].astype(BF16)
-        line = lax.broadcasted_iota(jnp.int32, (16, HEAD_DIM), 0)
+            early[turn * part : (turn + 1) * part, half(head)] = wide[head, 0, where, :].astype(BF16)
         marks = jnp.where(line == 0, off[head, 0], jnp.where(line == 1, off[head, 1], off[head, 2]))
         early[3 * part :, half(head)] = marks.astype(F32).astype(BF16)
         at = 0
         for level, step in enumerate(STEPS):
             count = rows // step
             where = rows_of(off[head, level], rows, step)
-            some[head, at : at + count, :] = wide[0, where, :]
-            some_logs[head, at : at + count, :] = wide[1, where, :]
+            some[head, at : at + count, :] = wide[head, 0, where, :]
+            some_logs[head, at : at + count, :] = wide[head, 1, where, :]
             at += count
-    for slot, out in enumerate((own, out1, out2, out3)):
-        moves.append(copy(early, out.at[pl.ds(0, 3 * rows // 4 + 16), :], sems.at[10 + slot]))
-    moves += [copy(some, mixed, sems.at[14]), copy(some_logs, logs, sems.at[15])]
+        lanes = pl.ds(head * HEAD_DIM, HEAD_DIM)
+        for slot, target in enumerate((own, out1, out2, out3)):
+            place = target.at[pl.ds(0, 3 * part + 16), lanes]
+            moves.append(copy(early.at[:, lanes], place, sems.at[8 + 4 * head + slot]))
+        moves.append(copy(some.at[head], mixed.at[head], sems.at[16 + 2 * head]))
+        moves.append(copy(some_logs.at[head], logs.at[head], sems.at[17 + 2 * head]))
+        if head == 0:
+            column.wait()
+            for shift, target in enumerate((out1, out2, out3), 1):
+                for side in range(2):
+                    place = pl.multiple_of((2 * lax.rem(chip + shift, 4) + side) * width, width)
+                    at = 3 * part + 16 + side * width
+                    sem = sems.at[18 + 2 * shift + side]
+                    moves.append(copy(held.at[:, pl.ds(place, width)], target.at[pl.ds(at, width), :], sem))
     for moved in moves:
         moved.wait()
 
 
-def near_kernel(own_q, near_in, mixed, logs, queries, near, some, some_logs, sems):
+def merge(parts):
+    top = parts[0][1]
+    for _, log in parts[1:]:
+        top = jnp.maximum(top, log)
+    total, out = 0.0, 0.0
+    for value, log in parts:
+        share = jnp.exp(log - top)
+        total = total + share
+        out = out + share * value
+    return out / total, top + jnp.log(total)
+
+
+def spread_rows(off, head, packed, wide):
+    rows, at = wide.shape[1], 0
+    for level, step in enumerate(STEPS):
+        count = rows // step
+        wide[head, rows_of(off[head, level], rows, step), :] = packed[head, at : at + count, :]
+        at += count
+
+
+def gather_rows(off, head, wide, packed):
+    rows, at = wide.shape[1], 0
+    for level, step in enumerate(STEPS):
+        count = rows // step
+        packed[head, at : at + count, :] = wide[head, rows_of(off[head, level], rows, step), :].astype(packed.dtype)
+        at += count
+
+
+def near_kernel(
+    off_in, own_q, near_in, m_in, l_in, m_out, l_out, off, queries, near, mixed, logs, run, run_logs, sems
+):
     count = own_q.shape[0]
-    loads = [copy(own_q, queries, sems.at[0]), copy(near_in.at[:, pl.ds(0, 2 * count), :], near, sems.at[3])]
+    rows = 4 * count
+    places = ((off_in, off), (own_q, queries), (near_in.at[:, pl.ds(0, 2 * count), :], near), (m_in, mixed), (l_in, logs))
+    loads = [copy(source, target, sems.at[slot]) for slot, (source, target) in enumerate(places)]
     for moved in loads:
         moved.wait()
     mine = lax.rem(lax.axis_index("seq"), 4)
@@ -189,18 +225,24 @@
         query = mine * count + lax.broadcasted_iota(jnp.int32, dims, 0)
         key = lax.broadcasted_iota(jnp.int32, dims, 1)
         out, log = attend(queries[:, half(head)], keys, values, key <= query)
-        some[head] = out
-        some_logs[head] = jnp.broadcast_to(log, out.shape)
-    moves = [copy(some, mixed, sems.at[1]), copy(some_logs, logs, sems.at[2])]
+        log = jnp.broadcast_to(log, out.shape)
+        out, log = merge([(mixed[head, :count, :], logs[head, :count, :]), (out, log)])
+        spread_rows(off, head, mixed, run)
+        spread_rows(off, head, logs, run_logs)
+        where = rows_of(off[head, 0], rows, 4)
+        run[head, where, :] = out
+        run_logs[head, where, :] = log
+        gather_rows(off, head, run, mixed)
+        gather_rows(off, head, run_logs, logs)
+    moves = [copy(mixed, m_out, sems.at[0]), copy(logs, l_out, sems.at[1])]
     for moved in moves:
         moved.wait()
 
 
-def far_kernel(near_in, z0, z1, z2, z3, far_z, back, near, zs, hi, part, sems):
+def far_kernel(near_in, z0, z1, z2, z3, hi, _, back, near, zs, part, sems):
     seq = lax.axis_index("seq")
     mine, line = lax.rem(seq, 4), lax.div(seq, 4)
     loads = [copy(z.at[pl.ds(0, 128), :], zs.at[shift], sems.at[2 + shift]) for shift, z in enumerate((z0, z1, z2, z3))]
-    loads.append(copy(far_z, hi, sems.at[6]))
     loads.append(copy(near_in.at[:, pl.ds(512, 80), :], near, sems.at[0]))
     for moved in loads:
         moved.wait()
@@ -224,9 +266,13 @@
             key = (source * 4 + mine) * count + lax.rem(key, count)
             out, log = attend(queries, keys, values, key <= query)
             logs.append(log)
-            part[:, at : at + count, half(head)] = out.reshape(4, count, HEAD_DIM)
+            part[:, at : at + count, half(head)] = out.reshape(4, count, HEAD_DIM).astype(BF16)
         lane = lax.broadcasted_iota(jnp.int32, (4 * count, HEAD_DIM), 1)
-        both = jnp.where(lane < HEAD_DIM // 2, logs[0], logs[1])
+        left = jnp.where(lane < HEAD_DIM // 2, logs[0], logs[1])
+        both = left.astype(BF16)
+        for piece in range(1, 3):
+            left = left - left.astype(BF16).astype(F32)
+            both = jnp.where(lax.rem(lane, HEAD_DIM // 2) < 16 * piece, both, left.astype(BF16))
         part[:, at : at + count, 2 * HEAD_DIM :] = both.reshape(4, count, HEAD_DIM)
         at += count
     moves = [copy(part, back, sems.at[1])]
@@ -234,49 +280,28 @@
         moved.wait()
 
 
-def merge(parts):
-    top = parts[0][1]
-    for _, log in parts[1:]:
-        top = jnp.maximum(top, log)
-    total, out = 0.0, 0.0
-    for value, log in parts:
-        share = jnp.exp(log - top)
-        total = total + share
-        out = out + share * value
-    return out / total, top + jnp.log(total)
-
-
-def merge_kernel(off_in, m_in, l_in, nm_in, nl_in, back_in, _1, _2, _3, late, off, mixed, logs, near_mixed, near_logs, back, run, run_logs, pack, sems):
+def merge_kernel(off_in, m_in, l_in, back, _1, _2, late, off, mixed, logs, run, run_logs, pack, sems):
     rows = run.shape[1]
-    places = ((off_in, off), (m_in, mixed), (l_in, logs), (nm_in, near_mixed), (nl_in, near_logs), (back_in, back))
+    places = ((off_in, off), (m_in, mixed), (l_in, logs))
     loads = [copy(source, target, sems.at[slot]) for slot, (source, target) in enumerate(places)]
     for moved in loads:
         moved.wait()
     for head in range(2):
+        spread_rows(off, head, mixed, run)
+        spread_rows(off, head, logs, run_logs)
         at = 0
-        for level, step in enumerate(STEPS):
-            count = rows // step
-            where = rows_of(off[head, level], rows, step)
-            run[head, where, :] = mixed[head, at : at + count, :]
-            run_logs[head, where, :] = logs[head, at : at + count, :]
+        for level in (1, 2):
+            count = rows // STEPS[level]
+            where = rows_of(off[head, level], rows, STEPS[level])
+            parts = [(run[head, where, :], run_logs[head, where, :])]
+            for source in range(4):
+                lane = head * (HEAD_DIM // 2)
+                pieces = back[source, at : at + count, 2 * HEAD_DIM :].astype(F32)
+                log = sum(pieces[:, lane + 16 * piece : lane + 16 * piece + 1] for piece in range(3))
+                value = back[source, at : at + count, half(head)].astype(F32)
+                parts.append((value, jnp.broadcast_to(log, (count, HEAD_DIM))))
             at += count
-        at = 0
-        for level, step in enumerate(STEPS):
-            count = rows // step
-            where = rows_of(off[head, level], rows, step)
-            if level == 0:
-                new = (near_mixed[head], near_logs[head])
-            else:
-                parts = []
-                for source in range(4):
-                    lane = 2 * HEAD_DIM + head * (HEAD_DIM // 2)
-                    log = back[source, at : at + count, lane : lane + 1]
-                    parts.append(
-                        (back[source, at : at + count, half(head)], jnp.broadcast_to(log, (count, HEAD_DIM)))
-                    )
-                new = merge(parts)
-                at += count
-            out, log = merge([(run[head, where, :], run_logs[head, where, :]), new])
+            out, log = merge(parts)
             run[head, where, :] = out
             run_logs[head, where, :] = log
         at = 0
@@ -284,7 +309,7 @@
             count = rows // step
             pack[at : at + count, half(head)] = run[head, rows_of(off[head, level], rows, step), :].astype(BF16)
             at += count
-    moves = [copy(pack, late.at[target], sems.at[6 + target]) for target in range(4)]
+    moves = [copy(pack, late.at[target], sems.at[target]) for target in range(4)]
     for moved in moves:
         moved.wait()
 
@@ -402,13 +427,13 @@
         (HBM,) * 6,
         [
             pltpu.SMEM((2, 3), jnp.int32),
-            pltpu.VMEM((3, rows, width), BF16),
-            pltpu.VMEM((2, rows, HEAD_DIM), F32),
+            pltpu.VMEM((2, 3, rows, HEAD_DIM), BF16),
+            pltpu.VMEM((2, 2, rows, HEAD_DIM), F32),
             pltpu.VMEM((most + 16, width), BF16),
             pltpu.VMEM((2, late_rows, HEAD_DIM), F32),
             pltpu.VMEM((2, late_rows, HEAD_DIM), F32),
             pltpu.VMEM(w_out.shape, BF16),
-            dma((17,)),
+            dma((26,)),
         ],
     )(offsets, queries, keys, values, w_out)
     far_z = call(
@@ -417,51 +442,50 @@
     far_z = swap(far_z, "seq", far_lines)
     packs = [shift_x(pack, by) for by, pack in enumerate(packs, 1)]
     marks = jnp.stack([part[most : most + 3, ::HEAD_DIM] for part in [early] + packs]).astype(jnp.int32)
-    near_mixed, near_logs = call(
+    mixed, logs = call(
         near_kernel,
-        (pltpu.HBM((2, count[0], HEAD_DIM), F32),) * 2,
-        [HBM, ANY],
+        (kept, kept),
+        [HBM] * 2 + [ANY] + [HBM] * 2,
         (HBM,) * 2,
         [
+            pltpu.SMEM((2, 3), jnp.int32),
             pltpu.VMEM((count[0], width), BF16),
             pltpu.VMEM((4, 2 * count[0], width), BF16),
-            pltpu.VMEM((2, count[0], HEAD_DIM), F32),
-            pltpu.VMEM((2, count[0], HEAD_DIM), F32),
-            dma((4,)),
+            pltpu.VMEM(mixed.shape, F32),
+            pltpu.VMEM(mixed.shape, F32),
+            pltpu.VMEM((2, rows, HEAD_DIM), F32),
+            pltpu.VMEM((2, rows, HEAD_DIM), F32),
+            dma((5,)),
         ],
-    )(stay(own_q), near)
+    )(offsets, stay(own_q), near, stay(mixed), stay(logs))
     back = call(
         far_kernel,
-        pltpu.HBM((4, count[1] + count[2], 3 * HEAD_DIM), F32),
-        [ANY] * 6,
+        pltpu.HBM((4, count[1] + count[2], 3 * HEAD_DIM), BF16),
+        [ANY] * 5 + [VMEM, HBM],
         HBM,
         [
             pltpu.VMEM((4, count[1] + count[2], width), BF16),
             pltpu.VMEM((4, 2 * count[1], width), BF16),
-            pltpu.VMEM((4, 4, 2 * count[2], width), BF16),
-            pltpu.VMEM((4, count[1] + count[2], 3 * HEAD_DIM), F32),
+            pltpu.VMEM((4, count[1] + count[2], 3 * HEAD_DIM), BF16),
             dma((7,)),
         ],
-    )(near, *zs, far_z)
+    )(near, *zs, far_z, stay(mixed))
     back = swap(back, "seq", along_y)
     late = call(
         merge_kernel,
         pltpu.HBM((4, late_rows, width), BF16),
-        [HBM] * 5 + [ANY] * 4,
+        [HBM] * 3 + [VMEM] + [ANY] * 2,
         HBM,
         [
             pltpu.SMEM((2, 3), jnp.int32),
             pltpu.VMEM(mixed.shape, F32),
             pltpu.VMEM(mixed.shape, F32),
-            pltpu.VMEM(near_mixed.shape, F32),
-            pltpu.VMEM(near_mixed.shape, F32),
-            pltpu.VMEM(back.shape, F32),
             pltpu.VMEM((2, rows, HEAD_DIM), F32),
             pltpu.VMEM((2, rows, HEAD_DIM), F32),
             pltpu.VMEM((late_rows, width), BF16),
-            dma((10,)),
+            dma((4,)),
         ],
-    )(offsets, *map(stay, (mixed, logs, near_mixed, near_logs)), back, *packs)
+    )(offsets, stay(mixed), stay(logs), back, packs[0], packs[2])
     late = swap(late, "head", along_x)
     send, keep = call(
         project_kernel,

time: 105 us -> 101 us (0.962)
  waiting for transfers between devices: 25.3 us -> 14 us
  starting transfers between devices: 52.6 us -> 60.1 us
    ppermute x3, waiting for transfers between devices: 12.4 us -> 0.01 us  [shift_x(): lax.ppermute(value, 'head', [(place, (place + 2 * by) % heads) for place...]
    ppermute x1, starting transfers between devices: 4.05 us -> 13.8 us  [shards(): lax.ppermute(send, 'head', [(place, place ^ 1) for place in range(heads)])]
    all_to_all x4, starting transfers between devices: 27.6 us -> 25.9 us  [swap(): return lax.all_to_all(value, axis, 0, 0, axis_index_groups=groups)]
    all_to_all x4, waiting for transfers between devices: 11.4 us -> 12.5 us  [swap(): return lax.all_to_all(value, axis, 0, 0, axis_index_groups=groups)]
  transfers between devices with their start and end apart: 11 -> 11, of which waited for: 5 -> 3; matrix products, arithmetic and copies ran while one was open for 1% -> 1% of each run, Pallas kernels for 12% -> 15%
where the time goes in v3:
time: 101 us; the launch traced here: 99.7 us
  starting transfers between devices  60.1 us (60%)
  Pallas kernels  23.7 us (23%)
  waiting for transfers between devices  14 us (14%)
  local copies, waits for them, and re-layouts  1.71 us (2%)
    all_to_all x4, starting transfers between devices, swap(): return lax.all_to_all(value, axis, 0, 0, axis_index_groups=groups)  25.9 us
    ppermute x1, starting transfers between devices, shards(): lax.ppermute(send, 'head', [(place, place ^ 1) for place in range(heads)])  13.8 us
    all_to_all x4, waiting for transfers between devices, swap(): return lax.all_to_all(value, axis, 0, 0, axis_index_groups=groups)  12.5 us
    ppermute x3, starting transfers between devices, shift_z(): return lax.ppermute(value, 'seq', hops)  10.4 us
    ppermute x3, starting transfers between devices, shift_x(): lax.ppermute(value, 'head', [(place, (place + 2 * by) % heads) for place...  9.98 us
    pallas_call x1, Pallas kernels, shards(): call(local_kernel, (pltpu.HBM((most + 16, width), BF16), packed, packed,...  6.05 us
    pallas_call x1, Pallas kernels, shards(): call(near_kernel, (kept, kept), [HBM] * 2 + [ANY] + [HBM] * 2, (HBM,) * 2...  3.87 us
    pallas_call x1, Pallas kernels, shards(): call(project_kernel, (shape((rows, width), BF16), shape((rows, width), F3...  3.27 us
  transfers between devices with their start and end apart: 11, of which 3 were waited for; matrix products, arithmetic and copies ran while one was open for 1% of the time, Pallas kernels for 15%

profile of v3, /device:TPU:1, one launch (start us, length us, event | category | flops | bytes accessed | tf_op | source)
XLA Modules:
  0.0 99.7 jit_solution(5341880338338238310)
XLA Ops:
  0.0 2.7 %shard_map.56 = (bf16[4,592,256]{2,1,0:T(8,128)(2,1)}, bf16[160,256]{1,0:T(8,128)(2,1)}, bf16[256,256]{1,0:T(8,128)(2,1)}) custom-call(s32[2,3]{1,0:T(2,128)} %off_in.7, bf16[1024,256]{1,0:T(8,128)(2,1)} %q.3, bf16[1024,256]{1,0:T(8,128)(2,1)} %k.3, bf16[1024,256]{1,0:T(8,128)(2,1)} %v.3), custom_call_target="tpu_custom_call" | custom-call | tf_op jit(solution)/shard_map/pallas_call | solution.py:403
  2.7 0.0 copy-start
  2.7 5.2 %all-to-all-start = ((bf16[4,592,256]{2,1,0:T(8,128)(2,1)}), bf16[4,592,256]{2,1,0:T(8,128)(2,1)S(1)}, u32[]{:S(2)}, u32[]{:S(2)}) async-start(bf16[4,592,256]{2,1,0:T(8,128)(2,1)} %get-tuple-element.23), calls=%async_computation | async-start | bytes 2424832 | tf_op jit(solution)/shard_map/all_to_all | solution.py:389
  7.9 0.0 copy-done
  7.9 6.2 %collective-permute-start.5 = (bf16[160,256]{1,0:T(8,128)(2,1)S(1)}, bf16[160,256]{1,0:T(8,128)(2,1)S(1)}, u32[]{:S(2)}, u32[]{:S(2)}) collective-permute-start(bf16[160,256]{1,0:T(8,128)(2,1)S(1)} %copy-done), channel_id=1, source_target_pairs={{0,96},{8,104},{16,112},{24,120},{32,0},{40,8},{48,16},{56,24},{64... | collective-permute-start | bytes 245768 | tf_op jit(solution)/shard_map/ppermute | solution.py:393
  14.1 1.9 %collective-permute-start.4 = (bf16[160,256]{1,0:T(8,128)(2,1)S(1)}, bf16[160,256]{1,0:T(8,128)(2,1)S(1)}, u32[]{:S(2)}, u32[]{:S(2)}) collective-permute-start(bf16[160,256]{1,0:T(8,128)(2,1)S(1)} %copy-done), channel_id=1, source_target_pairs={{0,64},{8,72},{16,80},{24,88},{32,96},{40,104},{48,112},{56,120},{... | collective-permute-start | bytes 245768 | tf_op jit(solution)/shard_map/ppermute | solution.py:393
  16.1 2.2 %collective-permute-start.3 = (bf16[160,256]{1,0:T(8,128)(2,1)S(1)}, bf16[160,256]{1,0:T(8,128)(2,1)S(1)}, u32[]{:S(2)}, u32[]{:S(2)}) collective-permute-start(bf16[160,256]{1,0:T(8,128)(2,1)S(1)} %copy-done), channel_id=1, source_target_pairs={{0,32},{8,40},{16,48},{24,56},{32,64},{40,72},{48,80},{56,88},{64,... | collective-permute-start | bytes 245768 | tf_op jit(solution)/shard_map/ppermute | solution.py:393
  18.3 6.0 %shard_map.55 = (bf16[784,256]{1,0:T(8,128)(2,1)}, bf16[1296,256]{1,0:T(8,128)(2,1)}, bf16[1296,256]{1,0:T(8,128)(2,1)}, bf16[1296,256]{1,0:T(8,128)(2,1)}, f32[...) custom-call(s32[2,3]{1,0:T(2,128)} %off_in.7, bf16[1024,256]{1,0:T(8,128)(2,1)} %q.3, bf16[1024,256]{1,0:T(8,128)(2,1)} %k.3, ...), custom_call_target="tpu_custom_call" | custom-call | tf_op jit(solution)/shard_map/pallas_call | solution.py:423
  24.3 0.0 collective-permute-done.5.z3
  24.3 0.0 copy-start.1
  24.3 0.0 collective-permute-done.4.z2
  24.3 0.0 copy-start.2
  24.3 0.0 collective-permute-done.3.z1
  24.4 0.0 copy-start.3
  24.4 0.0 all-to-all-done.near_in._2
  24.4 0.6 copy-done.1
  25.0 0.1 copy-done.2
  25.0 0.0 copy-done.3
  25.0 1.5 %shard_map.58 = bf16[4,4,32,256]{3,2,1,0:T(8,128)(2,1)} custom-call(bf16[160,256]{1,0:T(8,128)(2,1)} %get-tuple-element.28.z0, bf16[160,256]{1,0:T(8,128)(2,1)} %copy-done.3, bf16[160,256]{1,0:T(8,128)(2,1)} %copy-done.2, bf16[160,256]{1,0:T(8,128)(2,1)} %copy-done.1, bf16[784,256]{1,0:T(8,128)(2,1)} %get-tuple-element.18._1.own, ...), custom_call_target="tpu_custom_call" | custom-call | tf_op jit(solution)/shard_map/pallas_call | solution.py:439
  26.6 13.6 %all-to-all-start.1 = ((bf16[4,4,32,256]{3,2,1,0:T(8,128)(2,1)}), bf16[4,4,32,256]{3,2,1,0:T(8,128)(2,1)S(1)}, u32[]{:S(2)}, u32[]{:S(2)}) async-start(bf16[4,4,32,256]{3,2,1,0:T(8,128)(2,1)} %shard_map.58), calls=%async_computation.1 | async-start | bytes 524288 | tf_op jit(solution)/shard_map/all_to_all | solution.py:389
  40.2 3.1 %collective-permute-start = (bf16[1296,256]{1,0:T(8,128)(2,1)}, bf16[1296,256]{1,0:T(8,128)(2,1)S(1)}, u32[]{:S(2)}, u32[]{:S(2)}) collective-permute-start(bf16[1296,256]{1,0:T(8,128)(2,1)} %get-tuple-element.19), channel_id=1, source_target_pairs={{0,2},{1,3},{2,4},{3,5},{4,6},{5,7},{6,0},{7,1},{8,10},{9,11},{10,... | collective-permute-start | bytes 1990664 | tf_op jit(solution)/shard_map/ppermute | solution.py:396
  43.3 3.3 %collective-permute-start.2 = (bf16[1296,256]{1,0:T(8,128)(2,1)}, bf16[1296,256]{1,0:T(8,128)(2,1)S(1)}, u32[]{:S(2)}, u32[]{:S(2)}) collective-permute-start(bf16[1296,256]{1,0:T(8,128)(2,1)} %get-tuple-element.21), channel_id=1, source_target_pairs={{0,6},{1,7},{2,0},{3,1},{4,2},{5,3},{6,4},{7,5},{8,14},{9,15},{10,... | collective-permute-start | bytes 1990664 | tf_op jit(solution)/shard_map/ppermute | solution.py:396
  46.7 3.5 %collective-permute-start.1 = (bf16[1296,256]{1,0:T(8,128)(2,1)}, bf16[1296,256]{1,0:T(8,128)(2,1)S(1)}, u32[]{:S(2)}, u32[]{:S(2)}) collective-permute-start(bf16[1296,256]{1,0:T(8,128)(2,1)} %get-tuple-element.20), channel_id=1, source_target_pairs={{0,4},{1,5},{2,6},{3,7},{4,0},{5,1},{6,2},{7,3},{8,12},{9,13},{10,... | collective-permute-start | bytes 1990664 | tf_op jit(solution)/shard_map/ppermute | solution.py:396
  50.2 3.9 %shard_map.57 = (f32[2,336,128]{2,1,0:T(8,128)}, f32[2,336,128]{2,1,0:T(8,128)}) custom-call(s32[2,3]{1,0:T(2,128)} %off_in.7, bf16[256,256]{1,0:T(8,128)(2,1)} %get-tuple-element.22.own_q, bf16[4,592,256]{2,1,0:T(8,128)(2,1)S(1)} %all-to-all-done.near_in._2, f32[2,336,128]{2,1,0:T(8,128)} %get-tuple-element.24.m_in, f32[2,336,128]{2,1,0:T(8,128)} %get-tuple-element.25.l_in), custom_call_target="tpu_custom_call" | custom-call | tf_op jit(solution)/shard_map/pallas_call | solution.py:445
  54.1 0.0 all-to-all-done.1.hi
  54.1 2.5 %shard_map.59 = bf16[4,80,384]{2,1,0:T(8,128)(2,1)} custom-call(bf16[4,592,256]{2,1,0:T(8,128)(2,1)S(1)} %all-to-all-done.near_in._2, bf16[160,256]{1,0:T(8,128)(2,1)} %get-tuple-element.28.z0, bf16[160,256]{1,0:T(8,128)(2,1)} %copy-done.3, bf16[160,256]{1,0:T(8,128)(2,1)} %copy-done.2, bf16[160,256]{1,0:T(8,128)(2,1)} %copy-done.1, ...), custom_call_target="tpu_custom_call" | custom-call | tf_op jit(solution)/shard_map/pallas_call | solution.py:461
  56.6 3.4 %all-to-all-start.2 = ((bf16[4,80,384]{2,1,0:T(8,128)(2,1)}), bf16[4,80,384]{2,1,0:T(8,128)(2,1)S(1)}, u32[]{:S(2)}, u32[]{:S(2)}) async-start(bf16[4,80,384]{2,1,0:T(8,128)(2,1)} %shard_map.59), calls=%async_computation.2 | async-start | bytes 491520 | tf_op jit(solution)/shard_map/all_to_all | solution.py:389
  60.0 0.0 collective-permute-done._1.e1
  60.0 0.0 collective-permute-done.2._2.e3
  60.0 5.7 %all-to-all-done.2.back = bf16[4,80,384]{2,1,0:T(8,128)(2,1)S(1)} async-done(((bf16[4,80,384]{2,1,0:T(8,128)(2,1)}), bf16[4,80,384]{2,1,0:T(8,128)(2,1)S(1)}, u32[]{:S(2)}, u32[]{:S(2)}) %all-to-all-start.2) | async-done | bytes 245792 | tf_op jit(solution)/shard_map/all_to_all | solution.py:389
  65.8 2.8 %shard_map.60 = bf16[4,336,256]{2,1,0:T(8,128)(2,1)} custom-call(s32[2,3]{1,0:T(2,128)} %off_in.7, f32[2,336,128]{2,1,0:T(8,128)} %get-tuple-element.26._.m_in, f32[2,336,128]{2,1,0:T(8,128)} %get-tuple-element.27.l_in, bf16[4,80,384]{2,1,0:T(8,128)(2,1)S(1)} %all-to-all-done.2.back, bf16[1296,256]{1,0:T(8,128)(2,1)S(1)} %collective-permute-done._1.e1, ...), custom_call_target="tpu_custom_call" | custom-call | tf_op jit(solution)/shard_map/pallas_call | solution.py:474
  68.6 3.7 %all-to-all-start.3 = ((bf16[4,336,256]{2,1,0:T(8,128)(2,1)}), bf16[4,336,256]{2,1,0:T(8,128)(2,1)S(1)}, u32[]{:S(2)}, u32[]{:S(2)}) async-start(bf16[4,336,256]{2,1,0:T(8,128)(2,1)} %shard_map.60), calls=%async_computation.3 | async-start | bytes 1376256 | tf_op jit(solution)/shard_map/all_to_all | solution.py:389
  72.3 0.8 slice.12
  73.1 0.1 slice.13
  73.2 0.1 slice.15
  73.2 0.0 collective-permute-done.1.e2
  73.2 0.1 slice.14
  73.4 6.7 %all-to-all-done.3.late = bf16[4,336,256]{2,1,0:T(8,128)(2,1)S(1)} async-done(((bf16[4,336,256]{2,1,0:T(8,128)(2,1)}), bf16[4,336,256]{2,1,0:T(8,128)(2,1)S(1)}, u32[]{:S(2)}, u32[]{:S(2)}) %all-to-all-start.3) | async-done | bytes 688160 | tf_op jit(solution)/shard_map/all_to_all | solution.py:389
  80.1 3.3 %shard_map.61 = (bf16[1024,256]{1,0:T(8,128)(2,1)S(1)}, f32[1024,256]{1,0:T(8,128)S(1)}) custom-call(s32[4,3,2]{2,1,0:T(4,128)S(1)} %maximum_convert_fusion.marks, bf16[784,256]{1,0:T(8,128)(2,1)} %get-tuple-element.18._1.own, bf16[1296,256]{1,0:T(8,128)(2,1)S(1)} %collective-permute-done._1.e1, bf16[1296,256]{1,0:T(8,128)(2,1)S(1)} %collective-permute-done.1.e2, ...), custom_call_target="tpu_custom_call" | custom-call | tf_op jit(solution)/shard_map/pallas_call | solution.py:490
  83.4 13.8 %collective-permute-start.6 = (bf16[1024,256]{1,0:T(8,128)(2,1)S(1)}, bf16[1024,256]{1,0:T(8,128)(2,1)S(1)}, u32[]{:S(2)}, u32[]{:S(2)}) collective-permute-start(bf16[1024,256]{1,0:T(8,128)(2,1)S(1)} %get-tuple-element.30), channel_id=1, source_target_pairs={{0,1},{1,0},{2,3},{3,2},{4,5},{5,4},{6,7},{7,6},{8,9},{9,8},{10,11... | collective-permute-start | bytes 1572872 | tf_op jit(solution)/shard_map/ppermute | solution.py:503
  97.2 1.5 %collective-permute-done.6.other = bf16[1024,256]{1,0:T(8,128)(2,1)S(1)} collective-permute-done((bf16[1024,256]{1,0:T(8,128)(2,1)S(1)}, bf16[1024,256]{1,0:T(8,128)(2,1)S(1)}, u32[]{:S(2)}, u32[]{:S(2)}) %collective-permute-start.6) | collective-permute-done | bytes 524320 | tf_op jit(solution)/shard_map/ppermute | solution.py:503
  98.7 1.0 %shard_map.62 = bf16[1024,256]{1,0:T(8,128)(2,1)} custom-call(f32[1024,256]{1,0:T(8,128)S(1)} %get-tuple-element.29.keep, bf16[1024,256]{1,0:T(8,128)(2,1)S(1)} %collective-permute-done.6.other), custom_call_target="tpu_custom_call" | custom-call | tf_op jit(solution)/shard_map/pallas_call | solution.py:504
  (1 shorter events, 0.0 us)
Async XLA Ops:
  2.7 5.2 %copy-start = (bf16[160,256]{1,0:T(8,128)(2,1)S(1)}, bf16[160,256]{1,0:T(8,128)(2,1)}, u32[]{:S(2)}) copy-start(bf16[160,256]{1,0:T(8,128)(2,1)} %get-tuple-element.28.z0) | copy-start | bytes 245764
  2.7 21.7 %all-to-all-start = ((bf16[4,592,256]{2,1,0:T(8,128)(2,1)}), bf16[4,592,256]{2,1,0:T(8,128)(2,1)S(1)}, u32[]{:S(2)}, u32[]{:S(2)}) async-start(bf16[4,592,256]{2,1,0:T(8,128)(2,1)} %get-tuple-element.23), calls=%async_computation | async-start | bytes 2424832 | tf_op jit(solution)/shard_map/all_to_all | solution.py:389
  7.9 16.4 %collective-permute-start.5 = (bf16[160,256]{1,0:T(8,128)(2,1)S(1)}, bf16[160,256]{1,0:T(8,128)(2,1)S(1)}, u32[]{:S(2)}, u32[]{:S(2)}) collective-permute-start(bf16[160,256]{1,0:T(8,128)(2,1)S(1)} %copy-done), channel_id=1, source_target_pairs={{0,96},{8,104},{16,112},{24,120},{32,0},{40,8},{48,16},{56,24},{64... | collective-permute-start | bytes 245768 | tf_op jit(solution)/shard_map/ppermute | solution.py:393
  14.1 10.2 %collective-permute-start.4 = (bf16[160,256]{1,0:T(8,128)(2,1)S(1)}, bf16[160,256]{1,0:T(8,128)(2,1)S(1)}, u32[]{:S(2)}, u32[]{:S(2)}) collective-permute-start(bf16[160,256]{1,0:T(8,128)(2,1)S(1)} %copy-done), channel_id=1, source_target_pairs={{0,64},{8,72},{16,80},{24,88},{32,96},{40,104},{48,112},{56,120},{... | collective-permute-start | bytes 245768 | tf_op jit(solution)/shard_map/ppermute | solution.py:393
  16.1 8.3 %collective-permute-start.3 = (bf16[160,256]{1,0:T(8,128)(2,1)S(1)}, bf16[160,256]{1,0:T(8,128)(2,1)S(1)}, u32[]{:S(2)}, u32[]{:S(2)}) collective-permute-start(bf16[160,256]{1,0:T(8,128)(2,1)S(1)} %copy-done), channel_id=1, source_target_pairs={{0,32},{8,40},{16,48},{24,56},{32,64},{40,72},{48,80},{56,88},{64,... | collective-permute-start | bytes 245768 | tf_op jit(solution)/shard_map/ppermute | solution.py:393
  24.3 0.6 copy-start.1
  24.3 0.7 copy-start.2
  24.4 0.7 copy-start.3
  26.6 27.5 %all-to-all-start.1 = ((bf16[4,4,32,256]{3,2,1,0:T(8,128)(2,1)}), bf16[4,4,32,256]{3,2,1,0:T(8,128)(2,1)S(1)}, u32[]{:S(2)}, u32[]{:S(2)}) async-start(bf16[4,4,32,256]{3,2,1,0:T(8,128)(2,1)} %shard_map.58), calls=%async_computation.1 | async-start | bytes 524288 | tf_op jit(solution)/shard_map/all_to_all | solution.py:389
  40.2 19.8 %collective-permute-start = (bf16[1296,256]{1,0:T(8,128)(2,1)}, bf16[1296,256]{1,0:T(8,128)(2,1)S(1)}, u32[]{:S(2)}, u32[]{:S(2)}) collective-permute-start(bf16[1296,256]{1,0:T(8,128)(2,1)} %get-tuple-element.19), channel_id=1, source_target_pairs={{0,2},{1,3},{2,4},{3,5},{4,6},{5,7},{6,0},{7,1},{8,10},{9,11},{10,... | collective-permute-start | bytes 1990664 | tf_op jit(solution)/shard_map/ppermute | solution.py:396
  43.3 16.7 %collective-permute-start.2 = (bf16[1296,256]{1,0:T(8,128)(2,1)}, bf16[1296,256]{1,0:T(8,128)(2,1)S(1)}, u32[]{:S(2)}, u32[]{:S(2)}) collective-permute-start(bf16[1296,256]{1,0:T(8,128)(2,1)} %get-tuple-element.21), channel_id=1, source_target_pairs={{0,6},{1,7},{2,0},{3,1},{4,2},{5,3},{6,4},{7,5},{8,14},{9,15},{10,... | collective-permute-start | bytes 1990664 | tf_op jit(solution)/shard_map/ppermute | solution.py:396
  46.7 26.5 %collective-permute-start.1 = (bf16[1296,256]{1,0:T(8,128)(2,1)}, bf16[1296,256]{1,0:T(8,128)(2,1)S(1)}, u32[]{:S(2)}, u32[]{:S(2)}) collective-permute-start(bf16[1296,256]{1,0:T(8,128)(2,1)} %get-tuple-element.20), channel_id=1, source_target_pairs={{0,4},{1,5},{2,6},{3,7},{4,0},{5,1},{6,2},{7,3},{8,12},{9,13},{10,... | collective-permute-start | bytes 1990664 | tf_op jit(solution)/shard_map/ppermute | solution.py:396
  56.6 9.2 %all-to-all-start.2 = ((bf16[4,80,384]{2,1,0:T(8,128)(2,1)}), bf16[4,80,384]{2,1,0:T(8,128)(2,1)S(1)}, u32[]{:S(2)}, u32[]{:S(2)}) async-start(bf16[4,80,384]{2,1,0:T(8,128)(2,1)} %shard_map.59), calls=%async_computation.2 | async-start | bytes 491520 | tf_op jit(solution)/shard_map/all_to_all | solution.py:389
  68.6 11.5 %all-to-all-start.3 = ((bf16[4,336,256]{2,1,0:T(8,128)(2,1)}), bf16[4,336,256]{2,1,0:T(8,128)(2,1)S(1)}, u32[]{:S(2)}, u32[]{:S(2)}) async-start(bf16[4,336,256]{2,1,0:T(8,128)(2,1)} %shard_map.60), calls=%async_computation.3 | async-start | bytes 1376256 | tf_op jit(solution)/shard_map/all_to_all | solution.py:389
  83.4 15.3 %collective-permute-start.6 = (bf16[1024,256]{1,0:T(8,128)(2,1)S(1)}, bf16[1024,256]{1,0:T(8,128)(2,1)S(1)}, u32[]{:S(2)}, u32[]{:S(2)}) collective-permute-start(bf16[1024,256]{1,0:T(8,128)(2,1)S(1)} %get-tuple-element.30), channel_id=1, source_target_pairs={{0,1},{1,0},{2,3},{3,2},{4,5},{5,4},{6,7},{7,6},{8,9},{9,8},{10,11... | collective-permute-start | bytes 1572872 | tf_op jit(solution)/shard_map/ppermute | solution.py:503

commit v4 on v3

--- a/solution.py
+++ b/solution.py
@@ -280,7 +280,7 @@
         moved.wait()
 
 
-def merge_kernel(off_in, m_in, l_in, back, _1, _2, late, off, mixed, logs, run, run_logs, pack, sems):
+def merge_kernel(off_in, m_in, l_in, back, late, off, mixed, logs, run, run_logs, pack, sems):
     rows = run.shape[1]
     places = ((off_in, off), (m_in, mixed), (l_in, logs))
     loads = [copy(source, target, sems.at[slot]) for slot, (source, target) in enumerate(places)]
@@ -474,7 +474,7 @@
     late = call(
         merge_kernel,
         pltpu.HBM((4, late_rows, width), BF16),
-        [HBM] * 3 + [VMEM] + [ANY] * 2,
+        [HBM] * 3 + [VMEM] + [ANY] * 0,
         HBM,
         [
             pltpu.SMEM((2, 3), jnp.int32),
@@ -485,7 +485,7 @@
             pltpu.VMEM((late_rows, width), BF16),
             dma((4,)),
         ],
-    )(offsets, stay(mixed), stay(logs), back, packs[0], packs[2])
+    )(offsets, stay(mixed), stay(logs), back)
     late = swap(late, "head", along_x)
     send, keep = call(
         project_kernel,

time: 101 us -> 98.3 us (0.973)
  blocking collectives: 0 us -> 9.14 us
  waiting for transfers between devices: 14 us -> 8.24 us
  starting transfers between devices: 60.1 us -> 54.4 us
    all_to_all x0 -> x1, blocking collectives: none -> 9.14 us  [swap(): return lax.all_to_all(value, axis, 0, 0, axis_index_groups=groups)]
    all_to_all x4 -> x3, waiting for transfers between devices: 12.5 us -> 4.19 us  [swap(): return lax.all_to_all(value, axis, 0, 0, axis_index_groups=groups)]
    all_to_all x4 -> x3, starting transfers between devices: 25.9 us -> 22.3 us  [swap(): return lax.all_to_all(value, axis, 0, 0, axis_index_groups=groups)]
    ppermute x1, starting transfers between devices: 13.8 us -> 11.2 us  [shards(): lax.ppermute(send, 'head', [(place, place ^ 1) for place in range(heads)])]
    ppermute x3, waiting for transfers between devices: 0.01 us -> 2.53 us  [shift_x(): lax.ppermute(value, 'head', [(place, (place + 2 * by) % heads) for place...]
  transfers between devices with their start and end apart: 11 -> 10, of which waited for: 3 -> 3; matrix products, arithmetic and copies ran while one was open for 1% -> 1% of each run, Pallas kernels for 15% -> 16%
where the time goes in v4:
time: 98.3 us; the launch traced here: 97.5 us
  starting transfers between devices  54.4 us (55%)
  Pallas kernels  23.8 us (24%)
  blocking collectives  9.14 us (9%)
  waiting for transfers between devices  8.24 us (8%)
  local copies, waits for them, and re-layouts  1.7 us (2%)
    all_to_all x3, starting transfers between devices, swap(): return lax.all_to_all(value, axis, 0, 0, axis_index_groups=groups)  22.3 us
    ppermute x1, starting transfers between devices, shards(): lax.ppermute(send, 'head', [(place, place ^ 1) for place in range(heads)])  11.2 us
    ppermute x3, starting transfers between devices, shift_x(): lax.ppermute(value, 'head', [(place, (place + 2 * by) % heads) for place...  10.6 us
    ppermute x3, starting transfers between devices, shift_z(): return lax.ppermute(value, 'seq', hops)  10.4 us
    all_to_all x1, blocking collectives, swap(): return lax.all_to_all(value, axis, 0, 0, axis_index_groups=groups)  9.14 us
    pallas_call x1, Pallas kernels, shards(): call(local_kernel, (pltpu.HBM((most + 16, width), BF16), packed, packed,...  6.04 us
    all_to_all x3, waiting for transfers between devices, swap(): return lax.all_to_all(value, axis, 0, 0, axis_index_groups=groups)  4.19 us
    pallas_call x1, Pallas kernels, shards(): call(near_kernel, (kept, kept), [HBM] * 2 + [ANY] + [HBM] * 2, (HBM,) * 2...  3.89 us
  transfers between devices with their start and end apart: 10, of which 3 were waited for; matrix products, arithmetic and copies ran while one was open for 1% of the time, Pallas kernels for 16%

profile of v4, /device:TPU:1, one launch (start us, length us, event | category | flops | bytes accessed | tf_op | source)
XLA Modules:
  0.0 97.5 jit_solution(8459640788892059233)
XLA Ops:
  0.0 2.7 %shard_map.56 = (bf16[4,592,256]{2,1,0:T(8,128)(2,1)}, bf16[160,256]{1,0:T(8,128)(2,1)}, bf16[256,256]{1,0:T(8,128)(2,1)}) custom-call(s32[2,3]{1,0:T(2,128)} %off_in.7, bf16[1024,256]{1,0:T(8,128)(2,1)} %q.3, bf16[1024,256]{1,0:T(8,128)(2,1)} %k.3, bf16[1024,256]{1,0:T(8,128)(2,1)} %v.3), custom_call_target="tpu_custom_call" | custom-call | tf_op jit(solution)/shard_map/pallas_call | solution.py:403
  2.7 0.0 copy-start
  2.8 5.2 %all-to-all-start = ((bf16[4,592,256]{2,1,0:T(8,128)(2,1)}), bf16[4,592,256]{2,1,0:T(8,128)(2,1)S(1)}, u32[]{:S(2)}, u32[]{:S(2)}) async-start(bf16[4,592,256]{2,1,0:T(8,128)(2,1)} %get-tuple-element.23), calls=%async_computation | async-start | bytes 2424832 | tf_op jit(solution)/shard_map/all_to_all | solution.py:389
  7.9 0.0 copy-done
  7.9 6.2 %collective-permute-start.5 = (bf16[160,256]{1,0:T(8,128)(2,1)S(1)}, bf16[160,256]{1,0:T(8,128)(2,1)S(1)}, u32[]{:S(2)}, u32[]{:S(2)}) collective-permute-start(bf16[160,256]{1,0:T(8,128)(2,1)S(1)} %copy-done), channel_id=1, source_target_pairs={{0,96},{8,104},{16,112},{24,120},{32,0},{40,8},{48,16},{56,24},{64... | collective-permute-start | bytes 245768 | tf_op jit(solution)/shard_map/ppermute | solution.py:393
  14.2 1.9 %collective-permute-start.4 = (bf16[160,256]{1,0:T(8,128)(2,1)S(1)}, bf16[160,256]{1,0:T(8,128)(2,1)S(1)}, u32[]{:S(2)}, u32[]{:S(2)}) collective-permute-start(bf16[160,256]{1,0:T(8,128)(2,1)S(1)} %copy-done), channel_id=1, source_target_pairs={{0,64},{8,72},{16,80},{24,88},{32,96},{40,104},{48,112},{56,120},{... | collective-permute-start | bytes 245768 | tf_op jit(solution)/shard_map/ppermute | solution.py:393
  16.1 2.2 %collective-permute-start.3 = (bf16[160,256]{1,0:T(8,128)(2,1)S(1)}, bf16[160,256]{1,0:T(8,128)(2,1)S(1)}, u32[]{:S(2)}, u32[]{:S(2)}) collective-permute-start(bf16[160,256]{1,0:T(8,128)(2,1)S(1)} %copy-done), channel_id=1, source_target_pairs={{0,32},{8,40},{16,48},{24,56},{32,64},{40,72},{48,80},{56,88},{64,... | collective-permute-start | bytes 245768 | tf_op jit(solution)/shard_map/ppermute | solution.py:393
  18.3 6.0 %shard_map.55 = (bf16[784,256]{1,0:T(8,128)(2,1)}, bf16[1296,256]{1,0:T(8,128)(2,1)}, bf16[1296,256]{1,0:T(8,128)(2,1)}, bf16[1296,256]{1,0:T(8,128)(2,1)}, f32[...) custom-call(s32[2,3]{1,0:T(2,128)} %off_in.7, bf16[1024,256]{1,0:T(8,128)(2,1)} %q.3, bf16[1024,256]{1,0:T(8,128)(2,1)} %k.3, ...), custom_call_target="tpu_custom_call" | custom-call | tf_op jit(solution)/shard_map/pallas_call | solution.py:423
  24.3 0.0 collective-permute-done.5.z3
  24.4 0.0 copy-start.1
  24.4 0.0 collective-permute-done.4.z2
  24.4 0.0 copy-start.2
  24.4 0.0 collective-permute-done.3.z1
  24.4 0.0 copy-start.3
  24.4 0.0 all-to-all-done.near_in._2
  24.4 0.6 copy-done.1
  25.0 0.1 copy-done.2
  25.0 0.0 copy-done.3
  25.1 1.5 %shard_map.58 = bf16[4,4,32,256]{3,2,1,0:T(8,128)(2,1)} custom-call(bf16[160,256]{1,0:T(8,128)(2,1)} %get-tuple-element.28.z0, bf16[160,256]{1,0:T(8,128)(2,1)} %copy-done.3, bf16[160,256]{1,0:T(8,128)(2,1)} %copy-done.2, bf16[160,256]{1,0:T(8,128)(2,1)} %copy-done.1, bf16[784,256]{1,0:T(8,128)(2,1)} %get-tuple-element.18._1.own, ...), custom_call_target="tpu_custom_call" | custom-call | tf_op jit(solution)/shard_map/pallas_call | solution.py:439
  26.6 13.6 %all-to-all-start.1 = ((bf16[4,4,32,256]{3,2,1,0:T(8,128)(2,1)}), bf16[4,4,32,256]{3,2,1,0:T(8,128)(2,1)S(1)}, u32[]{:S(2)}, u32[]{:S(2)}) async-start(bf16[4,4,32,256]{3,2,1,0:T(8,128)(2,1)} %shard_map.58), calls=%async_computation.1 | async-start | bytes 524288 | tf_op jit(solution)/shard_map/all_to_all | solution.py:389
  40.2 3.1 %collective-permute-start = (bf16[1296,256]{1,0:T(8,128)(2,1)}, bf16[1296,256]{1,0:T(8,128)(2,1)S(1)}, u32[]{:S(2)}, u32[]{:S(2)}) collective-permute-start(bf16[1296,256]{1,0:T(8,128)(2,1)} %get-tuple-element.19), channel_id=1, source_target_pairs={{0,2},{1,3},{2,4},{3,5},{4,6},{5,7},{6,0},{7,1},{8,10},{9,11},{10,... | collective-permute-start | bytes 1990664 | tf_op jit(solution)/shard_map/ppermute | solution.py:396
  43.4 4.3 %collective-permute-start.1 = (bf16[1296,256]{1,0:T(8,128)(2,1)}, bf16[1296,256]{1,0:T(8,128)(2,1)S(1)}, u32[]{:S(2)}, u32[]{:S(2)}) collective-permute-start(bf16[1296,256]{1,0:T(8,128)(2,1)} %get-tuple-element.20), channel_id=1, source_target_pairs={{0,4},{1,5},{2,6},{3,7},{4,0},{5,1},{6,2},{7,3},{8,12},{9,13},{10,... | collective-permute-start | bytes 1990664 | tf_op jit(solution)/shard_map/ppermute | solution.py:396
  47.7 3.1 %collective-permute-start.2 = (bf16[1296,256]{1,0:T(8,128)(2,1)}, bf16[1296,256]{1,0:T(8,128)(2,1)S(1)}, u32[]{:S(2)}, u32[]{:S(2)}) collective-permute-start(bf16[1296,256]{1,0:T(8,128)(2,1)} %get-tuple-element.21), channel_id=1, source_target_pairs={{0,6},{1,7},{2,0},{3,1},{4,2},{5,3},{6,4},{7,5},{8,14},{9,15},{10,... | collective-permute-start | bytes 1990664 | tf_op jit(solution)/shard_map/ppermute | solution.py:396
  50.8 3.9 %shard_map.57 = (f32[2,336,128]{2,1,0:T(8,128)}, f32[2,336,128]{2,1,0:T(8,128)}) custom-call(s32[2,3]{1,0:T(2,128)} %off_in.7, bf16[256,256]{1,0:T(8,128)(2,1)} %get-tuple-element.22.own_q, bf16[4,592,256]{2,1,0:T(8,128)(2,1)S(1)} %all-to-all-done.near_in._2, f32[2,336,128]{2,1,0:T(8,128)} %get-tuple-element.24.m_in, f32[2,336,128]{2,1,0:T(8,128)} %get-tuple-element.25.l_in), custom_call_target="tpu_custom_call" | custom-call | tf_op jit(solution)/shard_map/pallas_call | solution.py:445
  54.7 0.0 all-to-all-done.1.hi
  54.7 2.5 %shard_map.59 = bf16[4,80,384]{2,1,0:T(8,128)(2,1)} custom-call(bf16[4,592,256]{2,1,0:T(8,128)(2,1)S(1)} %all-to-all-done.near_in._2, bf16[160,256]{1,0:T(8,128)(2,1)} %get-tuple-element.28.z0, bf16[160,256]{1,0:T(8,128)(2,1)} %copy-done.3, bf16[160,256]{1,0:T(8,128)(2,1)} %copy-done.2, bf16[160,256]{1,0:T(8,128)(2,1)} %copy-done.1, ...), custom_call_target="tpu_custom_call" | custom-call | tf_op jit(solution)/shard_map/pallas_call | solution.py:461
  57.2 9.1 %all_to_all.20.back = bf16[4,80,384]{2,1,0:T(8,128)(2,1)S(1)} all-to-all(bf16[4,80,384]{2,1,0:T(8,128)(2,1)} %shard_map.59), channel_id=1, replica_groups={{0,8,16,24},{32,40,48,56},{64,72,80,88},{96,104,112,120},{128,136,144,1..., dimensions={0} | all-to-all | bytes 491520 | tf_op jit(solution)/shard_map/all_to_all | solution.py:389
  66.4 2.8 %shard_map.60 = bf16[4,336,256]{2,1,0:T(8,128)(2,1)} custom-call(s32[2,3]{1,0:T(2,128)} %off_in.7, f32[2,336,128]{2,1,0:T(8,128)} %get-tuple-element.26._.m_in, f32[2,336,128]{2,1,0:T(8,128)} %get-tuple-element.27.l_in, bf16[4,80,384]{2,1,0:T(8,128)(2,1)S(1)} %all_to_all.20.back), custom_call_target="tpu_custom_call" | custom-call | tf_op jit(solution)/shard_map/pallas_call | solution.py:474
  69.2 3.5 %all-to-all-start.3 = ((bf16[4,336,256]{2,1,0:T(8,128)(2,1)}), bf16[4,336,256]{2,1,0:T(8,128)(2,1)S(1)}, u32[]{:S(2)}, u32[]{:S(2)}) async-start(bf16[4,336,256]{2,1,0:T(8,128)(2,1)} %shard_map.60), calls=%async_computation.3 | async-start | bytes 1376256 | tf_op jit(solution)/shard_map/all_to_all | solution.py:389
  72.7 0.8 slice.12
  73.5 0.0 collective-permute-done.e1
  73.5 0.1 slice.13
  73.6 0.0 collective-permute-done.1.e2
  73.6 0.1 slice.14
  73.7 2.5 %collective-permute-done.2.e3 = bf16[1296,256]{1,0:T(8,128)(2,1)S(1)} collective-permute-done((bf16[1296,256]{1,0:T(8,128)(2,1)}, bf16[1296,256]{1,0:T(8,128)(2,1)S(1)}, u32[]{:S(2)}, u32[]{:S(2)}) %collective-permute-start.2) | collective-permute-done | bytes 663584 | tf_op jit(solution)/shard_map/ppermute | solution.py:396
  76.2 0.1 slice.15
  76.3 4.2 %all-to-all-done.3.late = bf16[4,336,256]{2,1,0:T(8,128)(2,1)S(1)} async-done(((bf16[4,336,256]{2,1,0:T(8,128)(2,1)}), bf16[4,336,256]{2,1,0:T(8,128)(2,1)S(1)}, u32[]{:S(2)}, u32[]{:S(2)}) %all-to-all-start.3) | async-done | bytes 688160 | tf_op jit(solution)/shard_map/all_to_all | solution.py:389
  80.5 3.3 %shard_map.61 = (bf16[1024,256]{1,0:T(8,128)(2,1)S(1)}, f32[1024,256]{1,0:T(8,128)S(1)}) custom-call(s32[4,3,2]{2,1,0:T(4,128)S(1)} %maximum_convert_fusion.marks, bf16[784,256]{1,0:T(8,128)(2,1)} %get-tuple-element.18._1.own, bf16[1296,256]{1,0:T(8,128)(2,1)S(1)} %collective-permute-done.e1, bf16[1296,256]{1,0:T(8,128)(2,1)S(1)} %collective-permute-done.1.e2, ...), custom_call_target="tpu_custom_call" | custom-call | tf_op jit(solution)/shard_map/pallas_call | solution.py:490
  83.7 11.2 %collective-permute-start.6 = (bf16[1024,256]{1,0:T(8,128)(2,1)S(1)}, bf16[1024,256]{1,0:T(8,128)(2,1)S(1)}, u32[]{:S(2)}, u32[]{:S(2)}) collective-permute-start(bf16[1024,256]{1,0:T(8,128)(2,1)S(1)} %get-tuple-element.30), channel_id=1, source_target_pairs={{0,1},{1,0},{2,3},{3,2},{4,5},{5,4},{6,7},{7,6},{8,9},{9,8},{10,11... | collective-permute-start | bytes 1572872 | tf_op jit(solution)/shard_map/ppermute | solution.py:503
  94.9 1.5 %collective-permute-done.6.other = bf16[1024,256]{1,0:T(8,128)(2,1)S(1)} collective-permute-done((bf16[1024,256]{1,0:T(8,128)(2,1)S(1)}, bf16[1024,256]{1,0:T(8,128)(2,1)S(1)}, u32[]{:S(2)}, u32[]{:S(2)}) %collective-permute-start.6) | collective-permute-done | bytes 524320 | tf_op jit(solution)/shard_map/ppermute | solution.py:503
  96.4 1.0 %shard_map.62 = bf16[1024,256]{1,0:T(8,128)(2,1)} custom-call(f32[1024,256]{1,0:T(8,128)S(1)} %get-tuple-element.29.keep, bf16[1024,256]{1,0:T(8,128)(2,1)S(1)} %collective-permute-done.6.other), custom_call_target="tpu_custom_call" | custom-call | tf_op jit(solution)/shard_map/pallas_call | solution.py:504
  (1 shorter events, 0.0 us)
Async XLA Ops:
  2.7 5.2 %copy-start = (bf16[160,256]{1,0:T(8,128)(2,1)S(1)}, bf16[160,256]{1,0:T(8,128)(2,1)}, u32[]{:S(2)}) copy-start(bf16[160,256]{1,0:T(8,128)(2,1)} %get-tuple-element.28.z0) | copy-start | bytes 245764
  2.8 21.7 %all-to-all-start = ((bf16[4,592,256]{2,1,0:T(8,128)(2,1)}), bf16[4,592,256]{2,1,0:T(8,128)(2,1)S(1)}, u32[]{:S(2)}, u32[]{:S(2)}) async-start(bf16[4,592,256]{2,1,0:T(8,128)(2,1)} %get-tuple-element.23), calls=%async_computation | async-start | bytes 2424832 | tf_op jit(solution)/shard_map/all_to_all | solution.py:389
  7.9 16.4 %collective-permute-start.5 = (bf16[160,256]{1,0:T(8,128)(2,1)S(1)}, bf16[160,256]{1,0:T(8,128)(2,1)S(1)}, u32[]{:S(2)}, u32[]{:S(2)}) collective-permute-start(bf16[160,256]{1,0:T(8,128)(2,1)S(1)} %copy-done), channel_id=1, source_target_pairs={{0,96},{8,104},{16,112},{24,120},{32,0},{40,8},{48,16},{56,24},{64... | collective-permute-start | bytes 245768 | tf_op jit(solution)/shard_map/ppermute | solution.py:393
  14.2 10.2 %collective-permute-start.4 = (bf16[160,256]{1,0:T(8,128)(2,1)S(1)}, bf16[160,256]{1,0:T(8,128)(2,1)S(1)}, u32[]{:S(2)}, u32[]{:S(2)}) collective-permute-start(bf16[160,256]{1,0:T(8,128)(2,1)S(1)} %copy-done), channel_id=1, source_target_pairs={{0,64},{8,72},{16,80},{24,88},{32,96},{40,104},{48,112},{56,120},{... | collective-permute-start | bytes 245768 | tf_op jit(solution)/shard_map/ppermute | solution.py:393
  16.1 8.3 %collective-permute-start.3 = (bf16[160,256]{1,0:T(8,128)(2,1)S(1)}, bf16[160,256]{1,0:T(8,128)(2,1)S(1)}, u32[]{:S(2)}, u32[]{:S(2)}) collective-permute-start(bf16[160,256]{1,0:T(8,128)(2,1)S(1)} %copy-done), channel_id=1, source_target_pairs={{0,32},{8,40},{16,48},{24,56},{32,64},{40,72},{48,80},{56,88},{64,... | collective-permute-start | bytes 245768 | tf_op jit(solution)/shard_map/ppermute | solution.py:393
  24.4 0.6 copy-start.1
  24.4 0.7 copy-start.2
  24.4 0.7 copy-start.3
  26.6 28.1 %all-to-all-start.1 = ((bf16[4,4,32,256]{3,2,1,0:T(8,128)(2,1)}), bf16[4,4,32,256]{3,2,1,0:T(8,128)(2,1)S(1)}, u32[]{:S(2)}, u32[]{:S(2)}) async-start(bf16[4,4,32,256]{3,2,1,0:T(8,128)(2,1)} %shard_map.58), calls=%async_computation.1 | async-start | bytes 524288 | tf_op jit(solution)/shard_map/all_to_all | solution.py:389
  40.2 33.2 %collective-permute-start = (bf16[1296,256]{1,0:T(8,128)(2,1)}, bf16[1296,256]{1,0:T(8,128)(2,1)S(1)}, u32[]{:S(2)}, u32[]{:S(2)}) collective-permute-start(bf16[1296,256]{1,0:T(8,128)(2,1)} %get-tuple-element.19), channel_id=1, source_target_pairs={{0,2},{1,3},{2,4},{3,5},{4,6},{5,7},{6,0},{7,1},{8,10},{9,11},{10,... | collective-permute-start | bytes 1990664 | tf_op jit(solution)/shard_map/ppermute | solution.py:396
  43.4 30.2 %collective-permute-start.1 = (bf16[1296,256]{1,0:T(8,128)(2,1)}, bf16[1296,256]{1,0:T(8,128)(2,1)S(1)}, u32[]{:S(2)}, u32[]{:S(2)}) collective-permute-start(bf16[1296,256]{1,0:T(8,128)(2,1)} %get-tuple-element.20), channel_id=1, source_target_pairs={{0,4},{1,5},{2,6},{3,7},{4,0},{5,1},{6,2},{7,3},{8,12},{9,13},{10,... | collective-permute-start | bytes 1990664 | tf_op jit(solution)/shard_map/ppermute | solution.py:396
  47.7 28.4 %collective-permute-start.2 = (bf16[1296,256]{1,0:T(8,128)(2,1)}, bf16[1296,256]{1,0:T(8,128)(2,1)S(1)}, u32[]{:S(2)}, u32[]{:S(2)}) collective-permute-start(bf16[1296,256]{1,0:T(8,128)(2,1)} %get-tuple-element.21), channel_id=1, source_target_pairs={{0,6},{1,7},{2,0},{3,1},{4,2},{5,3},{6,4},{7,5},{8,14},{9,15},{10,... | collective-permute-start | bytes 1990664 | tf_op jit(solution)/shard_map/ppermute | solution.py:396
  69.2 11.3 %all-to-all-start.3 = ((bf16[4,336,256]{2,1,0:T(8,128)(2,1)}), bf16[4,336,256]{2,1,0:T(8,128)(2,1)S(1)}, u32[]{:S(2)}, u32[]{:S(2)}) async-start(bf16[4,336,256]{2,1,0:T(8,128)(2,1)} %shard_map.60), calls=%async_computation.3 | async-start | bytes 1376256 | tf_op jit(solution)/shard_map/all_to_all | solution.py:389
  83.7 12.7 %collective-permute-start.6 = (bf16[1024,256]{1,0:T(8,128)(2,1)S(1)}, bf16[1024,256]{1,0:T(8,128)(2,1)S(1)}, u32[]{:S(2)}, u32[]{:S(2)}) collective-permute-start(bf16[1024,256]{1,0:T(8,128)(2,1)S(1)} %get-tuple-element.30), channel_id=1, source_target_pairs={{0,1},{1,0},{2,3},{3,2},{4,5},{5,4},{6,7},{7,6},{8,9},{9,8},{10,11... | collective-permute-start | bytes 1572872 | tf_op jit(solution)/shard_map/ppermute | solution.py:503

commit v5 on v4

--- a/solution.py
+++ b/solution.py
@@ -99,15 +99,14 @@
         moved.wait()
 
 
-def relay_kernel(z0, z1, z2, z3, _1, _2, far_z, part, sems):
+def relay_kernel(z0, z1, z2, z3, _1, _2, far_z, middle, part, sems):
     line = lax.rem(lax.div(lax.axis_index("seq"), 4), 4)
-    loads = [
-        copy(z.at[pl.ds(128, 32), :], part.at[lax.rem(line + 4 - shift, 4)], sems.at[shift])
-        for shift, z in enumerate((z0, z1, z2, z3))
-    ]
-    for moved in loads:
-        moved.wait()
-    moves = [copy(part, far_z.at[target], sems.at[4 + target]) for target in range(far_z.shape[0])]
+    moves = []
+    for shift, z in enumerate((z0, z1, z2, z3)):
+        place = lax.rem(line + 4 - shift, 4)
+        part[place] = z[128:160, :]
+        moves.append(copy(z.at[pl.ds(0, 128), :], middle.at[place], sems.at[shift]))
+    moves += [copy(part, far_z.at[target], sems.at[4 + target]) for target in range(far_z.shape[0])]
     for moved in moves:
         moved.wait()
 
@@ -239,10 +238,10 @@
         moved.wait()
 
 
-def far_kernel(near_in, z0, z1, z2, z3, hi, _, back, near, zs, part, sems):
+def far_kernel(near_in, middle, hi, _, back, near, zs, part, sems):
     seq = lax.axis_index("seq")
     mine, line = lax.rem(seq, 4), lax.div(seq, 4)
-    loads = [copy(z.at[pl.ds(0, 128), :], zs.at[shift], sems.at[2 + shift]) for shift, z in enumerate((z0, z1, z2, z3))]
+    loads = [copy(middle, zs, sems.at[2])]
     loads.append(copy(near_in.at[:, pl.ds(512, 80), :], near, sems.at[0]))
     for moved in loads:
         moved.wait()
@@ -262,8 +261,7 @@
             row = lax.broadcasted_iota(jnp.int32, dims, 0)
             query = place * 4 * count + row
             key = lax.broadcasted_iota(jnp.int32, dims, 1)
-            source = lax.rem(place + 4 - lax.div(key, count), 4) if level == 1 else lax.div(key, count)
-            key = (source * 4 + mine) * count + lax.rem(key, count)
+            key = (lax.div(key, count) * 4 + mine) * count + lax.rem(key, count)
             out, log = attend(queries, keys, values, key <= query)
             logs.append(log)
             part[:, at : at + count, half(head)] = out.reshape(4, count, HEAD_DIM).astype(BF16)
@@ -314,8 +312,8 @@
         moved.wait()
 
 
-def project_kernel(marks, own, e1, e2, e3, late, w, send, keep, e0, wide, whole, weight, sems):
-    rows, width = keep.shape
+def project_kernel(marks, own, e1, e2, e3, late, w, send, whole, e0, wide, weight, sems):
+    rows, width = send.shape
     part = rows // 4
     most = 3 * part
     place = lax.axis_index("head")
@@ -351,20 +349,26 @@
                 whole[pl.ds(block, part), half(slot)] = wide[held].astype(BF16)
                 at += count
 
-    def product(which):
-        total = 0.0
-        for shift, pack in enumerate((None, e1, e2, e3)):
-            if shift:
-                chosen = pack[pl.ds(pl.multiple_of(most + 16 + which * width, 16), width), :]
-            else:
-                chosen = weight[:, pl.ds(pl.multiple_of(which * width, width), width)]
-            total = total + jnp.dot(
-                whole[:, shift * width : (shift + 1) * width], chosen, preferred_element_type=F32
-            )
-        return total
-
-    send[...] = product(1 - core).astype(BF16)
-    keep[...] = product(core)
+    send[...] = product(whole, (e1, e2, e3), weight, 1 - core).astype(BF16)
+
+
+def product(whole, packs, weight, which):
+    rows, width = whole.shape[0], weight.shape[0]
+    first = weight[:, pl.ds(pl.multiple_of(which * width, width), width)]
+    total = jnp.dot(whole[:, :width], first, preferred_element_type=F32)
+    for shift, pack in enumerate(packs, 1):
+        chosen = pack[pl.ds(pl.multiple_of(3 * rows // 4 + 16 + which * width, 16), width), :]
+        total = total + jnp.dot(whole[:, shift * width : (shift + 1) * width], chosen, preferred_element_type=F32)
+    return total
+
+
+def keep_kernel(whole, e1, e2, e3, w, keep, weight, sem):
+    place = lax.axis_index("head")
+    chip, core = lax.div(place, 2), lax.rem(place, 2)
+    width = weight.shape[0]
+    column = pl.multiple_of(2 * chip * width, width)
+    copy(w.at[:, pl.ds(column, 2 * width)], weight, sem).wait()
+    keep[...] = product(whole, (e1, e2, e3), weight, core)
 
 
 def finish_kernel(keep, other, out, wide):
@@ -415,7 +419,7 @@
             dma((13,)),
         ],
     )(offsets, queries, keys, values)
-    zs = [stay(part) for part in [near_z] + [shift_z(near_z, by) for by in (1, 2, 3)]]
+    zs = [near_z] + [shift_z(near_z, by) for by in (1, 2, 3)]
     near = swap(near, "seq", along_y)
     most = 3 * rows // 4
     packed = pltpu.HBM((most + 16 + 2 * width, width), BF16)
@@ -436,8 +440,12 @@
             dma((26,)),
         ],
     )(offsets, queries, keys, values, w_out)
-    far_z = call(
-        relay_kernel, pltpu.HBM((4, 4, 2 * count[2], width), BF16), [ANY] * 4 + [HBM, ANY], HBM, [pltpu.VMEM((4, 2 * count[2], width), BF16), dma((8,))]
+    far_z, middle = call(
+        relay_kernel,
+        (pltpu.HBM((4, 4, 2 * count[2], width), BF16), pltpu.HBM((4, 2 * count[1], width), BF16)),
+        [VMEM] * 4 + [HBM, ANY],
+        (HBM,) * 2,
+        [pltpu.VMEM((4, 2 * count[2], width), BF16), dma((8,))],
     )(*zs, stay(early), near)
     far_z = swap(far_z, "seq", far_lines)
     packs = [shift_x(pack, by) for by, pack in enumerate(packs, 1)]
@@ -461,7 +469,7 @@
     back = call(
         far_kernel,
         pltpu.HBM((4, count[1] + count[2], 3 * HEAD_DIM), BF16),
-        [ANY] * 5 + [VMEM, HBM],
+        [ANY, HBM, VMEM, HBM],
         HBM,
         [
             pltpu.VMEM((4, count[1] + count[2], width), BF16),
@@ -469,7 +477,7 @@
             pltpu.VMEM((4, count[1] + count[2], 3 * HEAD_DIM), BF16),
             dma((7,)),
         ],
-    )(near, *zs, far_z, stay(mixed))
+    )(near, stay(middle), far_z, stay(mixed))
     back = swap(back, "seq", along_y)
     late = call(
         merge_kernel,
@@ -487,19 +495,25 @@
         ],
     )(offsets, stay(mixed), stay(logs), back)
     late = swap(late, "head", along_x)
-    send, keep = call(
+    send, whole = call(
         project_kernel,
-        (shape((rows, width), BF16), shape((rows, width), F32)),
+        (shape((rows, width), BF16), shape((rows, 4 * width), BF16)),
         [SMEM, HBM] + [VMEM] * 4 + [HBM],
         (VMEM,) * 2,
         [
             pltpu.VMEM((most, width), BF16),
             pltpu.VMEM((16, count[0], HEAD_DIM), F32),
-            pltpu.VMEM((rows, 4 * width), BF16),
             pltpu.VMEM((width, 2 * width), BF16),
             dma((2,)),
         ],
     )(marks, stay(early), *packs, late, w_out)
+    keep = call(
+        keep_kernel,
+        shape((rows, width), F32),
+        [VMEM] * 4 + [HBM],
+        VMEM,
+        [pltpu.VMEM((width, 2 * width), BF16), dma(())],
+    )(whole, *packs, w_out)
     other = lax.ppermute(send, "head", [(place, place ^ 1) for place in range(heads)])
     return call(
         finish_kernel,

time: 98.3 us -> 96.6 us (0.983)
  waiting for transfers between devices: 8.24 us -> 6.73 us
    ppermute x1, waiting for transfers between devices: 1.51 us -> 0.01 us  [shards(): lax.ppermute(send, 'head', [(place, place ^ 1) for place in range(heads)])]
    pallas_call x2 -> x3, Pallas kernels: 4.8 us -> 5.31 us  [the longest x1 2.73 us: shards(): call(project_kernel, (shape((rows, width), BF16), shape((rows, 4 * width)...]
  transfers between devices with their start and end apart: 10 -> 10, of which waited for: 3 -> 2; matrix products, arithmetic and copies ran while one was open for 1% -> 1% of each run, Pallas kernels for 16% -> 18%
where the time goes in v5:
time: 96.6 us; the launch traced here: 95.7 us
  starting transfers between devices  54.5 us (56%)
  Pallas kernels  24.2 us (25%)
  blocking collectives  9.11 us (9%)
  waiting for transfers between devices  6.73 us (7%)
  local copies, waits for them, and re-layouts  1.05 us (1%)
    all_to_all x3, starting transfers between devices, swap(): return lax.all_to_all(value, axis, 0, 0, axis_index_groups=groups)  23 us
    ppermute x1, starting transfers between devices, shards(): lax.ppermute(send, 'head', [(place, place ^ 1) for place in range(heads)])  10.6 us
    ppermute x3, starting transfers between devices, shift_x(): lax.ppermute(value, 'head', [(place, (place + 2 * by) % heads) for place...  10.5 us
    ppermute x3, starting transfers between devices, shift_z(): return lax.ppermute(value, 'seq', hops)  10.4 us
    all_to_all x1, blocking collectives, swap(): return lax.all_to_all(value, axis, 0, 0, axis_index_groups=groups)  9.11 us
    pallas_call x1, Pallas kernels, shards(): call(local_kernel, (pltpu.HBM((most + 16, width), BF16), packed, packed,...  6.04 us
    all_to_all x3, waiting for transfers between devices, swap(): return lax.all_to_all(value, axis, 0, 0, axis_index_groups=groups)  4.07 us
    pallas_call x1, Pallas kernels, shards(): call(near_kernel, (kept, kept), [HBM] * 2 + [ANY] + [HBM] * 2, (HBM,) * 2...  3.88 us
  transfers between devices with their start and end apart: 10, of which 2 were waited for; matrix products, arithmetic and copies ran while one was open for 1% of the time, Pallas kernels for 18%

profile of v5, /device:TPU:1, one launch (start us, length us, event | category | flops | bytes accessed | tf_op | source)
XLA Modules:
  0.0 95.7 jit_solution(17786227111107306471)
XLA Ops:
  0.0 2.7 %shard_map.56 = (bf16[4,592,256]{2,1,0:T(8,128)(2,1)}, bf16[160,256]{1,0:T(8,128)(2,1)}, bf16[256,256]{1,0:T(8,128)(2,1)}) custom-call(s32[2,3]{1,0:T(2,128)} %off_in.7, bf16[1024,256]{1,0:T(8,128)(2,1)} %q.3, bf16[1024,256]{1,0:T(8,128)(2,1)} %k.3, bf16[1024,256]{1,0:T(8,128)(2,1)} %v.3), custom_call_target="tpu_custom_call" | custom-call | tf_op jit(solution)/shard_map/pallas_call | solution.py:407
  2.7 0.0 copy-start
  2.7 5.2 %all-to-all-start = ((bf16[4,592,256]{2,1,0:T(8,128)(2,1)}), bf16[4,592,256]{2,1,0:T(8,128)(2,1)S(1)}, u32[]{:S(2)}, u32[]{:S(2)}) async-start(bf16[4,592,256]{2,1,0:T(8,128)(2,1)} %get-tuple-element.25), calls=%async_computation | async-start | bytes 2424832 | tf_op jit(solution)/shard_map/all_to_all | solution.py:393
  7.9 0.0 copy-done
  7.9 6.2 %collective-permute-start.5 = (bf16[160,256]{1,0:T(8,128)(2,1)S(1)}, bf16[160,256]{1,0:T(8,128)(2,1)S(1)}, u32[]{:S(2)}, u32[]{:S(2)}) collective-permute-start(bf16[160,256]{1,0:T(8,128)(2,1)S(1)} %copy-done), channel_id=1, source_target_pairs={{0,96},{8,104},{16,112},{24,120},{32,0},{40,8},{48,16},{56,24},{64... | collective-permute-start | bytes 245768 | tf_op jit(solution)/shard_map/ppermute | solution.py:397
  14.1 1.9 %collective-permute-start.4 = (bf16[160,256]{1,0:T(8,128)(2,1)S(1)}, bf16[160,256]{1,0:T(8,128)(2,1)S(1)}, u32[]{:S(2)}, u32[]{:S(2)}) collective-permute-start(bf16[160,256]{1,0:T(8,128)(2,1)S(1)} %copy-done), channel_id=1, source_target_pairs={{0,64},{8,72},{16,80},{24,88},{32,96},{40,104},{48,112},{56,120},{... | collective-permute-start | bytes 245768 | tf_op jit(solution)/shard_map/ppermute | solution.py:397
  16.1 2.2 %collective-permute-start.3 = (bf16[160,256]{1,0:T(8,128)(2,1)S(1)}, bf16[160,256]{1,0:T(8,128)(2,1)S(1)}, u32[]{:S(2)}, u32[]{:S(2)}) collective-permute-start(bf16[160,256]{1,0:T(8,128)(2,1)S(1)} %copy-done), channel_id=1, source_target_pairs={{0,32},{8,40},{16,48},{24,56},{32,64},{40,72},{48,80},{56,88},{64,... | collective-permute-start | bytes 245768 | tf_op jit(solution)/shard_map/ppermute | solution.py:397
  18.3 6.0 %shard_map.55 = (bf16[784,256]{1,0:T(8,128)(2,1)}, bf16[1296,256]{1,0:T(8,128)(2,1)}, bf16[1296,256]{1,0:T(8,128)(2,1)}, bf16[1296,256]{1,0:T(8,128)(2,1)}, f32[...) custom-call(s32[2,3]{1,0:T(2,128)} %off_in.7, bf16[1024,256]{1,0:T(8,128)(2,1)} %q.3, bf16[1024,256]{1,0:T(8,128)(2,1)} %k.3, ...), custom_call_target="tpu_custom_call" | custom-call | tf_op jit(solution)/shard_map/pallas_call | solution.py:427
  24.3 0.0 collective-permute-done.5.z3
  24.3 0.0 collective-permute-done.4.z2
  24.3 0.0 collective-permute-done.3.z1
  24.3 0.0 all-to-all-done.near_in._2
  24.3 0.9 shard_map.58
  25.2 14.3 %all-to-all-start.1 = ((bf16[4,4,32,256]{3,2,1,0:T(8,128)(2,1)}), bf16[4,4,32,256]{3,2,1,0:T(8,128)(2,1)S(1)}, u32[]{:S(2)}, u32[]{:S(2)}) async-start(bf16[4,4,32,256]{3,2,1,0:T(8,128)(2,1)} %get-tuple-element.32), calls=%async_computation.1 | async-start | bytes 524288 | tf_op jit(solution)/shard_map/all_to_all | solution.py:393
  39.5 3.1 %collective-permute-start = (bf16[1296,256]{1,0:T(8,128)(2,1)}, bf16[1296,256]{1,0:T(8,128)(2,1)S(1)}, u32[]{:S(2)}, u32[]{:S(2)}) collective-permute-start(bf16[1296,256]{1,0:T(8,128)(2,1)} %get-tuple-element.21), channel_id=1, source_target_pairs={{0,2},{1,3},{2,4},{3,5},{4,6},{5,7},{6,0},{7,1},{8,10},{9,11},{10,... | collective-permute-start | bytes 1990664 | tf_op jit(solution)/shard_map/ppermute | solution.py:400
  42.6 4.4 %collective-permute-start.1 = (bf16[1296,256]{1,0:T(8,128)(2,1)}, bf16[1296,256]{1,0:T(8,128)(2,1)S(1)}, u32[]{:S(2)}, u32[]{:S(2)}) collective-permute-start(bf16[1296,256]{1,0:T(8,128)(2,1)} %get-tuple-element.22), channel_id=1, source_target_pairs={{0,4},{1,5},{2,6},{3,7},{4,0},{5,1},{6,2},{7,3},{8,12},{9,13},{10,... | collective-permute-start | bytes 1990664 | tf_op jit(solution)/shard_map/ppermute | solution.py:400
  47.0 3.1 %collective-permute-start.2 = (bf16[1296,256]{1,0:T(8,128)(2,1)}, bf16[1296,256]{1,0:T(8,128)(2,1)S(1)}, u32[]{:S(2)}, u32[]{:S(2)}) collective-permute-start(bf16[1296,256]{1,0:T(8,128)(2,1)} %get-tuple-element.23), channel_id=1, source_target_pairs={{0,6},{1,7},{2,0},{3,1},{4,2},{5,3},{6,4},{7,5},{8,14},{9,15},{10,... | collective-permute-start | bytes 1990664 | tf_op jit(solution)/shard_map/ppermute | solution.py:400
  50.1 3.9 %shard_map.57 = (f32[2,336,128]{2,1,0:T(8,128)}, f32[2,336,128]{2,1,0:T(8,128)}) custom-call(s32[2,3]{1,0:T(2,128)} %off_in.7, bf16[256,256]{1,0:T(8,128)(2,1)} %get-tuple-element.24.own_q, bf16[4,592,256]{2,1,0:T(8,128)(2,1)S(1)} %all-to-all-done.near_in._2, f32[2,336,128]{2,1,0:T(8,128)} %get-tuple-element.26.m_in, f32[2,336,128]{2,1,0:T(8,128)} %get-tuple-element.27.l_in), custom_call_target="tpu_custom_call" | custom-call | tf_op jit(solution)/shard_map/pallas_call | solution.py:453
  54.0 0.0 all-to-all-done.1.hi
  54.0 2.5 %shard_map.59 = bf16[4,80,384]{2,1,0:T(8,128)(2,1)} custom-call(bf16[4,592,256]{2,1,0:T(8,128)(2,1)S(1)} %all-to-all-done.near_in._2, bf16[4,128,256]{2,1,0:T(8,128)(2,1)} %get-tuple-element.31.middle, bf16[4,4,32,256]{3,2,1,0:T(8,128)(2,1)S(1)} %all-to-all-done.1.hi, f32[2,336,128]{2,1,0:T(8,128)} %get-tuple-element.28._.m_in), custom_call_target="tpu_custom_call" | custom-call | tf_op jit(solution)/shard_map/pallas_call | solution.py:469
  56.5 9.1 %all_to_all.20.back = bf16[4,80,384]{2,1,0:T(8,128)(2,1)S(1)} all-to-all(bf16[4,80,384]{2,1,0:T(8,128)(2,1)} %shard_map.59), channel_id=1, replica_groups={{0,8,16,24},{32,40,48,56},{64,72,80,88},{96,104,112,120},{128,136,144,1..., dimensions={0} | all-to-all | bytes 491520 | tf_op jit(solution)/shard_map/all_to_all | solution.py:393
  65.6 2.8 %shard_map.60 = bf16[4,336,256]{2,1,0:T(8,128)(2,1)} custom-call(s32[2,3]{1,0:T(2,128)} %off_in.7, f32[2,336,128]{2,1,0:T(8,128)} %get-tuple-element.28._.m_in, f32[2,336,128]{2,1,0:T(8,128)} %get-tuple-element.29.l_in, bf16[4,80,384]{2,1,0:T(8,128)(2,1)S(1)} %all_to_all.20.back), custom_call_target="tpu_custom_call" | custom-call | tf_op jit(solution)/shard_map/pallas_call | solution.py:482
  68.4 3.5 %all-to-all-start.3 = ((bf16[4,336,256]{2,1,0:T(8,128)(2,1)}), bf16[4,336,256]{2,1,0:T(8,128)(2,1)S(1)}, u32[]{:S(2)}, u32[]{:S(2)}) async-start(bf16[4,336,256]{2,1,0:T(8,128)(2,1)} %shard_map.60), calls=%async_computation.3 | async-start | bytes 1376256 | tf_op jit(solution)/shard_map/all_to_all | solution.py:393
  71.9 0.8 slice.12
  72.6 0.0 collective-permute-done.e1
  72.6 0.1 slice.13
  72.7 0.0 collective-permute-done.1.e2
  72.7 0.1 slice.14
  72.8 2.6 %collective-permute-done.2.e3 = bf16[1296,256]{1,0:T(8,128)(2,1)S(1)} collective-permute-done((bf16[1296,256]{1,0:T(8,128)(2,1)}, bf16[1296,256]{1,0:T(8,128)(2,1)S(1)}, u32[]{:S(2)}, u32[]{:S(2)}) %collective-permute-start.2) | collective-permute-done | bytes 663584 | tf_op jit(solution)/shard_map/ppermute | solution.py:400
  75.5 0.1 slice.15
  75.6 4.1 %all-to-all-done.3.late = bf16[4,336,256]{2,1,0:T(8,128)(2,1)S(1)} async-done(((bf16[4,336,256]{2,1,0:T(8,128)(2,1)}), bf16[4,336,256]{2,1,0:T(8,128)(2,1)S(1)}, u32[]{:S(2)}, u32[]{:S(2)}) %all-to-all-start.3) | async-done | bytes 688160 | tf_op jit(solution)/shard_map/all_to_all | solution.py:393
  79.6 2.7 %shard_map.61 = (bf16[1024,256]{1,0:T(8,128)(2,1)S(1)}, bf16[1024,1024]{1,0:T(8,128)(2,1)S(1)}) custom-call(s32[4,3,2]{2,1,0:T(4,128)S(1)} %maximum_convert_fusion.marks, bf16[784,256]{1,0:T(8,128)(2,1)} %get-tuple-element.20._1.own, bf16[1296,256]{1,0:T(8,128)(2,1)S(1)} %collective-permute-done.e1, bf16[1296,256]{1,0:T(8,128)(2,1)S(1)} %collective-permute-done.1.e2, ...), custom_call_target="tpu_custom_call" | custom-call | tf_op jit(solution)/shard_map/pallas_call | solution.py:498
  82.4 10.6 %collective-permute-start.6 = (bf16[1024,256]{1,0:T(8,128)(2,1)S(1)}, bf16[1024,256]{1,0:T(8,128)(2,1)S(1)}, u32[]{:S(2)}, u32[]{:S(2)}) collective-permute-start(bf16[1024,256]{1,0:T(8,128)(2,1)S(1)} %get-tuple-element.34), channel_id=1, source_target_pairs={{0,1},{1,0},{2,3},{3,2},{4,5},{5,4},{6,7},{7,6},{8,9},{9,8},{10,11... | collective-permute-start | bytes 1572872 | tf_op jit(solution)/shard_map/ppermute | solution.py:517
  93.0 1.7 %shard_map.62.keep = f32[1024,256]{1,0:T(8,128)S(1)} custom-call(bf16[1024,1024]{1,0:T(8,128)(2,1)S(1)} %get-tuple-element.33.whole, bf16[1296,256]{1,0:T(8,128)(2,1)S(1)} %collective-permute-done.e1, bf16[1296,256]{1,0:T(8,128)(2,1)S(1)} %collective-permute-done.1.e2, bf16[1296,256]{1,0:T(8,128)(2,1)S(1)} %collective-permute-done.2.e3, bf16[256,2048]{1,0:T(8,128)(2,1)} %w.5), custom_call_target="tpu_custom_call" | custom-call | tf_op jit(solution)/shard_map/pallas_call | solution.py:510
  94.7 0.0 collective-permute-done.6.other
  94.7 1.0 %shard_map.63 = bf16[1024,256]{1,0:T(8,128)(2,1)} custom-call(f32[1024,256]{1,0:T(8,128)S(1)} %shard_map.62.keep, bf16[1024,256]{1,0:T(8,128)(2,1)S(1)} %collective-permute-done.6.other), custom_call_target="tpu_custom_call" | custom-call | tf_op jit(solution)/shard_map/pallas_call | solution.py:518
  (1 shorter events, 0.0 us)
Async XLA Ops:
  2.7 5.2 %copy-start = (bf16[160,256]{1,0:T(8,128)(2,1)S(1)}, bf16[160,256]{1,0:T(8,128)(2,1)}, u32[]{:S(2)}) copy-start(bf16[160,256]{1,0:T(8,128)(2,1)} %get-tuple-element.30.z0) | copy-start | bytes 245764
  2.7 21.6 %all-to-all-start = ((bf16[4,592,256]{2,1,0:T(8,128)(2,1)}), bf16[4,592,256]{2,1,0:T(8,128)(2,1)S(1)}, u32[]{:S(2)}, u32[]{:S(2)}) async-start(bf16[4,592,256]{2,1,0:T(8,128)(2,1)} %get-tuple-element.25), calls=%async_computation | async-start | bytes 2424832 | tf_op jit(solution)/shard_map/all_to_all | solution.py:393
  7.9 16.4 %collective-permute-start.5 = (bf16[160,256]{1,0:T(8,128)(2,1)S(1)}, bf16[160,256]{1,0:T(8,128)(2,1)S(1)}, u32[]{:S(2)}, u32[]{:S(2)}) collective-permute-start(bf16[160,256]{1,0:T(8,128)(2,1)S(1)} %copy-done), channel_id=1, source_target_pairs={{0,96},{8,104},{16,112},{24,120},{32,0},{40,8},{48,16},{56,24},{64... | collective-permute-start | bytes 245768 | tf_op jit(solution)/shard_map/ppermute | solution.py:397
  14.1 10.2 %collective-permute-start.4 = (bf16[160,256]{1,0:T(8,128)(2,1)S(1)}, bf16[160,256]{1,0:T(8,128)(2,1)S(1)}, u32[]{:S(2)}, u32[]{:S(2)}) collective-permute-start(bf16[160,256]{1,0:T(8,128)(2,1)S(1)} %copy-done), channel_id=1, source_target_pairs={{0,64},{8,72},{16,80},{24,88},{32,96},{40,104},{48,112},{56,120},{... | collective-permute-start | bytes 245768 | tf_op jit(solution)/shard_map/ppermute | solution.py:397
  16.1 8.3 %collective-permute-start.3 = (bf16[160,256]{1,0:T(8,128)(2,1)S(1)}, bf16[160,256]{1,0:T(8,128)(2,1)S(1)}, u32[]{:S(2)}, u32[]{:S(2)}) collective-permute-start(bf16[160,256]{1,0:T(8,128)(2,1)S(1)} %copy-done), channel_id=1, source_target_pairs={{0,32},{8,40},{16,48},{24,56},{32,64},{40,72},{48,80},{56,88},{64,... | collective-permute-start | bytes 245768 | tf_op jit(solution)/shard_map/ppermute | solution.py:397
  25.2 28.7 %all-to-all-start.1 = ((bf16[4,4,32,256]{3,2,1,0:T(8,128)(2,1)}), bf16[4,4,32,256]{3,2,1,0:T(8,128)(2,1)S(1)}, u32[]{:S(2)}, u32[]{:S(2)}) async-start(bf16[4,4,32,256]{3,2,1,0:T(8,128)(2,1)} %get-tuple-element.32), calls=%async_computation.1 | async-start | bytes 524288 | tf_op jit(solution)/shard_map/all_to_all | solution.py:393
  39.5 33.1 %collective-permute-start = (bf16[1296,256]{1,0:T(8,128)(2,1)}, bf16[1296,256]{1,0:T(8,128)(2,1)S(1)}, u32[]{:S(2)}, u32[]{:S(2)}) collective-permute-start(bf16[1296,256]{1,0:T(8,128)(2,1)} %get-tuple-element.21), channel_id=1, source_target_pairs={{0,2},{1,3},{2,4},{3,5},{4,6},{5,7},{6,0},{7,1},{8,10},{9,11},{10,... | collective-permute-start | bytes 1990664 | tf_op jit(solution)/shard_map/ppermute | solution.py:400
  42.6 30.1 %collective-permute-start.1 = (bf16[1296,256]{1,0:T(8,128)(2,1)}, bf16[1296,256]{1,0:T(8,128)(2,1)S(1)}, u32[]{:S(2)}, u32[]{:S(2)}) collective-permute-start(bf16[1296,256]{1,0:T(8,128)(2,1)} %get-tuple-element.22), channel_id=1, source_target_pairs={{0,4},{1,5},{2,6},{3,7},{4,0},{5,1},{6,2},{7,3},{8,12},{9,13},{10,... | collective-permute-start | bytes 1990664 | tf_op jit(solution)/shard_map/ppermute | solution.py:400
  47.0 28.4 %collective-permute-start.2 = (bf16[1296,256]{1,0:T(8,128)(2,1)}, bf16[1296,256]{1,0:T(8,128)(2,1)S(1)}, u32[]{:S(2)}, u32[]{:S(2)}) collective-permute-start(bf16[1296,256]{1,0:T(8,128)(2,1)} %get-tuple-element.23), channel_id=1, source_target_pairs={{0,6},{1,7},{2,0},{3,1},{4,2},{5,3},{6,4},{7,5},{8,14},{9,15},{10,... | collective-permute-start | bytes 1990664 | tf_op jit(solution)/shard_map/ppermute | solution.py:400
  68.4 11.3 %all-to-all-start.3 = ((bf16[4,336,256]{2,1,0:T(8,128)(2,1)}), bf16[4,336,256]{2,1,0:T(8,128)(2,1)S(1)}, u32[]{:S(2)}, u32[]{:S(2)}) async-start(bf16[4,336,256]{2,1,0:T(8,128)(2,1)} %shard_map.60), calls=%async_computation.3 | async-start | bytes 1376256 | tf_op jit(solution)/shard_map/all_to_all | solution.py:393
  82.4 12.3 %collective-permute-start.6 = (bf16[1024,256]{1,0:T(8,128)(2,1)S(1)}, bf16[1024,256]{1,0:T(8,128)(2,1)S(1)}, u32[]{:S(2)}, u32[]{:S(2)}) collective-permute-start(bf16[1024,256]{1,0:T(8,128)(2,1)S(1)} %get-tuple-element.34), channel_id=1, source_target_pairs={{0,1},{1,0},{2,3},{3,2},{4,5},{5,4},{6,7},{7,6},{8,9},{9,8},{10,11... | collective-permute-start | bytes 1572872 | tf_op jit(solution)/shard_map/ppermute | solution.py:517

commit v6 on v5

--- a/solution.py
+++ b/solution.py
@@ -72,6 +72,7 @@
     first = copy(off_in, off, sems.at[0])
     loads = [copy(source, raw.at[slot], sems.at[1 + slot]) for slot, source in enumerate((k, v, q))]
     moves = []
+    cuts = (0, count[0], 2 * count[0], near.shape[0])
     first.wait()
     for slot in range(3):
         loads[slot].wait()
@@ -91,10 +92,12 @@
                 at = 2 * count[0]
                 near[at : at + count[1], half(head)] = picks[1]
                 near[at + count[1] : at + count[1] + count[2], half(head)] = picks[2]
+        piece = pl.ds(cuts[slot], cuts[slot + 1] - cuts[slot])
+        for target in range(4):
+            moves.append(copy(near.at[piece, :], near_out.at[target, piece, :], sems.at[9 + 4 * slot + target]))
         if slot == 1:
-            moves = [copy(pack, near_z, sems.at[4])]
+            moves.append(copy(pack, near_z, sems.at[4]))
     moves.append(copy(query, own_q, sems.at[8]))
-    moves += [copy(near, near_out.at[target], sems.at[9 + target]) for target in range(4)]
     for moved in moves:
         moved.wait()
 
@@ -238,19 +241,18 @@
         moved.wait()
 
 
-def far_kernel(near_in, middle, hi, _, back, near, zs, part, sems):
+def far_kernel(near, middle, hi, _, back, zs, part, sems):
     seq = lax.axis_index("seq")
     mine, line = lax.rem(seq, 4), lax.div(seq, 4)
-    loads = [copy(middle, zs, sems.at[2])]
-    loads.append(copy(near_in.at[:, pl.ds(512, 80), :], near, sems.at[0]))
-    for moved in loads:
-        moved.wait()
-    at = 0
-    for level, count in ((1, 64), (2, 16)):
+    skip = near.shape[1] - part.shape[1]
+    held = copy(middle, zs, sems.at[0])
+    for level, count, at in ((2, 16, 64), (1, 64, 0)):
+        if level == 1:
+            held.wait()
         place = lax.rem(line, 4) if level == 1 else line
         logs = []
         for head in range(2):
-            queries = near[:, at : at + count, half(head)].reshape(-1, HEAD_DIM)
+            queries = near[:, skip + at : skip + at + count, half(head)].reshape(-1, HEAD_DIM)
             if level == 1:
                 keys = zs[:, :count, half(head)].reshape(-1, HEAD_DIM)
                 values = zs[:, count:, half(head)].reshape(-1, HEAD_DIM)
@@ -272,18 +274,13 @@
             left = left - left.astype(BF16).astype(F32)
             both = jnp.where(lax.rem(lane, HEAD_DIM // 2) < 16 * piece, both, left.astype(BF16))
         part[:, at : at + count, 2 * HEAD_DIM :] = both.reshape(4, count, HEAD_DIM)
-        at += count
     moves = [copy(part, back, sems.at[1])]
     for moved in moves:
         moved.wait()
 
 
-def merge_kernel(off_in, m_in, l_in, back, late, off, mixed, logs, run, run_logs, pack, sems):
+def merge_kernel(off, mixed, logs, back, late, run, run_logs, pack, sems):
     rows = run.shape[1]
-    places = ((off_in, off), (m_in, mixed), (l_in, logs))
-    loads = [copy(source, target, sems.at[slot]) for slot, (source, target) in enumerate(places)]
-    for moved in loads:
-        moved.wait()
     for head in range(2):
         spread_rows(off, head, mixed, run)
         spread_rows(off, head, logs, run_logs)
@@ -403,6 +400,7 @@
     late_rows = sum(count)
     near_rows = 2 * count[0] + count[1] + count[2]
     z_rows = 2 * count[1] + 2 * count[2]
+    raw_offsets = offsets
     queries, keys, values, offsets, w_out = map(stay, (queries, keys, values, offsets, w_out))
     near, near_z, own_q = call(
         pick_kernel,
@@ -416,7 +414,7 @@
             pltpu.VMEM((near_rows, width), BF16),
             pltpu.VMEM((z_rows, width), BF16),
             pltpu.VMEM((count[0], width), BF16),
-            dma((13,)),
+            dma((21,)),
         ],
     )(offsets, queries, keys, values)
     zs = [near_z] + [shift_z(near_z, by) for by in (1, 2, 3)]
@@ -469,31 +467,27 @@
     back = call(
         far_kernel,
         pltpu.HBM((4, count[1] + count[2], 3 * HEAD_DIM), BF16),
-        [ANY, HBM, VMEM, HBM],
+        [VMEM, HBM, VMEM, HBM],
         HBM,
         [
-            pltpu.VMEM((4, count[1] + count[2], width), BF16),
             pltpu.VMEM((4, 2 * count[1], width), BF16),
             pltpu.VMEM((4, count[1] + count[2], 3 * HEAD_DIM), BF16),
-            dma((7,)),
+            dma((2,)),
         ],
     )(near, stay(middle), far_z, stay(mixed))
     back = swap(back, "seq", along_y)
     late = call(
         merge_kernel,
         pltpu.HBM((4, late_rows, width), BF16),
-        [HBM] * 3 + [VMEM] + [ANY] * 0,
+        [SMEM] + [VMEM] * 3,
         HBM,
         [
-            pltpu.SMEM((2, 3), jnp.int32),
-            pltpu.VMEM(mixed.shape, F32),
-            pltpu.VMEM(mixed.shape, F32),
             pltpu.VMEM((2, rows, HEAD_DIM), F32),
             pltpu.VMEM((2, rows, HEAD_DIM), F32),
             pltpu.VMEM((late_rows, width), BF16),
             dma((4,)),
         ],
-    )(offsets, stay(mixed), stay(logs), back)
+    )(raw_offsets, mixed, logs, back)
     late = swap(late, "head", along_x)
     send, whole = call(
         project_kernel,

time: 96.6 us -> 96.2 us (level)
  no operation moved by 1% of the time
where the time goes in v6:
time: 96.2 us; the launch traced here: 95.5 us
  starting transfers between devices  54.5 us (57%)
  Pallas kernels  23.9 us (25%)
  blocking collectives  9.11 us (9%)
  waiting for transfers between devices  6.73 us (7%)
  local copies, waits for them, and re-layouts  1.07 us (1%)
    all_to_all x3, starting transfers between devices, swap(): return lax.all_to_all(value, axis, 0, 0, axis_index_groups=groups)  22.9 us
    ppermute x1, starting transfers between devices, shards(): lax.ppermute(send, 'head', [(place, place ^ 1) for place in range(heads)])  10.7 us
    ppermute x3, starting transfers between devices, shift_x(): lax.ppermute(value, 'head', [(place, (place + 2 * by) % heads) for place...  10.5 us
    ppermute x3, starting transfers between devices, shift_z(): return lax.ppermute(value, 'seq', hops)  10.4 us
    all_to_all x1, blocking collectives, swap(): return lax.all_to_all(value, axis, 0, 0, axis_index_groups=groups)  9.11 us
    pallas_call x1, Pallas kernels, shards(): call(local_kernel, (pltpu.HBM((most + 16, width), BF16), packed, packed,...  6.04 us
    all_to_all x3, waiting for transfers between devices, swap(): return lax.all_to_all(value, axis, 0, 0, axis_index_groups=groups)  4.02 us
    pallas_call x1, Pallas kernels, shards(): call(near_kernel, (kept, kept), [HBM] * 2 + [ANY] + [HBM] * 2, (HBM,) * 2...  3.92 us
  transfers between devices with their start and end apart: 10, of which 2 were waited for; matrix products, arithmetic and copies ran while one was open for 1% of the time, Pallas kernels for 18%

profile of v6, /device:TPU:1, one launch (start us, length us, event | category | flops | bytes accessed | tf_op | source)
XLA Modules:
  0.0 95.5 jit_solution(9745905688907211837)
XLA Ops:
  0.0 2.4 %shard_map.56 = (bf16[4,592,256]{2,1,0:T(8,128)(2,1)}, bf16[160,256]{1,0:T(8,128)(2,1)}, bf16[256,256]{1,0:T(8,128)(2,1)}) custom-call(s32[2,3]{1,0:T(2,128)} %off.1, bf16[1024,256]{1,0:T(8,128)(2,1)} %q.3, bf16[1024,256]{1,0:T(8,128)(2,1)} %k.3, bf16[1024,256]{1,0:T(8,128)(2,1)} %v.3), custom_call_target="tpu_custom_call" | custom-call | tf_op jit(solution)/shard_map/pallas_call | solution.py:405
  2.4 0.0 copy-start.2
  2.4 5.2 %all-to-all-start = ((bf16[4,592,256]{2,1,0:T(8,128)(2,1)}), bf16[4,592,256]{2,1,0:T(8,128)(2,1)S(1)}, u32[]{:S(2)}, u32[]{:S(2)}) async-start(bf16[4,592,256]{2,1,0:T(8,128)(2,1)} %get-tuple-element.25), calls=%async_computation | async-start | bytes 2424832 | tf_op jit(solution)/shard_map/all_to_all | solution.py:390
  7.6 0.0 copy-done.2
  7.6 6.2 %collective-permute-start.5 = (bf16[160,256]{1,0:T(8,128)(2,1)S(1)}, bf16[160,256]{1,0:T(8,128)(2,1)S(1)}, u32[]{:S(2)}, u32[]{:S(2)}) collective-permute-start(bf16[160,256]{1,0:T(8,128)(2,1)S(1)} %copy-done.2), channel_id=1, source_target_pairs={{0,96},{8,104},{16,112},{24,120},{32,0},{40,8},{48,16},{56,24},{64... | collective-permute-start | bytes 245768 | tf_op jit(solution)/shard_map/ppermute | solution.py:394
  13.9 1.9 %collective-permute-start.4 = (bf16[160,256]{1,0:T(8,128)(2,1)S(1)}, bf16[160,256]{1,0:T(8,128)(2,1)S(1)}, u32[]{:S(2)}, u32[]{:S(2)}) collective-permute-start(bf16[160,256]{1,0:T(8,128)(2,1)S(1)} %copy-done.2), channel_id=1, source_target_pairs={{0,64},{8,72},{16,80},{24,88},{32,96},{40,104},{48,112},{56,120},{... | collective-permute-start | bytes 245768 | tf_op jit(solution)/shard_map/ppermute | solution.py:394
  15.8 2.2 %collective-permute-start.3 = (bf16[160,256]{1,0:T(8,128)(2,1)S(1)}, bf16[160,256]{1,0:T(8,128)(2,1)S(1)}, u32[]{:S(2)}, u32[]{:S(2)}) collective-permute-start(bf16[160,256]{1,0:T(8,128)(2,1)S(1)} %copy-done.2), channel_id=1, source_target_pairs={{0,32},{8,40},{16,48},{24,56},{32,64},{40,72},{48,80},{56,88},{64,... | collective-permute-start | bytes 245768 | tf_op jit(solution)/shard_map/ppermute | solution.py:394
  18.0 6.0 %shard_map.55 = (bf16[784,256]{1,0:T(8,128)(2,1)}, bf16[1296,256]{1,0:T(8,128)(2,1)}, bf16[1296,256]{1,0:T(8,128)(2,1)}, bf16[1296,256]{1,0:T(8,128)(2,1)}, f32[...) custom-call(s32[2,3]{1,0:T(2,128)} %off.1, bf16[1024,256]{1,0:T(8,128)(2,1)} %q.3, bf16[1024,256]{1,0:T(8,128)(2,1)} %k.3, ...), custom_call_target="tpu_custom_call" | custom-call | tf_op jit(solution)/shard_map/pallas_call | solution.py:425
  24.0 0.0 collective-permute-done.5.z3
  24.0 0.0 collective-permute-done.4.z2
  24.1 0.0 collective-permute-done.3.z1
  24.1 0.0 all-to-all-done.near_in._2.near
  24.1 0.9 shard_map.58
  25.0 14.2 %all-to-all-start.1 = ((bf16[4,4,32,256]{3,2,1,0:T(8,128)(2,1)}), bf16[4,4,32,256]{3,2,1,0:T(8,128)(2,1)S(1)}, u32[]{:S(2)}, u32[]{:S(2)}) async-start(bf16[4,4,32,256]{3,2,1,0:T(8,128)(2,1)} %get-tuple-element.32), calls=%async_computation.1 | async-start | bytes 524288 | tf_op jit(solution)/shard_map/all_to_all | solution.py:390
  39.2 3.1 %collective-permute-start = (bf16[1296,256]{1,0:T(8,128)(2,1)}, bf16[1296,256]{1,0:T(8,128)(2,1)S(1)}, u32[]{:S(2)}, u32[]{:S(2)}) collective-permute-start(bf16[1296,256]{1,0:T(8,128)(2,1)} %get-tuple-element.21), channel_id=1, source_target_pairs={{0,2},{1,3},{2,4},{3,5},{4,6},{5,7},{6,0},{7,1},{8,10},{9,11},{10,... | collective-permute-start | bytes 1990664 | tf_op jit(solution)/shard_map/ppermute | solution.py:397
  42.4 4.3 %collective-permute-start.1 = (bf16[1296,256]{1,0:T(8,128)(2,1)}, bf16[1296,256]{1,0:T(8,128)(2,1)S(1)}, u32[]{:S(2)}, u32[]{:S(2)}) collective-permute-start(bf16[1296,256]{1,0:T(8,128)(2,1)} %get-tuple-element.22), channel_id=1, source_target_pairs={{0,4},{1,5},{2,6},{3,7},{4,0},{5,1},{6,2},{7,3},{8,12},{9,13},{10,... | collective-permute-start | bytes 1990664 | tf_op jit(solution)/shard_map/ppermute | solution.py:397
  46.7 3.1 %collective-permute-start.2 = (bf16[1296,256]{1,0:T(8,128)(2,1)}, bf16[1296,256]{1,0:T(8,128)(2,1)S(1)}, u32[]{:S(2)}, u32[]{:S(2)}) collective-permute-start(bf16[1296,256]{1,0:T(8,128)(2,1)} %get-tuple-element.23), channel_id=1, source_target_pairs={{0,6},{1,7},{2,0},{3,1},{4,2},{5,3},{6,4},{7,5},{8,14},{9,15},{10,... | collective-permute-start | bytes 1990664 | tf_op jit(solution)/shard_map/ppermute | solution.py:397
  49.8 3.9 %shard_map.57 = (f32[2,336,128]{2,1,0:T(8,128)}, f32[2,336,128]{2,1,0:T(8,128)}) custom-call(s32[2,3]{1,0:T(2,128)} %off.1, bf16[256,256]{1,0:T(8,128)(2,1)} %get-tuple-element.24.own_q, bf16[4,592,256]{2,1,0:T(8,128)(2,1)S(1)} %all-to-all-done.near_in._2.near, f32[2,336,128]{2,1,0:T(8,128)} %get-tuple-element.26.m_in, f32[2,336,128]{2,1,0:T(8,128)} %get-tuple-element.27.l_in), custom_call_target="tpu_custom_call" | custom-call | tf_op jit(solution)/shard_map/pallas_call | solution.py:451
  53.7 0.0 all-to-all-done.1.hi
  53.7 0.0 copy-start
  53.7 0.0 copy-start.1
  53.7 0.0 copy-start.3
  53.7 2.8 %shard_map.59 = bf16[4,80,384]{2,1,0:T(8,128)(2,1)} custom-call(bf16[4,592,256]{2,1,0:T(8,128)(2,1)S(1)} %all-to-all-done.near_in._2.near, bf16[4,128,256]{2,1,0:T(8,128)(2,1)} %get-tuple-element.31.middle, bf16[4,4,32,256]{3,2,1,0:T(8,128)(2,1)S(1)} %all-to-all-done.1.hi, f32[2,336,128]{2,1,0:T(8,128)} %get-tuple-element.28._.mixed), custom_call_target="tpu_custom_call" | custom-call | tf_op jit(solution)/shard_map/pallas_call | solution.py:467
  56.5 9.1 %all_to_all.20.back = bf16[4,80,384]{2,1,0:T(8,128)(2,1)S(1)} all-to-all(bf16[4,80,384]{2,1,0:T(8,128)(2,1)} %shard_map.59), channel_id=1, replica_groups={{0,8,16,24},{32,40,48,56},{64,72,80,88},{96,104,112,120},{128,136,144,1..., dimensions={0} | all-to-all | bytes 491520 | tf_op jit(solution)/shard_map/all_to_all | solution.py:390
  65.6 0.0 copy-done
  65.7 0.0 copy-done.1
  65.7 0.0 copy-done.3
  65.7 2.3 %shard_map.60 = bf16[4,336,256]{2,1,0:T(8,128)(2,1)} custom-call(s32[2,3]{1,0:T(2,128)S(1)} %copy-done.3, f32[2,336,128]{2,1,0:T(8,128)S(1)} %copy-done, f32[2,336,128]{2,1,0:T(8,128)S(1)} %copy-done.1, bf16[4,80,384]{2,1,0:T(8,128)(2,1)S(1)} %all_to_all.20.back), custom_call_target="tpu_custom_call" | custom-call | tf_op jit(solution)/shard_map/pallas_call | solution.py:479
  68.0 3.5 %all-to-all-start.3 = ((bf16[4,336,256]{2,1,0:T(8,128)(2,1)}), bf16[4,336,256]{2,1,0:T(8,128)(2,1)S(1)}, u32[]{:S(2)}, u32[]{:S(2)}) async-start(bf16[4,336,256]{2,1,0:T(8,128)(2,1)} %shard_map.60), calls=%async_computation.3 | async-start | bytes 1376256 | tf_op jit(solution)/shard_map/all_to_all | solution.py:390
  71.5 0.8 slice.12
  72.3 0.0 collective-permute-done.e1
  72.3 0.1 slice.13
  72.4 0.0 collective-permute-done.1.e2
  72.4 0.1 slice.14
  72.5 2.7 %collective-permute-done.2.e3 = bf16[1296,256]{1,0:T(8,128)(2,1)S(1)} collective-permute-done((bf16[1296,256]{1,0:T(8,128)(2,1)}, bf16[1296,256]{1,0:T(8,128)(2,1)S(1)}, u32[]{:S(2)}, u32[]{:S(2)}) %collective-permute-start.2) | collective-permute-done | bytes 663584 | tf_op jit(solution)/shard_map/ppermute | solution.py:397
  75.2 0.1 slice.15
  75.3 4.0 %all-to-all-done.3.late = bf16[4,336,256]{2,1,0:T(8,128)(2,1)S(1)} async-done(((bf16[4,336,256]{2,1,0:T(8,128)(2,1)}), bf16[4,336,256]{2,1,0:T(8,128)(2,1)S(1)}, u32[]{:S(2)}, u32[]{:S(2)}) %all-to-all-start.3) | async-done | bytes 688160 | tf_op jit(solution)/shard_map/all_to_all | solution.py:390
  79.3 2.7 %shard_map.61 = (bf16[1024,256]{1,0:T(8,128)(2,1)S(1)}, bf16[1024,1024]{1,0:T(8,128)(2,1)S(1)}) custom-call(s32[4,3,2]{2,1,0:T(4,128)S(1)} %maximum_convert_fusion.marks, bf16[784,256]{1,0:T(8,128)(2,1)} %get-tuple-element.20._1.own, bf16[1296,256]{1,0:T(8,128)(2,1)S(1)} %collective-permute-done.e1, bf16[1296,256]{1,0:T(8,128)(2,1)S(1)} %collective-permute-done.1.e2, ...), custom_call_target="tpu_custom_call" | custom-call | tf_op jit(solution)/shard_map/pallas_call | solution.py:492
  82.0 10.7 %collective-permute-start.6 = (bf16[1024,256]{1,0:T(8,128)(2,1)S(1)}, bf16[1024,256]{1,0:T(8,128)(2,1)S(1)}, u32[]{:S(2)}, u32[]{:S(2)}) collective-permute-start(bf16[1024,256]{1,0:T(8,128)(2,1)S(1)} %get-tuple-element.34), channel_id=1, source_target_pairs={{0,1},{1,0},{2,3},{3,2},{4,5},{5,4},{6,7},{7,6},{8,9},{9,8},{10,11... | collective-permute-start | bytes 1572872 | tf_op jit(solution)/shard_map/ppermute | solution.py:511
  92.7 1.7 %shard_map.62.keep = f32[1024,256]{1,0:T(8,128)S(1)} custom-call(bf16[1024,1024]{1,0:T(8,128)(2,1)S(1)} %get-tuple-element.33.whole, bf16[1296,256]{1,0:T(8,128)(2,1)S(1)} %collective-permute-done.e1, bf16[1296,256]{1,0:T(8,128)(2,1)S(1)} %collective-permute-done.1.e2, bf16[1296,256]{1,0:T(8,128)(2,1)S(1)} %collective-permute-done.2.e3, bf16[256,2048]{1,0:T(8,128)(2,1)} %w.5), custom_call_target="tpu_custom_call" | custom-call | tf_op jit(solution)/shard_map/pallas_call | solution.py:504
  94.4 0.0 collective-permute-done.6.other
  94.4 1.0 %shard_map.63 = bf16[1024,256]{1,0:T(8,128)(2,1)} custom-call(f32[1024,256]{1,0:T(8,128)S(1)} %shard_map.62.keep, bf16[1024,256]{1,0:T(8,128)(2,1)S(1)} %collective-permute-done.6.other), custom_call_target="tpu_custom_call" | custom-call | tf_op jit(solution)/shard_map/pallas_call | solution.py:512
  (1 shorter events, 0.0 us)
Async XLA Ops:
  2.4 5.2 %copy-start.2 = (bf16[160,256]{1,0:T(8,128)(2,1)S(1)}, bf16[160,256]{1,0:T(8,128)(2,1)}, u32[]{:S(2)}) copy-start(bf16[160,256]{1,0:T(8,128)(2,1)} %get-tuple-element.30.z0) | copy-start | bytes 245764
  2.4 21.6 %all-to-all-start = ((bf16[4,592,256]{2,1,0:T(8,128)(2,1)}), bf16[4,592,256]{2,1,0:T(8,128)(2,1)S(1)}, u32[]{:S(2)}, u32[]{:S(2)}) async-start(bf16[4,592,256]{2,1,0:T(8,128)(2,1)} %get-tuple-element.25), calls=%async_computation | async-start | bytes 2424832 | tf_op jit(solution)/shard_map/all_to_all | solution.py:390
  7.6 16.4 %collective-permute-start.5 = (bf16[160,256]{1,0:T(8,128)(2,1)S(1)}, bf16[160,256]{1,0:T(8,128)(2,1)S(1)}, u32[]{:S(2)}, u32[]{:S(2)}) collective-permute-start(bf16[160,256]{1,0:T(8,128)(2,1)S(1)} %copy-done.2), channel_id=1, source_target_pairs={{0,96},{8,104},{16,112},{24,120},{32,0},{40,8},{48,16},{56,24},{64... | collective-permute-start | bytes 245768 | tf_op jit(solution)/shard_map/ppermute | solution.py:394
  13.9 10.2 %collective-permute-start.4 = (bf16[160,256]{1,0:T(8,128)(2,1)S(1)}, bf16[160,256]{1,0:T(8,128)(2,1)S(1)}, u32[]{:S(2)}, u32[]{:S(2)}) collective-permute-start(bf16[160,256]{1,0:T(8,128)(2,1)S(1)} %copy-done.2), channel_id=1, source_target_pairs={{0,64},{8,72},{16,80},{24,88},{32,96},{40,104},{48,112},{56,120},{... | collective-permute-start | bytes 245768 | tf_op jit(solution)/shard_map/ppermute | solution.py:394
  15.8 8.3 %collective-permute-start.3 = (bf16[160,256]{1,0:T(8,128)(2,1)S(1)}, bf16[160,256]{1,0:T(8,128)(2,1)S(1)}, u32[]{:S(2)}, u32[]{:S(2)}) collective-permute-start(bf16[160,256]{1,0:T(8,128)(2,1)S(1)} %copy-done.2), channel_id=1, source_target_pairs={{0,32},{8,40},{16,48},{24,56},{32,64},{40,72},{48,80},{56,88},{64,... | collective-permute-start | bytes 245768 | tf_op jit(solution)/shard_map/ppermute | solution.py:394
  25.0 28.7 %all-to-all-start.1 = ((bf16[4,4,32,256]{3,2,1,0:T(8,128)(2,1)}), bf16[4,4,32,256]{3,2,1,0:T(8,128)(2,1)S(1)}, u32[]{:S(2)}, u32[]{:S(2)}) async-start(bf16[4,4,32,256]{3,2,1,0:T(8,128)(2,1)} %get-tuple-element.32), calls=%async_computation.1 | async-start | bytes 524288 | tf_op jit(solution)/shard_map/all_to_all | solution.py:390
  39.2 33.1 %collective-permute-start = (bf16[1296,256]{1,0:T(8,128)(2,1)}, bf16[1296,256]{1,0:T(8,128)(2,1)S(1)}, u32[]{:S(2)}, u32[]{:S(2)}) collective-permute-start(bf16[1296,256]{1,0:T(8,128)(2,1)} %get-tuple-element.21), channel_id=1, source_target_pairs={{0,2},{1,3},{2,4},{3,5},{4,6},{5,7},{6,0},{7,1},{8,10},{9,11},{10,... | collective-permute-start | bytes 1990664 | tf_op jit(solution)/shard_map/ppermute | solution.py:397
  42.4 30.0 %collective-permute-start.1 = (bf16[1296,256]{1,0:T(8,128)(2,1)}, bf16[1296,256]{1,0:T(8,128)(2,1)S(1)}, u32[]{:S(2)}, u32[]{:S(2)}) collective-permute-start(bf16[1296,256]{1,0:T(8,128)(2,1)} %get-tuple-element.22), channel_id=1, source_target_pairs={{0,4},{1,5},{2,6},{3,7},{4,0},{5,1},{6,2},{7,3},{8,12},{9,13},{10,... | collective-permute-start | bytes 1990664 | tf_op jit(solution)/shard_map/ppermute | solution.py:397
  46.7 28.5 %collective-permute-start.2 = (bf16[1296,256]{1,0:T(8,128)(2,1)}, bf16[1296,256]{1,0:T(8,128)(2,1)S(1)}, u32[]{:S(2)}, u32[]{:S(2)}) collective-permute-start(bf16[1296,256]{1,0:T(8,128)(2,1)} %get-tuple-element.23), channel_id=1, source_target_pairs={{0,6},{1,7},{2,0},{3,1},{4,2},{5,3},{6,4},{7,5},{8,14},{9,15},{10,... | collective-permute-start | bytes 1990664 | tf_op jit(solution)/shard_map/ppermute | solution.py:397
  53.7 11.9 %copy-start = (f32[2,336,128]{2,1,0:T(8,128)S(1)}, f32[2,336,128]{2,1,0:T(8,128)}, u32[]{:S(2)}) copy-start(f32[2,336,128]{2,1,0:T(8,128)} %get-tuple-element.28._.mixed) | copy-start | bytes 1032196
  53.7 11.9 %copy-start.1 = (f32[2,336,128]{2,1,0:T(8,128)S(1)}, f32[2,336,128]{2,1,0:T(8,128)}, u32[]{:S(2)}) copy-start(f32[2,336,128]{2,1,0:T(8,128)} %get-tuple-element.29.logs) | copy-start | bytes 1032196
  53.7 11.9 %copy-start.3 = (s32[2,3]{1,0:T(2,128)S(1)}, s32[2,3]{1,0:T(2,128)}, u32[]{:S(2)}) copy-start(s32[2,3]{1,0:T(2,128)} %off.1) | copy-start | bytes 76
  68.0 11.3 %all-to-all-start.3 = ((bf16[4,336,256]{2,1,0:T(8,128)(2,1)}), bf16[4,336,256]{2,1,0:T(8,128)(2,1)S(1)}, u32[]{:S(2)}, u32[]{:S(2)}) async-start(bf16[4,336,256]{2,1,0:T(8,128)(2,1)} %shard_map.60), calls=%async_computation.3 | async-start | bytes 1376256 | tf_op jit(solution)/shard_map/all_to_all | solution.py:390
  82.0 12.4 %collective-permute-start.6 = (bf16[1024,256]{1,0:T(8,128)(2,1)S(1)}, bf16[1024,256]{1,0:T(8,128)(2,1)S(1)}, u32[]{:S(2)}, u32[]{:S(2)}) collective-permute-start(bf16[1024,256]{1,0:T(8,128)(2,1)S(1)} %get-tuple-element.34), channel_id=1, source_target_pairs={{0,1},{1,0},{2,3},{3,2},{4,5},{5,4},{6,7},{7,6},{8,9},{9,8},{10,11... | collective-permute-start | bytes 1572872 | tf_op jit(solution)/shard_map/ppermute | solution.py:511

commit v7 on v6

--- a/solution.py
+++ b/solution.py
@@ -245,10 +245,8 @@
     seq = lax.axis_index("seq")
     mine, line = lax.rem(seq, 4), lax.div(seq, 4)
     skip = near.shape[1] - part.shape[1]
-    held = copy(middle, zs, sems.at[0])
-    for level, count, at in ((2, 16, 64), (1, 64, 0)):
-        if level == 1:
-            held.wait()
+    copy(middle, zs, sems.at[0]).wait()
+    for level, count, at in ((1, 64, 0), (2, 16, 64)):
         place = lax.rem(line, 4) if level == 1 else line
         logs = []
         for head in range(2):

time: 96.2 us -> 96 us (level)
  transfers between devices with their start and end apart: 10 -> 10, of which waited for: 2 -> 2; matrix products, arithmetic and copies ran while one was open for 1% -> 1% of each run, Pallas kernels for 18% -> 17%
where the time goes in v7:
time: 96 us; the launch traced here: 95.2 us
  starting transfers between devices  54.4 us (57%)
  Pallas kernels  23.6 us (25%)
  blocking collectives  9.11 us (9%)
  waiting for transfers between devices  6.73 us (7%)
  local copies, waits for them, and re-layouts  1.07 us (1%)
    all_to_all x3, starting transfers between devices, swap(): return lax.all_to_all(value, axis, 0, 0, axis_index_groups=groups)  22.9 us
    ppermute x1, starting transfers between devices, shards(): lax.ppermute(send, 'head', [(place, place ^ 1) for place in range(heads)])  10.7 us
    ppermute x3, starting transfers between devices, shift_x(): lax.ppermute(value, 'head', [(place, (place + 2 * by) % heads) for place...  10.5 us
    ppermute x3, starting transfers between devices, shift_z(): return lax.ppermute(value, 'seq', hops)  10.4 us
    all_to_all x1, blocking collectives, swap(): return lax.all_to_all(value, axis, 0, 0, axis_index_groups=groups)  9.11 us
    pallas_call x1, Pallas kernels, shards(): call(local_kernel, (pltpu.HBM((most + 16, width), BF16), packed, packed,...  6.04 us
    pallas_call x1, Pallas kernels, shards(): call(near_kernel, (kept, kept), [HBM] * 2 + [ANY] + [HBM] * 2, (HBM,) * 2...  3.91 us
    all_to_all x3, waiting for transfers between devices, swap(): return lax.all_to_all(value, axis, 0, 0, axis_index_groups=groups)  3.71 us
  transfers between devices with their start and end apart: 10, of which 2 were waited for; matrix products, arithmetic and copies ran while one was open for 1% of the time, Pallas kernels for 17%

profile of v7, /device:TPU:1, one launch (start us, length us, event | category | flops | bytes accessed | tf_op | source)
XLA Modules:
  0.0 95.2 jit_solution(13023926700736580781)
XLA Ops:
  0.0 2.4 %shard_map.56 = (bf16[4,592,256]{2,1,0:T(8,128)(2,1)}, bf16[160,256]{1,0:T(8,128)(2,1)}, bf16[256,256]{1,0:T(8,128)(2,1)}) custom-call(s32[2,3]{1,0:T(2,128)} %off.1, bf16[1024,256]{1,0:T(8,128)(2,1)} %q.3, bf16[1024,256]{1,0:T(8,128)(2,1)} %k.3, bf16[1024,256]{1,0:T(8,128)(2,1)} %v.3), custom_call_target="tpu_custom_call" | custom-call | tf_op jit(solution)/shard_map/pallas_call | solution.py:403
  2.5 0.0 copy-start.2
  2.5 5.2 %all-to-all-start = ((bf16[4,592,256]{2,1,0:T(8,128)(2,1)}), bf16[4,592,256]{2,1,0:T(8,128)(2,1)S(1)}, u32[]{:S(2)}, u32[]{:S(2)}) async-start(bf16[4,592,256]{2,1,0:T(8,128)(2,1)} %get-tuple-element.25), calls=%async_computation | async-start | bytes 2424832 | tf_op jit(solution)/shard_map/all_to_all | solution.py:388
  7.6 0.0 copy-done.2
  7.6 6.2 %collective-permute-start.5 = (bf16[160,256]{1,0:T(8,128)(2,1)S(1)}, bf16[160,256]{1,0:T(8,128)(2,1)S(1)}, u32[]{:S(2)}, u32[]{:S(2)}) collective-permute-start(bf16[160,256]{1,0:T(8,128)(2,1)S(1)} %copy-done.2), channel_id=1, source_target_pairs={{0,96},{8,104},{16,112},{24,120},{32,0},{40,8},{48,16},{56,24},{64... | collective-permute-start | bytes 245768 | tf_op jit(solution)/shard_map/ppermute | solution.py:392
  13.9 1.9 %collective-permute-start.4 = (bf16[160,256]{1,0:T(8,128)(2,1)S(1)}, bf16[160,256]{1,0:T(8,128)(2,1)S(1)}, u32[]{:S(2)}, u32[]{:S(2)}) collective-permute-start(bf16[160,256]{1,0:T(8,128)(2,1)S(1)} %copy-done.2), channel_id=1, source_target_pairs={{0,64},{8,72},{16,80},{24,88},{32,96},{40,104},{48,112},{56,120},{... | collective-permute-start | bytes 245768 | tf_op jit(solution)/shard_map/ppermute | solution.py:392
  15.8 2.2 %collective-permute-start.3 = (bf16[160,256]{1,0:T(8,128)(2,1)S(1)}, bf16[160,256]{1,0:T(8,128)(2,1)S(1)}, u32[]{:S(2)}, u32[]{:S(2)}) collective-permute-start(bf16[160,256]{1,0:T(8,128)(2,1)S(1)} %copy-done.2), channel_id=1, source_target_pairs={{0,32},{8,40},{16,48},{24,56},{32,64},{40,72},{48,80},{56,88},{64,... | collective-permute-start | bytes 245768 | tf_op jit(solution)/shard_map/ppermute | solution.py:392
  18.0 6.0 %shard_map.55 = (bf16[784,256]{1,0:T(8,128)(2,1)}, bf16[1296,256]{1,0:T(8,128)(2,1)}, bf16[1296,256]{1,0:T(8,128)(2,1)}, bf16[1296,256]{1,0:T(8,128)(2,1)}, f32[...) custom-call(s32[2,3]{1,0:T(2,128)} %off.1, bf16[1024,256]{1,0:T(8,128)(2,1)} %q.3, bf16[1024,256]{1,0:T(8,128)(2,1)} %k.3, ...), custom_call_target="tpu_custom_call" | custom-call | tf_op jit(solution)/shard_map/pallas_call | solution.py:423
  24.1 0.0 collective-permute-done.5.z3
  24.1 0.0 collective-permute-done.4.z2
  24.1 0.0 collective-permute-done.3.z1
  24.1 0.0 all-to-all-done.near_in._2.near
  24.1 0.9 shard_map.58
  25.0 14.3 %all-to-all-start.1 = ((bf16[4,4,32,256]{3,2,1,0:T(8,128)(2,1)}), bf16[4,4,32,256]{3,2,1,0:T(8,128)(2,1)S(1)}, u32[]{:S(2)}, u32[]{:S(2)}) async-start(bf16[4,4,32,256]{3,2,1,0:T(8,128)(2,1)} %get-tuple-element.32), calls=%async_computation.1 | async-start | bytes 524288 | tf_op jit(solution)/shard_map/all_to_all | solution.py:388
  39.3 3.1 %collective-permute-start = (bf16[1296,256]{1,0:T(8,128)(2,1)}, bf16[1296,256]{1,0:T(8,128)(2,1)S(1)}, u32[]{:S(2)}, u32[]{:S(2)}) collective-permute-start(bf16[1296,256]{1,0:T(8,128)(2,1)} %get-tuple-element.21), channel_id=1, source_target_pairs={{0,2},{1,3},{2,4},{3,5},{4,6},{5,7},{6,0},{7,1},{8,10},{9,11},{10,... | collective-permute-start | bytes 1990664 | tf_op jit(solution)/shard_map/ppermute | solution.py:395
  42.4 4.4 %collective-permute-start.1 = (bf16[1296,256]{1,0:T(8,128)(2,1)}, bf16[1296,256]{1,0:T(8,128)(2,1)S(1)}, u32[]{:S(2)}, u32[]{:S(2)}) collective-permute-start(bf16[1296,256]{1,0:T(8,128)(2,1)} %get-tuple-element.22), channel_id=1, source_target_pairs={{0,4},{1,5},{2,6},{3,7},{4,0},{5,1},{6,2},{7,3},{8,12},{9,13},{10,... | collective-permute-start | bytes 1990664 | tf_op jit(solution)/shard_map/ppermute | solution.py:395
  46.8 3.0 %collective-permute-start.2 = (bf16[1296,256]{1,0:T(8,128)(2,1)}, bf16[1296,256]{1,0:T(8,128)(2,1)S(1)}, u32[]{:S(2)}, u32[]{:S(2)}) collective-permute-start(bf16[1296,256]{1,0:T(8,128)(2,1)} %get-tuple-element.23), channel_id=1, source_target_pairs={{0,6},{1,7},{2,0},{3,1},{4,2},{5,3},{6,4},{7,5},{8,14},{9,15},{10,... | collective-permute-start | bytes 1990664 | tf_op jit(solution)/shard_map/ppermute | solution.py:395
  49.8 3.9 %shard_map.57 = (f32[2,336,128]{2,1,0:T(8,128)}, f32[2,336,128]{2,1,0:T(8,128)}) custom-call(s32[2,3]{1,0:T(2,128)} %off.1, bf16[256,256]{1,0:T(8,128)(2,1)} %get-tuple-element.24.own_q, bf16[4,592,256]{2,1,0:T(8,128)(2,1)S(1)} %all-to-all-done.near_in._2.near, f32[2,336,128]{2,1,0:T(8,128)} %get-tuple-element.26.m_in, f32[2,336,128]{2,1,0:T(8,128)} %get-tuple-element.27.l_in), custom_call_target="tpu_custom_call" | custom-call | tf_op jit(solution)/shard_map/pallas_call | solution.py:449
  53.7 0.0 all-to-all-done.1.hi
  53.7 0.0 copy-start
  53.7 0.0 copy-start.1
  53.7 0.0 copy-start.3
  53.7 2.5 %shard_map.59 = bf16[4,80,384]{2,1,0:T(8,128)(2,1)} custom-call(bf16[4,592,256]{2,1,0:T(8,128)(2,1)S(1)} %all-to-all-done.near_in._2.near, bf16[4,128,256]{2,1,0:T(8,128)(2,1)} %get-tuple-element.31.middle, bf16[4,4,32,256]{3,2,1,0:T(8,128)(2,1)S(1)} %all-to-all-done.1.hi, f32[2,336,128]{2,1,0:T(8,128)} %get-tuple-element.28._.mixed), custom_call_target="tpu_custom_call" | custom-call | tf_op jit(solution)/shard_map/pallas_call | solution.py:465
  56.3 9.1 %all_to_all.20.back = bf16[4,80,384]{2,1,0:T(8,128)(2,1)S(1)} all-to-all(bf16[4,80,384]{2,1,0:T(8,128)(2,1)} %shard_map.59), channel_id=1, replica_groups={{0,8,16,24},{32,40,48,56},{64,72,80,88},{96,104,112,120},{128,136,144,1..., dimensions={0} | all-to-all | bytes 491520 | tf_op jit(solution)/shard_map/all_to_all | solution.py:388
  65.4 0.0 copy-done
  65.4 0.0 copy-done.1
  65.4 0.0 copy-done.3
  65.4 2.3 %shard_map.60 = bf16[4,336,256]{2,1,0:T(8,128)(2,1)} custom-call(s32[2,3]{1,0:T(2,128)S(1)} %copy-done.3, f32[2,336,128]{2,1,0:T(8,128)S(1)} %copy-done, f32[2,336,128]{2,1,0:T(8,128)S(1)} %copy-done.1, bf16[4,80,384]{2,1,0:T(8,128)(2,1)S(1)} %all_to_all.20.back), custom_call_target="tpu_custom_call" | custom-call | tf_op jit(solution)/shard_map/pallas_call | solution.py:477
  67.8 3.5 %all-to-all-start.3 = ((bf16[4,336,256]{2,1,0:T(8,128)(2,1)}), bf16[4,336,256]{2,1,0:T(8,128)(2,1)S(1)}, u32[]{:S(2)}, u32[]{:S(2)}) async-start(bf16[4,336,256]{2,1,0:T(8,128)(2,1)} %shard_map.60), calls=%async_computation.3 | async-start | bytes 1376256 | tf_op jit(solution)/shard_map/all_to_all | solution.py:388
  71.3 0.8 slice.12
  72.0 0.0 collective-permute-done.e1
  72.0 0.1 slice.13
  72.1 0.0 collective-permute-done.1.e2
  72.1 0.1 slice.14
  72.2 3.0 %collective-permute-done.2.e3 = bf16[1296,256]{1,0:T(8,128)(2,1)S(1)} collective-permute-done((bf16[1296,256]{1,0:T(8,128)(2,1)}, bf16[1296,256]{1,0:T(8,128)(2,1)S(1)}, u32[]{:S(2)}, u32[]{:S(2)}) %collective-permute-start.2) | collective-permute-done | bytes 663584 | tf_op jit(solution)/shard_map/ppermute | solution.py:395
  75.2 0.1 slice.15
  75.3 3.7 %all-to-all-done.3.late = bf16[4,336,256]{2,1,0:T(8,128)(2,1)S(1)} async-done(((bf16[4,336,256]{2,1,0:T(8,128)(2,1)}), bf16[4,336,256]{2,1,0:T(8,128)(2,1)S(1)}, u32[]{:S(2)}, u32[]{:S(2)}) %all-to-all-start.3) | async-done | bytes 688160 | tf_op jit(solution)/shard_map/all_to_all | solution.py:388
  79.0 2.7 %shard_map.61 = (bf16[1024,256]{1,0:T(8,128)(2,1)S(1)}, bf16[1024,1024]{1,0:T(8,128)(2,1)S(1)}) custom-call(s32[4,3,2]{2,1,0:T(4,128)S(1)} %maximum_convert_fusion.marks, bf16[784,256]{1,0:T(8,128)(2,1)} %get-tuple-element.20._1.own, bf16[1296,256]{1,0:T(8,128)(2,1)S(1)} %collective-permute-done.e1, bf16[1296,256]{1,0:T(8,128)(2,1)S(1)} %collective-permute-done.1.e2, ...), custom_call_target="tpu_custom_call" | custom-call | tf_op jit(solution)/shard_map/pallas_call | solution.py:490
  81.8 10.7 %collective-permute-start.6 = (bf16[1024,256]{1,0:T(8,128)(2,1)S(1)}, bf16[1024,256]{1,0:T(8,128)(2,1)S(1)}, u32[]{:S(2)}, u32[]{:S(2)}) collective-permute-start(bf16[1024,256]{1,0:T(8,128)(2,1)S(1)} %get-tuple-element.34), channel_id=1, source_target_pairs={{0,1},{1,0},{2,3},{3,2},{4,5},{5,4},{6,7},{7,6},{8,9},{9,8},{10,11... | collective-permute-start | bytes 1572872 | tf_op jit(solution)/shard_map/ppermute | solution.py:509
  92.5 1.7 %shard_map.62.keep = f32[1024,256]{1,0:T(8,128)S(1)} custom-call(bf16[1024,1024]{1,0:T(8,128)(2,1)S(1)} %get-tuple-element.33.whole, bf16[1296,256]{1,0:T(8,128)(2,1)S(1)} %collective-permute-done.e1, bf16[1296,256]{1,0:T(8,128)(2,1)S(1)} %collective-permute-done.1.e2, bf16[1296,256]{1,0:T(8,128)(2,1)S(1)} %collective-permute-done.2.e3, bf16[256,2048]{1,0:T(8,128)(2,1)} %w.5), custom_call_target="tpu_custom_call" | custom-call | tf_op jit(solution)/shard_map/pallas_call | solution.py:502
  94.2 0.0 collective-permute-done.6.other
  94.2 1.0 %shard_map.63 = bf16[1024,256]{1,0:T(8,128)(2,1)} custom-call(f32[1024,256]{1,0:T(8,128)S(1)} %shard_map.62.keep, bf16[1024,256]{1,0:T(8,128)(2,1)S(1)} %collective-permute-done.6.other), custom_call_target="tpu_custom_call" | custom-call | tf_op jit(solution)/shard_map/pallas_call | solution.py:510
  (1 shorter events, 0.0 us)
Async XLA Ops:
  2.5 5.2 %copy-start.2 = (bf16[160,256]{1,0:T(8,128)(2,1)S(1)}, bf16[160,256]{1,0:T(8,128)(2,1)}, u32[]{:S(2)}) copy-start(bf16[160,256]{1,0:T(8,128)(2,1)} %get-tuple-element.30.z0) | copy-start | bytes 245764
  2.5 21.6 %all-to-all-start = ((bf16[4,592,256]{2,1,0:T(8,128)(2,1)}), bf16[4,592,256]{2,1,0:T(8,128)(2,1)S(1)}, u32[]{:S(2)}, u32[]{:S(2)}) async-start(bf16[4,592,256]{2,1,0:T(8,128)(2,1)} %get-tuple-element.25), calls=%async_computation | async-start | bytes 2424832 | tf_op jit(solution)/shard_map/all_to_all | solution.py:388
  7.6 16.4 %collective-permute-start.5 = (bf16[160,256]{1,0:T(8,128)(2,1)S(1)}, bf16[160,256]{1,0:T(8,128)(2,1)S(1)}, u32[]{:S(2)}, u32[]{:S(2)}) collective-permute-start(bf16[160,256]{1,0:T(8,128)(2,1)S(1)} %copy-done.2), channel_id=1, source_target_pairs={{0,96},{8,104},{16,112},{24,120},{32,0},{40,8},{48,16},{56,24},{64... | collective-permute-start | bytes 245768 | tf_op jit(solution)/shard_map/ppermute | solution.py:392
  13.9 10.2 %collective-permute-start.4 = (bf16[160,256]{1,0:T(8,128)(2,1)S(1)}, bf16[160,256]{1,0:T(8,128)(2,1)S(1)}, u32[]{:S(2)}, u32[]{:S(2)}) collective-permute-start(bf16[160,256]{1,0:T(8,128)(2,1)S(1)} %copy-done.2), channel_id=1, source_target_pairs={{0,64},{8,72},{16,80},{24,88},{32,96},{40,104},{48,112},{56,120},{... | collective-permute-start | bytes 245768 | tf_op jit(solution)/shard_map/ppermute | solution.py:392
  15.8 8.3 %collective-permute-start.3 = (bf16[160,256]{1,0:T(8,128)(2,1)S(1)}, bf16[160,256]{1,0:T(8,128)(2,1)S(1)}, u32[]{:S(2)}, u32[]{:S(2)}) collective-permute-start(bf16[160,256]{1,0:T(8,128)(2,1)S(1)} %copy-done.2), channel_id=1, source_target_pairs={{0,32},{8,40},{16,48},{24,56},{32,64},{40,72},{48,80},{56,88},{64,... | collective-permute-start | bytes 245768 | tf_op jit(solution)/shard_map/ppermute | solution.py:392
  25.0 28.7 %all-to-all-start.1 = ((bf16[4,4,32,256]{3,2,1,0:T(8,128)(2,1)}), bf16[4,4,32,256]{3,2,1,0:T(8,128)(2,1)S(1)}, u32[]{:S(2)}, u32[]{:S(2)}) async-start(bf16[4,4,32,256]{3,2,1,0:T(8,128)(2,1)} %get-tuple-element.32), calls=%async_computation.1 | async-start | bytes 524288 | tf_op jit(solution)/shard_map/all_to_all | solution.py:388
  39.3 32.7 %collective-permute-start = (bf16[1296,256]{1,0:T(8,128)(2,1)}, bf16[1296,256]{1,0:T(8,128)(2,1)S(1)}, u32[]{:S(2)}, u32[]{:S(2)}) collective-permute-start(bf16[1296,256]{1,0:T(8,128)(2,1)} %get-tuple-element.21), channel_id=1, source_target_pairs={{0,2},{1,3},{2,4},{3,5},{4,6},{5,7},{6,0},{7,1},{8,10},{9,11},{10,... | collective-permute-start | bytes 1990664 | tf_op jit(solution)/shard_map/ppermute | solution.py:395
  42.4 29.7 %collective-permute-start.1 = (bf16[1296,256]{1,0:T(8,128)(2,1)}, bf16[1296,256]{1,0:T(8,128)(2,1)S(1)}, u32[]{:S(2)}, u32[]{:S(2)}) collective-permute-start(bf16[1296,256]{1,0:T(8,128)(2,1)} %get-tuple-element.22), channel_id=1, source_target_pairs={{0,4},{1,5},{2,6},{3,7},{4,0},{5,1},{6,2},{7,3},{8,12},{9,13},{10,... | collective-permute-start | bytes 1990664 | tf_op jit(solution)/shard_map/ppermute | solution.py:395
  46.8 28.5 %collective-permute-start.2 = (bf16[1296,256]{1,0:T(8,128)(2,1)}, bf16[1296,256]{1,0:T(8,128)(2,1)S(1)}, u32[]{:S(2)}, u32[]{:S(2)}) collective-permute-start(bf16[1296,256]{1,0:T(8,128)(2,1)} %get-tuple-element.23), channel_id=1, source_target_pairs={{0,6},{1,7},{2,0},{3,1},{4,2},{5,3},{6,4},{7,5},{8,14},{9,15},{10,... | collective-permute-start | bytes 1990664 | tf_op jit(solution)/shard_map/ppermute | solution.py:395
  53.7 11.7 %copy-start = (f32[2,336,128]{2,1,0:T(8,128)S(1)}, f32[2,336,128]{2,1,0:T(8,128)}, u32[]{:S(2)}) copy-start(f32[2,336,128]{2,1,0:T(8,128)} %get-tuple-element.28._.mixed) | copy-start | bytes 1032196
  53.7 11.7 %copy-start.1 = (f32[2,336,128]{2,1,0:T(8,128)S(1)}, f32[2,336,128]{2,1,0:T(8,128)}, u32[]{:S(2)}) copy-start(f32[2,336,128]{2,1,0:T(8,128)} %get-tuple-element.29.logs) | copy-start | bytes 1032196
  53.7 11.7 %copy-start.3 = (s32[2,3]{1,0:T(2,128)S(1)}, s32[2,3]{1,0:T(2,128)}, u32[]{:S(2)}) copy-start(s32[2,3]{1,0:T(2,128)} %off.1) | copy-start | bytes 76
  67.8 11.3 %all-to-all-start.3 = ((bf16[4,336,256]{2,1,0:T(8,128)(2,1)}), bf16[4,336,256]{2,1,0:T(8,128)(2,1)S(1)}, u32[]{:S(2)}, u32[]{:S(2)}) async-start(bf16[4,336,256]{2,1,0:T(8,128)(2,1)} %shard_map.60), calls=%async_computation.3 | async-start | bytes 1376256 | tf_op jit(solution)/shard_map/all_to_all | solution.py:388
  81.8 12.4 %collective-permute-start.6 = (bf16[1024,256]{1,0:T(8,128)(2,1)S(1)}, bf16[1024,256]{1,0:T(8,128)(2,1)S(1)}, u32[]{:S(2)}, u32[]{:S(2)}) collective-permute-start(bf16[1024,256]{1,0:T(8,128)(2,1)S(1)} %get-tuple-element.34), channel_id=1, source_target_pairs={{0,1},{1,0},{2,3},{3,2},{4,5},{5,4},{6,7},{7,6},{8,9},{9,8},{10,11... | collective-permute-start | bytes 1572872 | tf_op jit(solution)/shard_map/ppermute | solution.py:509
